TPU v7x, 32 devices: a whole 2x2x4 slice. The times are simulated.
32 devices in a mesh: dp: 8 (over z, x), tensor: 4 (over y, core).
Axes of the slice: x: 2, y: 2, z: 4, core: 2. Of those that a mesh axis runs over, the one named last changes fastest.
Arguments:
- patches: bfloat16 [192, 50, 1024], P(('dp', 'tensor')), may hold values from -6 to 6
- keep_index: int32 [192, 50], P(('dp', 'tensor')), may hold values from 0 to 49, each once within a row
- kept_count: int32 [192], P(('dp', 'tensor')), may hold values from 25 to 50, as said below
- norm_gain: float32 [2, 2, 1024], replicated, may hold values from 0.5 to 1.5
- shifts: float32 [2, 4, 1024], replicated, may hold values from -3 to 3
- w_qkv: bfloat16 [2, 1024, 3, 1024], P(None, None, None, 'tensor'), may hold values from -0.1875 to 0.1875
- bias_qv: float32 [2, 2, 1024], P(None, None, 'tensor'), may hold values from -3 to 3
- w_out: bfloat16 [2, 1024, 1024], P(None, 'tensor'), may hold values from -1 to 1
- w_fc1: bfloat16 [2, 1024, 4096], P(None, None, 'tensor'), may hold values from -0.1875 to 0.1875
- bias_fc1: float32 [2, 4096], P(None, 'tensor'), may hold values from -3 to 3
- w_fc2: bfloat16 [2, 4096, 1024], P(None, 'tensor'), may hold values from -0.09375 to 0.09375
- cotangent: bfloat16 [192, 50, 1024], P(('dp', 'tensor')), may hold values from -6 to 6
Outputs:
- layer_out: float32 [192, 50, 1024], P(('dp', 'tensor'))
- grad_patches: float32 [192, 50, 1024], P(('dp', 'tensor'))
- grad_gain: float32 [2, 2, 1024], replicated
- grad_shifts: float32 [2, 4, 1024], replicated
- grad_qkv: float32 [2, 1024, 3, 1024], P(None, 'dp', None, 'tensor')
- grad_bias_qv: float32 [2, 2, 1024], replicated
- grad_out: float32 [2, 1024, 1024], P(None, 'tensor', 'dp')
- grad_fc1: float32 [2, 1024, 4096], P(None, 'dp', 'tensor')
- grad_bias_fc1: float32 [2, 4096], replicated
- grad_fc2: float32 [2, 4096, 1024], P(None, 'tensor', 'dp')
Inputs may be any that keep to these rules, and one draw needn't show every extreme that they name: Each row of keep_index holds every patch index once. `kept_count`: some image keeps all 50 slots and some keeps 25.
All inputs are finite; a program needn't handle non-finite values.
Results may differ from a plain program's by a relative error of at most 0.039.
Values may be sent and summed in bfloat16 or wider, within the bound.
A program may use at most 192 MiB of HBM per device.

v0:
```python
from functools import partial

import jax
import jax.numpy as jnp
from jax import lax
from jax.sharding import PartitionSpec as P

D = 1024
HEAD = 64
FF = 4096
LAYERS = 2
PATCHES = 50


EPS = 1e-06
HIGHEST = lax.Precision.HIGHEST


def norm_rows(values, scaling, offset):
    average = jnp.mean(values, axis=-1, keepdims=True)
    centred = values - average
    variance = jnp.mean(centred * centred, axis=-1, keepdims=True)
    return centred * lax.rsqrt(variance + EPS) * scaling + offset


def spread(rows, counts):
    return (
        lax.all_gather(rows, "tensor", axis=0, tiled=True),
        lax.all_gather(counts, "tensor", axis=0, tiled=True),
    )


def collect(partial_rows):
    return lax.psum_scatter(
        partial_rows.astype(jnp.bfloat16), "tensor", scatter_dimension=0, tiled=True
    ).astype(jnp.float32)


def spread_grad(rows):
    return lax.all_gather(rows, "tensor", axis=0, tiled=True)


def collect_grad(partial_rows):
    return lax.psum_scatter(
        partial_rows.astype(jnp.bfloat16), "tensor", scatter_dimension=0, tiled=True
    ).astype(jnp.float32)


def score_block(queries, key_rows, visible, score_scale):
    scores = (
        jnp.einsum("bqhe,bkhe->bhqk", queries, key_rows, preferred_element_type=jnp.float32)
        * score_scale
    )
    return jnp.where(visible[:, None, None, :], scores, -1e30)


def local(
    patches,
    keep_index,
    kept_count,
    norm_gain,
    shifts,
    w_qkv,
    bias_qv,
    w_out,
    w_fc1,
    bias_fc1,
    w_fc2,
    cotangent,
):
    width_local = w_qkv.shape[-1]
    hidden_local = w_fc1.shape[-1]
    heads_local = width_local // HEAD
    score_scale = HEAD ** (-0.5)
    slot_ids = jnp.arange(PATCHES, dtype=jnp.int32)
    selector = (keep_index[:, :, None] == slot_ids[None, None, :]).astype(jnp.bfloat16)
    residual = jnp.einsum("bsp,bpd->bsd", selector, patches, preferred_element_type=jnp.float32)
    stored = []
    visible = None
    shape_heads = None
    image_total = 0
    for layer_no in range(LAYERS):
        normed_own = norm_rows(residual, norm_gain[layer_no, 0], shifts[layer_no, 0]).astype(
            jnp.bfloat16
        )
        normed, counts_all = spread(normed_own, kept_count)
        visible = slot_ids[None, :] < counts_all[:, None]
        image_total = normed.shape[0]
        shape_heads = (image_total, PATCHES, heads_local, HEAD)
        triple = jnp.einsum(
            "bsd,dce->bsce", normed, w_qkv[layer_no], preferred_element_type=jnp.float32
        )
        queries = (triple[:, :, 0] + bias_qv[layer_no, 0]).astype(jnp.bfloat16).reshape(shape_heads)
        key_rows = triple[:, :, 1].astype(jnp.bfloat16).reshape(shape_heads)
        value_rows = (
            (triple[:, :, 2] + bias_qv[layer_no, 1]).astype(jnp.bfloat16).reshape(shape_heads)
        )
        scores = score_block(queries, key_rows, visible, score_scale)
        log_total = jax.nn.logsumexp(scores, axis=-1, keepdims=True)
        attn_weights = jnp.exp(scores - log_total).astype(jnp.bfloat16)
        attended = jnp.einsum(
            "bhqk,bkhe->bqhe", attn_weights, value_rows, preferred_element_type=jnp.float32
        )
        attended = attended.reshape(image_total, PATCHES, width_local).astype(jnp.bfloat16)
        mixed = collect(
            jnp.einsum("bse,ed->bsd", attended, w_out[layer_no], preferred_element_type=jnp.float32)
        )
        middle = residual + mixed + shifts[layer_no, 2]
        normed_mid = norm_rows(middle, norm_gain[layer_no, 1], shifts[layer_no, 1]).astype(
            jnp.bfloat16
        )
        normed_mlp, counts_again = spread(normed_mid, kept_count)
        pre_act = (
            jnp.einsum(
                "bsd,df->bsf", normed_mlp, w_fc1[layer_no], preferred_element_type=jnp.float32
            )
            + bias_fc1[layer_no]
        )
        activated = jax.nn.gelu(pre_act, approximate=False).astype(jnp.bfloat16)
        stored.append(
            (
                residual,
                normed,
                queries,
                key_rows,
                value_rows,
                log_total,
                attended,
                middle,
                normed_mlp,
                pre_act,
                activated,
            )
        )
        mlp_part = collect(
            jnp.einsum(
                "bsf,fd->bsd", activated, w_fc2[layer_no], preferred_element_type=jnp.float32
            )
        )
        residual = middle + mlp_part + shifts[layer_no, 3]
    own_mask = (slot_ids[None, :] < kept_count[:, None]).astype(jnp.float32)[:, :, None]
    layer_out = residual * own_mask
    gradient = cotangent.astype(jnp.float32) * own_mask
    offset_at = lax.axis_index("tensor") * width_local
    hidden_at = lax.axis_index("tensor") * hidden_local
    gain_terms = []
    shift_terms = []
    bias_qv_terms = []
    bias_fc1_terms = []
    weight_terms = []
    for layer_no in reversed(range(LAYERS)):
        (
            residual_in,
            normed,
            queries,
            key_rows,
            value_rows,
            log_total,
            attended,
            middle,
            normed_mlp,
            pre_act,
            activated,
        ) = stored[layer_no]
        grad_mlp = gradient.astype(jnp.bfloat16)
        shift_fc2 = jnp.sum(grad_mlp.astype(jnp.float32), axis=(0, 1))
        grad_rows = spread_grad(grad_mlp)
        d_fc2 = jnp.einsum("bsf,bsd->fd", activated, grad_rows, preferred_element_type=jnp.float32)
        d_act = jnp.einsum(
            "bsd,fd->bsf", grad_rows, w_fc2[layer_no], preferred_element_type=jnp.float32
        )
        gelu_pull = jax.vjp(partial(jax.nn.gelu, approximate=False), pre_act)[1]
        d_pre = gelu_pull(d_act)[0].astype(jnp.bfloat16)
        d_bias_fc1 = jnp.sum(d_pre.astype(jnp.float32), axis=(0, 1))
        d_fc1 = jnp.einsum("bsd,bsf->df", normed_mlp, d_pre, preferred_element_type=jnp.float32)
        d_normed = collect_grad(
            jnp.einsum("bsf,df->bsd", d_pre, w_fc1[layer_no], preferred_element_type=jnp.float32)
        )
        norm_pull = jax.vjp(norm_rows, middle, norm_gain[layer_no, 1], shifts[layer_no, 1])[1]
        d_middle, d_gain_mlp, d_shift_mlp = norm_pull(d_normed)
        gradient = gradient + d_middle
        grad_attn = gradient.astype(jnp.bfloat16)
        shift_attn = jnp.sum(grad_attn.astype(jnp.float32), axis=(0, 1))
        grad_rows = spread_grad(grad_attn)
        d_out = jnp.einsum("bse,bsd->ed", attended, grad_rows, preferred_element_type=jnp.float32)
        d_attended = jnp.einsum(
            "bsd,ed->bse", grad_rows, w_out[layer_no], preferred_element_type=jnp.float32
        )
        d_attended = d_attended.astype(jnp.bfloat16).reshape(shape_heads)
        scores = score_block(queries, key_rows, visible, score_scale)
        probability = jnp.exp(scores - log_total)
        d_values = jnp.einsum(
            "bhqk,bqhe->bkhe",
            probability.astype(jnp.bfloat16),
            d_attended,
            preferred_element_type=jnp.float32,
        )
        d_prob = jnp.einsum(
            "bqhe,bkhe->bhqk", d_attended, value_rows, preferred_element_type=jnp.float32
        )
        centre_term = jnp.sum(probability * d_prob, axis=-1, keepdims=True)
        d_scores = (probability * (d_prob - centre_term)).astype(jnp.bfloat16)
        d_queries = (
            jnp.einsum("bhqk,bkhe->bqhe", d_scores, key_rows, preferred_element_type=jnp.float32)
            * score_scale
        )
        d_keys = (
            jnp.einsum("bhqk,bqhe->bkhe", d_scores, queries, preferred_element_type=jnp.float32)
            * score_scale
        )
        d_triple = jnp.stack([d_queries, d_keys, d_values], axis=2)
        d_triple = d_triple.reshape(image_total, PATCHES, 3, width_local).astype(jnp.bfloat16)
        d_bias_qv = jnp.sum(d_triple[:, :, 0::2].astype(jnp.float32), axis=(0, 1))
        d_qkv = jnp.einsum("bsd,bsce->dce", normed, d_triple, preferred_element_type=jnp.float32)
        d_normed = collect_grad(
            jnp.einsum(
                "bsce,dce->bsd", d_triple, w_qkv[layer_no], preferred_element_type=jnp.float32
            )
        )
        norm_pull = jax.vjp(norm_rows, residual_in, norm_gain[layer_no, 0], shifts[layer_no, 0])[1]
        d_input, d_gain_attn, d_shift_attn = norm_pull(d_normed)
        gradient = gradient + d_input
        gain_terms.insert(0, jnp.stack([d_gain_attn, d_gain_mlp]))
        shift_terms.insert(0, jnp.stack([d_shift_attn, d_shift_mlp, shift_attn, shift_fc2]))
        bias_qv_terms.insert(0, d_bias_qv)
        bias_fc1_terms.insert(0, d_bias_fc1)
        weight_terms.insert(0, (d_qkv, d_out, d_fc1, d_fc2))
    grad_qkv, grad_out, grad_fc1, grad_fc2 = (
        lax.psum_scatter(
            jnp.stack([entry[0] for entry in weight_terms]), "dp", scatter_dimension=1, tiled=True
        ),
        lax.psum_scatter(
            jnp.stack([entry[1] for entry in weight_terms]), "dp", scatter_dimension=2, tiled=True
        ),
        lax.psum_scatter(
            jnp.stack([entry[2] for entry in weight_terms]), "dp", scatter_dimension=1, tiled=True
        ),
        lax.psum_scatter(
            jnp.stack([entry[3] for entry in weight_terms]), "dp", scatter_dimension=2, tiled=True
        ),
    )
    zero_at = offset_at * 0
    qv_full = lax.dynamic_update_slice(
        jnp.zeros((LAYERS, 2, D), jnp.float32),
        jnp.stack(bias_qv_terms),
        (zero_at, zero_at, offset_at),
    )
    fc1_full = lax.dynamic_update_slice(
        jnp.zeros((LAYERS, FF), jnp.float32), jnp.stack(bias_fc1_terms), (zero_at, hidden_at)
    )
    grad_gain, grad_shifts, grad_bias_qv, grad_bias_fc1 = lax.psum(
        (jnp.stack(gain_terms), jnp.stack(shift_terms), qv_full, fc1_full), ("dp", "tensor")
    )
    grad_patches = jnp.einsum(
        "bsp,bsd->bpd", selector.astype(jnp.float32), gradient, precision=HIGHEST
    )
    return (
        layer_out,
        grad_patches,
        grad_gain,
        grad_shifts,
        grad_qkv,
        grad_bias_qv,
        grad_out,
        grad_fc1,
        grad_bias_fc1,
        grad_fc2,
    )


def solution(mesh):
    in_specs = (
        P(("dp", "tensor"), None, None),
        P(("dp", "tensor"), None),
        P(("dp", "tensor")),
        P(),
        P(),
        P(None, None, None, "tensor"),
        P(None, None, "tensor"),
        P(None, "tensor", None),
        P(None, None, "tensor"),
        P(None, "tensor"),
        P(None, "tensor", None),
        P(("dp", "tensor"), None, None),
    )
    out_specs = (
        P(("dp", "tensor"), None, None),
        P(("dp", "tensor"), None, None),
        P(),
        P(),
        P(None, "dp", None, "tensor"),
        P(),
        P(None, "tensor", "dp"),
        P(None, "dp", "tensor"),
        P(),
        P(None, "tensor", "dp"),
    )
    return jax.shard_map(local, mesh=mesh, in_specs=in_specs, out_specs=out_specs, check_vma=False)
```

profile of v0, /device:TPU:0, one launch (start us, length us, event | category | flops | bytes accessed | tf_op | source)
XLA Modules:
  0.0 1395.1 jit_solution(3292938228315837027)
XLA Ops:
  14.7 6.4 all-reduce
  21.1 20.9 %all-gather.9.cloned.1.call-done = bf16[24,50,1024]{2,1,0:T(8,128)(2,1)} async-done(((bf16[6,50,1024]{2,1,0:T(8,128)(2,1)}), bf16[24,50,1024]{2,1,0:T(8,128)(2,1)}) %all-gather.9.cloned.1.call-update) | async-done | bytes 2457616 | tf_op jit(solution)/shard_map/all_gather | solution.py:28
  42.1 4.6 fusion.18
  49.5 3.2 squeeze.48
  71.9 3.8 convolution_convert_fusion.1
  75.9 35.4 %reduce-scatter.13.cloned.1.call-done = bf16[6,50,1024]{2,1,0:T(8,128)(2,1)} async-done(((bf16[24,50,1024]{2,1,0:T(8,128)(2,1)}), bf16[6,50,1024]{2,1,0:T(8,128)(2,1)}) %reduce-scatter.13.cloned.1.call-update) | async-done | bytes 614416 | tf_op jit(solution)/shard_map/reduce_scatter | solution.py:34
  114.8 25.8 %all-gather.11.cloned.1.call-done = bf16[24,50,1024]{2,1,0:T(8,128)(2,1)} async-done(((bf16[6,50,1024]{2,1,0:T(8,128)(2,1)}), bf16[24,50,1024]{2,1,0:T(8,128)(2,1)}) %all-gather.11.cloned.1.call-update) | async-done | bytes 2457616 | tf_op jit(solution)/shard_map/all_gather | solution.py:28
  140.6 7.1 convert_reduce_fusion.3
  147.8 13.3 multiply_convert_fusion.1
  162.6 4.4 convolution_convert_fusion.5
  167.1 35.6 %reduce-scatter.15.cloned.1.call-done = bf16[6,50,1024]{2,1,0:T(8,128)(2,1)} async-done(((bf16[24,50,1024]{2,1,0:T(8,128)(2,1)}), bf16[6,50,1024]{2,1,0:T(8,128)(2,1)}) %reduce-scatter.15.cloned.1.call-update) | async-done | bytes 614416 | tf_op jit(solution)/shard_map/reduce_scatter | solution.py:34
  206.7 25.3 %all-gather.13.cloned.1.call-done = bf16[24,50,1024]{2,1,0:T(8,128)(2,1)} async-done(((bf16[6,50,1024]{2,1,0:T(8,128)(2,1)}), bf16[24,50,1024]{2,1,0:T(8,128)(2,1)}) %all-gather.13.cloned.1.call-update) | async-done | bytes 2457616 | tf_op jit(solution)/shard_map/all_gather | solution.py:28
  232.0 4.6 fusion.14
  239.4 3.2 squeeze.54
  252.0 3.2 squeeze.53
  263.6 3.7 convolution_convert_fusion
  267.3 35.6 %reduce-scatter.17.cloned.1.call-done = bf16[6,50,1024]{2,1,0:T(8,128)(2,1)} async-done(((bf16[24,50,1024]{2,1,0:T(8,128)(2,1)}), bf16[6,50,1024]{2,1,0:T(8,128)(2,1)}) %reduce-scatter.17.cloned.1.call-update) | async-done | bytes 614416 | tf_op jit(solution)/shard_map/reduce_scatter | solution.py:34
  310.3 23.8 %all-gather.15.cloned.1.call-done = bf16[24,50,1024]{2,1,0:T(8,128)(2,1)} async-done(((bf16[6,50,1024]{2,1,0:T(8,128)(2,1)}), bf16[24,50,1024]{2,1,0:T(8,128)(2,1)}) %all-gather.15.cloned.1.call-update) | async-done | bytes 2457616 | tf_op jit(solution)/shard_map/all_gather | solution.py:28
  334.1 7.1 convert_reduce_fusion.1
  343.6 13.5 multiply_convert_fusion
  357.1 5.5 all-gather.17.cloned.1.call-done
  362.6 11.3 convert_reduce_fusion.4
  375.5 4.4 convolution_convert_fusion.3
  380.4 35.2 %reduce-scatter.21.cloned.1.call-done = bf16[6,50,1024]{2,1,0:T(8,128)(2,1)} async-done(((bf16[24,50,1024]{2,1,0:T(8,128)(2,1)}), bf16[6,50,1024]{2,1,0:T(8,128)(2,1)}) %reduce-scatter.21.cloned.1.call-update) | async-done | bytes 614416 | tf_op jit(solution)/shard_map/reduce_scatter | solution.py:44
  421.4 3.2 convert_reduce_fusion.13
  424.7 26.4 %all-gather.19.cloned.1.call-done = bf16[24,50,1024]{2,1,0:T(8,128)(2,1)} async-done(((bf16[6,50,1024]{2,1,0:T(8,128)(2,1)}), bf16[24,50,1024]{2,1,0:T(8,128)(2,1)}) %all-gather.19.cloned.1.call-update) | async-done | bytes 2457616 | tf_op jit(solution)/shard_map/all_gather | solution.py:40
  451.1 3.6 convolution_convert_fusion.11
  454.8 3.0 reshape.313
  457.8 3.2 fusion.64
  470.0 3.2 reshape.307
  473.2 2.8 copy.151
  476.1 3.2 reshape.306
  479.2 2.9 copy.150
  482.1 3.3 reshape.305
  489.3 4.0 bitcast_convert_fusion.1
  493.4 7.0 convolution_convert_fusion.4
  500.6 28.4 %reduce-scatter.23.cloned.1.call-done = bf16[6,50,1024]{2,1,0:T(8,128)(2,1)} async-done(((bf16[24,50,1024]{2,1,0:T(8,128)(2,1)}), bf16[6,50,1024]{2,1,0:T(8,128)(2,1)}) %reduce-scatter.23.cloned.1.call-update) | async-done | bytes 614416 | tf_op jit(solution)/shard_map/reduce_scatter | solution.py:44
  533.5 33.6 %reduce-scatter.19.cloned.1.call-done = bf16[6,50,1024]{2,1,0:T(8,128)(2,1)} async-done(((bf16[24,50,1024]{2,1,0:T(8,128)(2,1)}), bf16[6,50,1024]{2,1,0:T(8,128)(2,1)}) %reduce-scatter.19.cloned.1.call-update) | async-done | bytes 614416 | tf_op jit(solution)/shard_map/reduce_scatter | solution.py:34
  567.1 4.6 convert_reduce_fusion.14
  571.8 26.4 %all-gather.21.cloned.1.call-done = bf16[24,50,1024]{2,1,0:T(8,128)(2,1)} async-done(((bf16[6,50,1024]{2,1,0:T(8,128)(2,1)}), bf16[24,50,1024]{2,1,0:T(8,128)(2,1)}) %all-gather.21.cloned.1.call-update) | async-done | bytes 2457616 | tf_op jit(solution)/shard_map/all_gather | solution.py:40
  598.2 11.3 convert_reduce_fusion.5
  611.2 4.9 convolution_convert_fusion.2
  616.1 35.6 %reduce-scatter.25.cloned.1.call-done = bf16[6,50,1024]{2,1,0:T(8,128)(2,1)} async-done(((bf16[24,50,1024]{2,1,0:T(8,128)(2,1)}), bf16[6,50,1024]{2,1,0:T(8,128)(2,1)}) %reduce-scatter.25.cloned.1.call-update) | async-done | bytes 614416 | tf_op jit(solution)/shard_map/reduce_scatter | solution.py:44
  658.4 26.4 %all-gather.23.cloned.1.call-done = bf16[24,50,1024]{2,1,0:T(8,128)(2,1)} async-done(((bf16[6,50,1024]{2,1,0:T(8,128)(2,1)}), bf16[24,50,1024]{2,1,0:T(8,128)(2,1)}) %all-gather.23.cloned.1.call-update) | async-done | bytes 2457616 | tf_op jit(solution)/shard_map/all_gather | solution.py:40
  688.2 2.9 fusion.65
  701.1 2.9 copy.154
  703.9 3.2 reshape.309
  713.8 3.9 bitcast_convert_fusion
  718.8 3.8 fusion.91
  726.0 8.5 convolution_bitcast_fusion
  734.9 5.0 convolution_bitcast_fusion.1
  740.4 13.1 reduce-scatter.27.cloned.1.call-done
  758.2 8.4 pad_maximum_fusion.1
  766.9 6.3 convolution_bitcast_fusion.2
  773.3 3.5 convolution_bitcast_fusion.3
  776.8 4.1 pad_maximum_fusion
  781.3 5.3 fusion.39
  789.4 3.4 pad_maximum_fusion.2
  793.5 4.6 fusion.84
  798.0 27.4 %reduce-scatter.31.cloned.1.call-done = f32[2,256,128]{2,1,0:T(8,128)} async-done(((f32[2,256,1024]{2,1,0:T(8,128)}), f32[2,256,128]{2,1,0:T(8,128)}) %reduce-scatter.31.cloned.1.call-update) | async-done | bytes 262160 | tf_op jit(solution)/shard_map/reduce_scatter | solution.py:232
  825.5 128.3 %all-reduce.4.cloned.1.call-done = (f32[2,2,1024]{2,1,0:T(2,128)}, f32[2,4,1024]{2,1,0:T(4,128)}, f32[2,2,1024]{2,1,0:T(2,128)}, f32[2,4096]{1,0:T(2,128)}) async-done(((f32[2,2,1024]{2,1,0:T(2,128)}, f32[2,4,1024]{2,1,0:T(4,128)}, f32[2,2,1024]{2,1,0:T(2,128)}, f32[2,4096]{1,0:T(2,128)}), (f32[2,2,1024]{2,1,0:T(2,128)}, f32[2,4,1024]{2,1,0:T(4,128)}, f32[2,2,1024]{2,1,0:T(2,128)}, ...) | async-done | bytes 98320 | tf_op jit(solution)/shard_map/psum | solution.py:251
  953.8 154.5 %reduce-scatter.35.cloned.1.call-done = f32[2,1024,128]{2,1,0:T(8,128)} async-done(((f32[2,1024,1024]{2,1,0:T(8,128)}), f32[2,1024,128]{2,1,0:T(8,128)}) %reduce-scatter.35.cloned.1.call-update) | async-done | bytes 1048592 | tf_op jit(solution)/shard_map/reduce_scatter | solution.py:238
  1108.3 152.5 %reduce-scatter.33.cloned.1.call-done = f32[2,128,1024]{2,1,0:T(8,128)} async-done(((f32[2,1024,1024]{2,1,0:T(8,128)}), f32[2,128,1024]{2,1,0:T(8,128)}) %reduce-scatter.33.cloned.1.call-update) | async-done | bytes 1048592 | tf_op jit(solution)/shard_map/reduce_scatter | solution.py:235
  1260.8 121.6 %reduce-scatter.29.cloned.1.call-done = f32[2,128,3,256]{3,1,2,0:T(8,128)} async-done(((f32[2,1024,3,256]{3,1,2,0:T(8,128)}), f32[2,128,3,256]{3,1,2,0:T(8,128)}) %reduce-scatter.29.cloned.1.call-update) | async-done | bytes 786448 | tf_op jit(solution)/shard_map/reduce_scatter | solution.py:229
  (396 shorter events, 141.1 us)
Async XLA Ops:
  7.2 34.8 %all-gather.9.cloned.1.call-start = ((), (), s32[]{:S(2)}) async-start(), calls=%async_computation.12 | async-start | bytes 3440640 | tf_op jit(solution)/shard_map/all_gather | solution.py:28
  9.5 101.8 %copy-start.2 = (f32[6,50,1024]{2,1,0:T(8,128)}, f32[6,50,1024]{2,1,0:T(8,128)S(1)}, u32[]{:S(2)}) copy-start(f32[6,50,1024]{2,1,0:T(8,128)S(1)} %get-tuple-element.77) | copy-start | bytes 3686404
  9.5 32.6 %copy-start.47 = (f32[6,50]{1,0:T(8,128)}, f32[6,50]{1,0:T(8,128)S(1)}, u32[]{:S(2)}) copy-start(f32[6,50]{1,0:T(8,128)S(1)} %broadcast_multiply_fusion.3) | copy-start | bytes 3604
  10.5 36.2 %copy-start.63 = (f32[6,50]{1,0:T(8,128)}, f32[6,50]{1,0:T(8,128)S(1)}, u32[]{:S(2)}) copy-start(f32[6,50]{1,0:T(8,128)S(1)} %fusion.137) | copy-start | bytes 3604
  11.7 35.0 %copy-start.55 = (f32[1,1,1024]{2,1,0:T(1,128)}, f32[1,1,1024]{2,1,0:T(1,128)S(1)}, u32[]{:S(2)}) copy-start(f32[1,1,1024]{2,1,0:T(1,128)S(1)} %get-tuple-element.72) | copy-start | bytes 12292
  11.7 101.3 %copy-start.50 = (f32[1,1,1024]{2,1,0:T(1,128)}, f32[1,1,1024]{2,1,0:T(1,128)S(1)}, u32[]{:S(2)}) copy-start(f32[1,1,1024]{2,1,0:T(1,128)S(1)} %get-tuple-element.71) | copy-start | bytes 12292
  11.7 192.6 %copy-start.57 = (f32[1,1,1024]{2,1,0:T(1,128)}, f32[1,1,1024]{2,1,0:T(1,128)S(1)}, u32[]{:S(2)}) copy-start(f32[1,1,1024]{2,1,0:T(1,128)S(1)} %get-tuple-element.73) | copy-start | bytes 12292
  12.9 98.4 %reduce-scatter.13.cloned.1.call-start = ((), (), s32[]{:S(2)}) async-start(), calls=%async_computation.13 | async-start | bytes 3440640 | tf_op jit(solution)/shard_map/reduce_scatter | solution.py:34
  75.7 64.9 %all-gather.11.cloned.1.call-start = ((), (), s32[]{:S(2)}) async-start(), calls=%async_computation.14 | async-start | bytes 3440640 | tf_op jit(solution)/shard_map/all_gather | solution.py:28
  113.0 34.8 %copy-start.76 = (f32[6,50]{1,0:T(8,128)}, f32[6,50]{1,0:T(8,128)S(1)}, u32[]{:S(2)}) copy-start(f32[6,50]{1,0:T(8,128)S(1)} %multiply_reduce_fusion.4) | copy-start | bytes 3604
  113.0 34.7 %copy-start.59 = (f32[6,50]{1,0:T(8,128)}, f32[6,50]{1,0:T(8,128)S(1)}, u32[]{:S(2)}) copy-start(f32[6,50]{1,0:T(8,128)S(1)} %fusion.138) | copy-start | bytes 3604
  114.2 88.5 %reduce-scatter.15.cloned.1.call-start = ((), (), s32[]{:S(2)}) async-start(), calls=%async_computation.15 | async-start | bytes 3440640 | tf_op jit(solution)/shard_map/reduce_scatter | solution.py:34
  114.8 32.9 %copy-start.97 = (f32[1,1024]{1,0:T(1,128)}, f32[1,1024]{1,0:T(1,128)S(1)}, u32[]{:S(2)}) copy-start(f32[1,1024]{1,0:T(1,128)S(1)} %get-tuple-element.75) | copy-start | bytes 12292
  167.1 64.9 %all-gather.13.cloned.1.call-start = ((), (), s32[]{:S(2)}) async-start(), calls=%async_computation.16 | async-start | bytes 3440640 | tf_op jit(solution)/shard_map/all_gather | solution.py:28
  204.3 32.3 %copy-start.78 = (f32[6,50]{1,0:T(8,128)}, f32[6,50]{1,0:T(8,128)S(1)}, u32[]{:S(2)}) copy-start(f32[6,50]{1,0:T(8,128)S(1)} %multiply_reduce_fusion.3) | copy-start | bytes 3604
  204.3 32.3 %copy-start.65 = (f32[6,50]{1,0:T(8,128)}, f32[6,50]{1,0:T(8,128)S(1)}, u32[]{:S(2)}) copy-start(f32[6,50]{1,0:T(8,128)S(1)} %fusion.139) | copy-start | bytes 3604
  205.5 97.3 %reduce-scatter.17.cloned.1.call-start = ((), (), s32[]{:S(2)}) async-start(), calls=%async_computation.17 | async-start | bytes 3440640 | tf_op jit(solution)/shard_map/reduce_scatter | solution.py:34
  267.3 66.8 %all-gather.15.cloned.1.call-start = ((), (), s32[]{:S(2)}) async-start(), calls=%async_computation.18 | async-start | bytes 3440640 | tf_op jit(solution)/shard_map/all_gather | solution.py:28
  307.6 55.0 %all-gather.17.cloned.1.call-start = ((), (), s32[]{:S(2)}) async-start(), calls=%async_computation.20 | async-start | bytes 3440640 | tf_op jit(solution)/shard_map/all_gather | solution.py:40
  310.1 105.5 %reduce-scatter.21.cloned.1.call-start = ((), (), s32[]{:S(2)}) async-start(), calls=%async_computation.21 | async-start | bytes 3440640 | tf_op jit(solution)/shard_map/reduce_scatter | solution.py:44
  379.9 71.2 %all-gather.19.cloned.1.call-start = ((), (), s32[]{:S(2)}) async-start(), calls=%async_computation.22 | async-start | bytes 3440640 | tf_op jit(solution)/shard_map/all_gather | solution.py:40
  424.7 104.4 %reduce-scatter.23.cloned.1.call-start = ((), (), s32[]{:S(2)}) async-start(), calls=%async_computation.23 | async-start | bytes 3440640 | tf_op jit(solution)/shard_map/reduce_scatter | solution.py:44
  493.4 73.7 %reduce-scatter.19.cloned.1.call-start = ((), (), s32[]{:S(2)}) async-start(), calls=%async_computation.19 | async-start | bytes 3440640 | tf_op jit(solution)/shard_map/reduce_scatter | solution.py:34
  500.4 28.6 %copy-start.58 = (f32[1,1,1024]{2,1,0:T(1,128)S(1)}, f32[1,1,1024]{2,1,0:T(1,128)}, u32[]{:S(2)}) copy-start(f32[1,1,1024]{2,1,0:T(1,128)} %copy-done.57) | copy-start | bytes 12292
  500.4 30.7 %copy-start.79 = (f32[6,50]{1,0:T(8,128)S(1)}, f32[6,50]{1,0:T(8,128)}, u32[]{:S(2)}) copy-start(f32[6,50]{1,0:T(8,128)} %copy-done.78) | copy-start | bytes 3604
  500.4 30.7 %copy-start.66 = (f32[6,50]{1,0:T(8,128)S(1)}, f32[6,50]{1,0:T(8,128)}, u32[]{:S(2)}) copy-start(f32[6,50]{1,0:T(8,128)} %copy-done.65) | copy-start | bytes 3604
  500.4 66.7 %copy-start.49 = (f32[1,1,1024]{2,1,0:T(1,128)S(1)}, f32[1,1,1024]{2,1,0:T(1,128)}, u32[]{:S(2)}) copy-start(f32[1,1,1024]{2,1,0:T(1,128)} %get-tuple-element.70) | copy-start | bytes 12292
  500.5 66.7 %copy-start.54 = (f32[6,50]{1,0:T(8,128)S(1)}, f32[6,50]{1,0:T(8,128)}, u32[]{:S(2)}) copy-start(f32[6,50]{1,0:T(8,128)} %copy-done.53) | copy-start | bytes 3604
  500.5 66.6 %copy-start.62 = (f32[6,50]{1,0:T(8,128)S(1)}, f32[6,50]{1,0:T(8,128)}, u32[]{:S(2)}) copy-start(f32[6,50]{1,0:T(8,128)} %copy-done.61) | copy-start | bytes 3604
  500.5 66.6 %copy-start.68 = (f32[6,50]{1,0:T(8,128)S(1)}, f32[6,50]{1,0:T(8,128)}, u32[]{:S(2)}) copy-start(f32[6,50]{1,0:T(8,128)} %copy-done.67) | copy-start | bytes 3604
  500.5 66.6 %copy-start.73 = (f32[6,50]{1,0:T(8,128)S(1)}, f32[6,50]{1,0:T(8,128)}, u32[]{:S(2)}) copy-start(f32[6,50]{1,0:T(8,128)} %copy-done.72) | copy-start | bytes 3604
  500.5 66.6 %copy-start.85 = (f32[1,1,1024]{2,1,0:T(1,128)S(1)}, f32[1,1,1024]{2,1,0:T(1,128)}, u32[]{:S(2)}) copy-start(f32[1,1,1024]{2,1,0:T(1,128)} %get-tuple-element.62) | copy-start | bytes 12292
  500.5 97.7 %all-gather.21.cloned.1.call-start = ((), (), s32[]{:S(2)}) async-start(), calls=%async_computation.24 | async-start | bytes 3440640 | tf_op jit(solution)/shard_map/all_gather | solution.py:40
  567.1 31.1 %copy-start.98 = (f32[1,1024]{1,0:T(1,128)S(1)}, f32[1,1024]{1,0:T(1,128)}, u32[]{:S(2)}) copy-start(f32[1,1024]{1,0:T(1,128)} %copy-done.97) | copy-start | bytes 12292
  571.7 80.0 %reduce-scatter.25.cloned.1.call-start = ((), (), s32[]{:S(2)}) async-start(), calls=%async_computation.25 | async-start | bytes 3440640 | tf_op jit(solution)/shard_map/reduce_scatter | solution.py:44
  616.1 35.7 %copy-start.51 = (f32[1,1,1024]{2,1,0:T(1,128)S(1)}, f32[1,1,1024]{2,1,0:T(1,128)}, u32[]{:S(2)}) copy-start(f32[1,1,1024]{2,1,0:T(1,128)} %copy-done.50) | copy-start | bytes 12292
  616.1 37.8 %copy-start.77 = (f32[6,50]{1,0:T(8,128)S(1)}, f32[6,50]{1,0:T(8,128)}, u32[]{:S(2)}) copy-start(f32[6,50]{1,0:T(8,128)} %copy-done.76) | copy-start | bytes 3604
  616.1 37.8 %copy-start.60 = (f32[6,50]{1,0:T(8,128)S(1)}, f32[6,50]{1,0:T(8,128)}, u32[]{:S(2)}) copy-start(f32[6,50]{1,0:T(8,128)} %copy-done.59) | copy-start | bytes 3604
  616.1 40.2 %copy-start.12 = (f32[6,50,1024]{2,1,0:T(8,128)S(1)}, f32[6,50,1024]{2,1,0:T(8,128)}, u32[]{:S(2)}) copy-start(f32[6,50,1024]{2,1,0:T(8,128)} %get-tuple-element.42) | copy-start | bytes 3686404
  616.1 68.7 %all-gather.23.cloned.1.call-start = ((), (), s32[]{:S(2)}) async-start(), calls=%async_computation.26 | async-start | bytes 3440640 | tf_op jit(solution)/shard_map/all_gather | solution.py:40
  656.3 31.3 %copy-start.81 = (f32[6,50]{1,0:T(8,128)}, f32[6,50]{1,0:T(8,128)S(1)}, u32[]{:S(2)}) copy-start(f32[6,50]{1,0:T(8,128)S(1)} %negate_multiply_fusion.3) | copy-start | bytes 3604
  658.3 95.1 %reduce-scatter.27.cloned.1.call-start = ((), (), s32[]{:S(2)}) async-start(), calls=%async_computation.27 | async-start | bytes 3440640 | tf_op jit(solution)/shard_map/reduce_scatter | solution.py:44
  717.8 107.7 %reduce-scatter.31.cloned.1.call-start = ((), (), s32[]{:S(2)}) async-start(), calls=%async_computation.29 | async-start | bytes 2359296 | tf_op jit(solution)/shard_map/reduce_scatter | solution.py:232
  726.0 227.8 %all-reduce.4.cloned.1.call-start = ((), (), s32[]{:S(2)}) async-start(), calls=%async_computation.32 | async-start | bytes 196608 | tf_op jit(solution)/shard_map/psum | solution.py:251
  734.9 18.6 %copy-start.3 = (f32[6,50,1024]{2,1,0:T(8,128)S(1)}, f32[6,50,1024]{2,1,0:T(8,128)}, u32[]{:S(2)}) copy-start(f32[6,50,1024]{2,1,0:T(8,128)} %copy-done.2) | copy-start | bytes 3686404
  734.9 18.6 %copy-start.48 = (f32[6,50]{1,0:T(8,128)S(1)}, f32[6,50]{1,0:T(8,128)}, u32[]{:S(2)}) copy-start(f32[6,50]{1,0:T(8,128)} %copy-done.47) | copy-start | bytes 3604
  734.9 18.5 %copy-start.56 = (f32[1,1,1024]{2,1,0:T(1,128)S(1)}, f32[1,1,1024]{2,1,0:T(1,128)}, u32[]{:S(2)}) copy-start(f32[1,1,1024]{2,1,0:T(1,128)} %copy-done.55) | copy-start | bytes 12292
  739.9 15.0 %copy-start.75 = (f32[6,50]{1,0:T(8,128)S(1)}, f32[6,50]{1,0:T(8,128)}, u32[]{:S(2)}) copy-start(f32[6,50]{1,0:T(8,128)} %copy-done.74) | copy-start | bytes 3604
  739.9 15.0 %copy-start.64 = (f32[6,50]{1,0:T(8,128)S(1)}, f32[6,50]{1,0:T(8,128)}, u32[]{:S(2)}) copy-start(f32[6,50]{1,0:T(8,128)} %copy-done.63) | copy-start | bytes 3604
  740.0 16.8 %copy-start.92 = (f32[1024]{0:T(1024)S(1)}, f32[1024]{0:T(1024)}, u32[]{:S(2)}) copy-start(f32[1024]{0:T(1024)} %get-tuple-element.20) | copy-start | bytes 12292
  740.0 16.8 %copy-start.93 = (f32[1024]{0:T(1024)S(1)}, f32[1024]{0:T(1024)}, u32[]{:S(2)}) copy-start(f32[1024]{0:T(1024)} %get-tuple-element.18) | copy-start | bytes 12292
  740.0 16.8 %copy-start.94 = (f32[1024]{0:T(1024)S(1)}, f32[1024]{0:T(1024)}, u32[]{:S(2)}) copy-start(f32[1024]{0:T(1024)} %get-tuple-element.16) | copy-start | bytes 12292
  740.0 17.5 %copy-start.86 = (f32[1024]{0:T(1024)S(1)}, f32[1024]{0:T(1024)}, u32[]{:S(2)}) copy-start(f32[1024]{0:T(1024)} %get-tuple-element.45) | copy-start | bytes 12292
  740.0 17.5 %copy-start.87 = (f32[1024]{0:T(1024)S(1)}, f32[1024]{0:T(1024)}, u32[]{:S(2)}) copy-start(f32[1024]{0:T(1024)} %get-tuple-element.28) | copy-start | bytes 12292
  740.0 17.4 %copy-start.88 = (f32[1024]{0:T(1024)S(1)}, f32[1024]{0:T(1024)}, u32[]{:S(2)}) copy-start(f32[1024]{0:T(1024)} %get-tuple-element.43) | copy-start | bytes 12292
  740.0 17.4 %copy-start.89 = (f32[1024]{0:T(1024)S(1)}, f32[1024]{0:T(1024)}, u32[]{:S(2)}) copy-start(f32[1024]{0:T(1024)} %get-tuple-element.26) | copy-start | bytes 12292
  740.0 17.4 %copy-start.90 = (f32[1024]{0:T(1024)S(1)}, f32[1024]{0:T(1024)}, u32[]{:S(2)}) copy-start(f32[1024]{0:T(1024)} %get-tuple-element.40) | copy-start | bytes 12292
  740.0 17.4 %copy-start.91 = (f32[1024]{0:T(1024)S(1)}, f32[1024]{0:T(1024)}, u32[]{:S(2)}) copy-start(f32[1024]{0:T(1024)} %get-tuple-element.24) | copy-start | bytes 12292
  740.0 17.4 %copy-start.96 = (f32[1024]{0:T(1024)S(1)}, f32[1024]{0:T(1024)}, u32[]{:S(2)}) copy-start(f32[1024]{0:T(1024)} %get-tuple-element.38) | copy-start | bytes 12292
  740.3 17.8 %copy-start.69 = (f32[2,2,1024]{2,1,0:T(2,128)}, f32[2,2,1024]{2,1,0:T(2,128)S(1)}, u32[]{:S(2)}) copy-start(f32[2,2,1024]{2,1,0:T(2,128)S(1)} %maximum_dynamic-update-slice_fusion.1) | copy-start | bytes 49156
  758.2 350.1 %reduce-scatter.35.cloned.1.call-start = ((), (), s32[]{:S(2)}) async-start(), calls=%async_computation.31 | async-start | bytes 9437184 | tf_op jit(solution)/shard_map/reduce_scatter | solution.py:238
  766.7 494.2 %reduce-scatter.33.cloned.1.call-start = ((), (), s32[]{:S(2)}) async-start(), calls=%async_computation.30 | async-start | bytes 9437184 | tf_op jit(solution)/shard_map/reduce_scatter | solution.py:235
  780.9 601.5 %reduce-scatter.29.cloned.1.call-start = ((), (), s32[]{:S(2)}) async-start(), calls=%async_computation.28 | async-start | bytes 7077888 | tf_op jit(solution)/shard_map/reduce_scatter | solution.py:229
  792.8 595.0 %copy-start.1 = (bf16[6,50,1024]{2,1,0:T(8,128)(2,1)S(1)}, bf16[6,50,1024]{2,1,0:T(8,128)(2,1)}, u32[]{:S(2)}) copy-start(bf16[6,50,1024]{2,1,0:T(8,128)(2,1)} %param.12) | copy-start | bytes 1843204
  (75 other events, 298.5 us)
Sparse Core Ops, SparseCore 0:
  13.0 28.9 all-gather.8
  75.8 35.4 reduce-scatter.12
  114.3 26.2 all-gather.10
  167.2 35.4 reduce-scatter.14
  205.7 26.2 all-gather.12
  267.4 35.4 reduce-scatter.16
  307.7 26.2 all-gather.14
  336.3 26.2 all-gather.16
  380.0 35.4 reduce-scatter.20
  424.8 26.3 all-gather.18
  493.5 35.4 reduce-scatter.22
  531.6 35.4 reduce-scatter.18
  571.9 26.2 all-gather.20
  616.2 35.4 reduce-scatter.24
  658.4 26.3 all-gather.22
  717.9 35.5 reduce-scatter.26
  757.4 68.0 reduce-scatter.30
  832.6 121.1 all-reduce.3
  958.0 150.2 reduce-scatter.34
  1112.8 148.0 reduce-scatter.32
  1265.0 117.3 reduce-scatter.28
where the time goes:
time: 1410 us; the launch traced here: 1400 us
  waiting for transfers between devices  1020 us (72%)
  matrix products  155 us (11%)
  other arithmetic  100 us (7%)
  local copies, waits for them, and re-layouts  96.5 us (7%)
  between operations  16.9 us (1%)
    reduce_scatter x1, waiting for transfers between devices, local(): lax.psum_scatter(jnp.stack([entry[3] for entry in weight_terms]), 'dp', s...  154 us
    reduce_scatter x1, waiting for transfers between devices, local(): lax.psum_scatter(jnp.stack([entry[2] for entry in weight_terms]), 'dp', s...  153 us
    reduce_scatter x4, waiting for transfers between devices, collect(): lax.psum_scatter(partial_rows.astype(jnp.bfloat16), 'tensor', scatter_dim...  140 us
    psum x1, waiting for transfers between devices, local(): lax.psum((jnp.stack(gain_terms), jnp.stack(shift_terms), qv_full, fc1_ful...  128 us
    reduce_scatter x1, waiting for transfers between devices, local(): lax.psum_scatter(jnp.stack([entry[0] for entry in weight_terms]), 'dp', s...  122 us
    reduce_scatter x4, waiting for transfers between devices, collect_grad(): lax.psum_scatter(partial_rows.astype(jnp.bfloat16), 'tensor', scatter_dim...  112 us
    all_gather x4, waiting for transfers between devices, spread(): lax.all_gather(rows, 'tensor', axis=0, tiled=True)  95.8 us
    all_gather x4, waiting for transfers between devices, spread_grad(): return lax.all_gather(rows, 'tensor', axis=0, tiled=True)  84.8 us
  transfers between devices with their start and end apart: 21, of which 21 were waited for; matrix products, arithmetic and copies ran while one was open for 7% of the time, Pallas kernels for 0%

commit v1 on v0

--- a/solution.py
+++ b/solution.py
@@ -43,6 +43,12 @@
 def collect_grad(partial_rows):
     return lax.psum_scatter(
         partial_rows.astype(jnp.bfloat16), "tensor", scatter_dimension=0, tiled=True
+    ).astype(jnp.float32)
+
+
+def collect_weight(partial_grad, split_dim):
+    return lax.psum_scatter(
+        partial_grad.astype(jnp.bfloat16), "dp", scatter_dimension=split_dim, tiled=True
     ).astype(jnp.float32)
 
 
@@ -224,20 +230,17 @@
         shift_terms.insert(0, jnp.stack([d_shift_attn, d_shift_mlp, shift_attn, shift_fc2]))
         bias_qv_terms.insert(0, d_bias_qv)
         bias_fc1_terms.insert(0, d_bias_fc1)
-        weight_terms.insert(0, (d_qkv, d_out, d_fc1, d_fc2))
+        weight_terms.insert(
+            0,
+            (
+                collect_weight(d_qkv, 0),
+                collect_weight(d_out, 1),
+                collect_weight(d_fc1, 0),
+                collect_weight(d_fc2, 1),
+            ),
+        )
     grad_qkv, grad_out, grad_fc1, grad_fc2 = (
-        lax.psum_scatter(
-            jnp.stack([entry[0] for entry in weight_terms]), "dp", scatter_dimension=1, tiled=True
-        ),
-        lax.psum_scatter(
-            jnp.stack([entry[1] for entry in weight_terms]), "dp", scatter_dimension=2, tiled=True
-        ),
-        lax.psum_scatter(
-            jnp.stack([entry[2] for entry in weight_terms]), "dp", scatter_dimension=1, tiled=True
-        ),
-        lax.psum_scatter(
-            jnp.stack([entry[3] for entry in weight_terms]), "dp", scatter_dimension=2, tiled=True
-        ),
+        jnp.stack([entry[k] for entry in weight_terms]) for k in range(4)
     )
     zero_at = offset_at * 0
     qv_full = lax.dynamic_update_slice(

time: 1410 us -> 1420 us (level)
    unnamed x21 -> x29, waiting for transfers between devices: 0.35 us -> 203 us
    reduce_scatter x4, waiting for transfers between devices: 456 us -> 273 us  [collect_weight(): lax.psum_scatter(partial_grad.astype(jnp.bfloat16), 'dp', scatter_dimensi...]
    all_gather x4, waiting for transfers between devices: 84.8 us -> 58.4 us  [spread_grad(): return lax.all_gather(rows, 'tensor', axis=0, tiled=True)]
    reduce_scatter x4, waiting for transfers between devices: 112 us -> 134 us  [collect_grad(): lax.psum_scatter(partial_rows.astype(jnp.bfloat16), 'tensor', scatter_dim...]
    unnamed x247 -> x219, local copies, waits for them, and re-layouts: 28.9 us -> 41.5 us
  transfers between devices with their start and end apart: 21 -> 25, of which waited for: 21 -> 24; matrix products, arithmetic and copies ran while one was open for 7% -> 10% of each run, Pallas kernels for 0% -> 0%
where the time goes in v1:
time: 1420 us; the launch traced here: 1400 us
  waiting for transfers between devices  1030 us (73%)
  matrix products  164 us (12%)
  local copies, waits for them, and re-layouts  99.4 us (7%)
  other arithmetic  89.3 us (6%)
  between operations  16.4 us (1%)
    reduce_scatter x4, waiting for transfers between devices, collect_weight(): lax.psum_scatter(partial_grad.astype(jnp.bfloat16), 'dp', scatter_dimensi...  273 us
    unnamed x29, waiting for transfers between devices  203 us
    reduce_scatter x4, waiting for transfers between devices, collect(): lax.psum_scatter(partial_rows.astype(jnp.bfloat16), 'tensor', scatter_dim...  140 us
    reduce_scatter x4, waiting for transfers between devices, collect_grad(): lax.psum_scatter(partial_rows.astype(jnp.bfloat16), 'tensor', scatter_dim...  134 us
    psum x1, waiting for transfers between devices, local(): lax.psum((jnp.stack(gain_terms), jnp.stack(shift_terms), qv_full, fc1_ful...  120 us
    all_gather x4, waiting for transfers between devices, spread(): lax.all_gather(rows, 'tensor', axis=0, tiled=True)  96.1 us
    all_gather x4, waiting for transfers between devices, spread_grad(): return lax.all_gather(rows, 'tensor', axis=0, tiled=True)  58.4 us
    unnamed x219, local copies, waits for them, and re-layouts  41.5 us
  transfers between devices with their start and end apart: 25, of which 24 were waited for; matrix products, arithmetic and copies ran while one was open for 10% of the time, Pallas kernels for 0%

profile of v1, /device:TPU:0, one launch (start us, length us, event | category | flops | bytes accessed | tf_op | source)
XLA Modules:
  0.0 1403.5 jit_solution(15501463727336067155)
XLA Ops:
  13.6 6.4 all-reduce
  20.1 20.9 %all-gather.9.cloned.1.call-done = bf16[24,50,1024]{2,1,0:T(8,128)(2,1)} async-done(((bf16[6,50,1024]{2,1,0:T(8,128)(2,1)}), bf16[24,50,1024]{2,1,0:T(8,128)(2,1)}) %all-gather.9.cloned.1.call-update) | async-done | bytes 2457616 | tf_op jit(solution)/shard_map/all_gather | solution.py:28
  41.0 4.6 fusion.18
  65.9 3.7 convolution_convert_fusion.1
  69.7 35.6 %reduce-scatter.25.cloned.1.call-done = bf16[6,50,1024]{2,1,0:T(8,128)(2,1)} async-done(((bf16[24,50,1024]{2,1,0:T(8,128)(2,1)}), bf16[6,50,1024]{2,1,0:T(8,128)(2,1)}) %reduce-scatter.25.cloned.1.call-update) | async-done | bytes 614416 | tf_op jit(solution)/shard_map/reduce_scatter | solution.py:34
  109.0 25.6 %all-gather.11.cloned.1.call-done = bf16[24,50,1024]{2,1,0:T(8,128)(2,1)} async-done(((bf16[6,50,1024]{2,1,0:T(8,128)(2,1)}), bf16[24,50,1024]{2,1,0:T(8,128)(2,1)}) %all-gather.11.cloned.1.call-update) | async-done | bytes 2457616 | tf_op jit(solution)/shard_map/all_gather | solution.py:28
  134.6 7.1 convert_reduce_fusion.3
  141.8 13.3 multiply_convert_fusion.1
  156.6 4.4 convolution_convert_fusion.5
  161.1 35.6 %reduce-scatter.27.cloned.1.call-done = bf16[6,50,1024]{2,1,0:T(8,128)(2,1)} async-done(((bf16[24,50,1024]{2,1,0:T(8,128)(2,1)}), bf16[6,50,1024]{2,1,0:T(8,128)(2,1)}) %reduce-scatter.27.cloned.1.call-update) | async-done | bytes 614416 | tf_op jit(solution)/shard_map/reduce_scatter | solution.py:34
  200.1 25.8 %all-gather.13.cloned.1.call-done = bf16[24,50,1024]{2,1,0:T(8,128)(2,1)} async-done(((bf16[6,50,1024]{2,1,0:T(8,128)(2,1)}), bf16[24,50,1024]{2,1,0:T(8,128)(2,1)}) %all-gather.13.cloned.1.call-update) | async-done | bytes 2457616 | tf_op jit(solution)/shard_map/all_gather | solution.py:28
  225.9 4.6 fusion.14
  233.3 3.3 squeeze.54
  246.0 3.2 squeeze.53
  257.5 3.7 convolution_convert_fusion
  261.3 35.6 %reduce-scatter.29.cloned.1.call-done = bf16[6,50,1024]{2,1,0:T(8,128)(2,1)} async-done(((bf16[24,50,1024]{2,1,0:T(8,128)(2,1)}), bf16[6,50,1024]{2,1,0:T(8,128)(2,1)}) %reduce-scatter.29.cloned.1.call-update) | async-done | bytes 614416 | tf_op jit(solution)/shard_map/reduce_scatter | solution.py:34
  303.2 23.8 %all-gather.15.cloned.1.call-done = bf16[24,50,1024]{2,1,0:T(8,128)(2,1)} async-done(((bf16[6,50,1024]{2,1,0:T(8,128)(2,1)}), bf16[24,50,1024]{2,1,0:T(8,128)(2,1)}) %all-gather.15.cloned.1.call-update) | async-done | bytes 2457616 | tf_op jit(solution)/shard_map/all_gather | solution.py:28
  326.9 7.1 convert_reduce_fusion.1
  336.4 13.5 multiply_convert_fusion
  349.9 5.5 all-gather.17.cloned.1.call-done
  355.5 11.3 convert_reduce_fusion.4
  368.5 4.4 convolution_convert_fusion.3
  373.4 35.2 %reduce-scatter.33.cloned.1.call-done = bf16[6,50,1024]{2,1,0:T(8,128)(2,1)} async-done(((bf16[24,50,1024]{2,1,0:T(8,128)(2,1)}), bf16[6,50,1024]{2,1,0:T(8,128)(2,1)}) %reduce-scatter.33.cloned.1.call-update) | async-done | bytes 614416 | tf_op jit(solution)/shard_map/reduce_scatter | solution.py:44
  413.7 3.2 convert_reduce_fusion.13
  416.9 26.4 %all-gather.19.cloned.1.call-done = bf16[24,50,1024]{2,1,0:T(8,128)(2,1)} async-done(((bf16[6,50,1024]{2,1,0:T(8,128)(2,1)}), bf16[24,50,1024]{2,1,0:T(8,128)(2,1)}) %all-gather.19.cloned.1.call-update) | async-done | bytes 2457616 | tf_op jit(solution)/shard_map/all_gather | solution.py:40
  443.4 3.6 convolution_convert_fusion.11
  447.0 3.0 reshape.321
  450.1 3.2 fusion.62
  462.3 3.2 reshape.307
  468.3 3.2 reshape.306
  474.3 3.3 reshape.305
  481.5 3.9 bitcast_convert_fusion.1
  485.6 7.0 convolution_convert_fusion.4
  492.7 28.5 %reduce-scatter.35.cloned.1.call-done = bf16[6,50,1024]{2,1,0:T(8,128)(2,1)} async-done(((bf16[24,50,1024]{2,1,0:T(8,128)(2,1)}), bf16[6,50,1024]{2,1,0:T(8,128)(2,1)}) %reduce-scatter.35.cloned.1.call-update) | async-done | bytes 614416 | tf_op jit(solution)/shard_map/reduce_scatter | solution.py:44
  525.6 33.5 %reduce-scatter.31.cloned.1.call-done = bf16[6,50,1024]{2,1,0:T(8,128)(2,1)} async-done(((bf16[24,50,1024]{2,1,0:T(8,128)(2,1)}), bf16[6,50,1024]{2,1,0:T(8,128)(2,1)}) %reduce-scatter.31.cloned.1.call-update) | async-done | bytes 614416 | tf_op jit(solution)/shard_map/reduce_scatter | solution.py:34
  559.2 4.6 convert_reduce_fusion.14
  563.8 26.4 %all-gather.21.cloned.1.call-done = bf16[24,50,1024]{2,1,0:T(8,128)(2,1)} async-done(((bf16[6,50,1024]{2,1,0:T(8,128)(2,1)}), bf16[24,50,1024]{2,1,0:T(8,128)(2,1)}) %all-gather.21.cloned.1.call-update) | async-done | bytes 2457616 | tf_op jit(solution)/shard_map/all_gather | solution.py:40
  590.2 11.3 convert_reduce_fusion.5
  603.1 4.6 convolution_convert_fusion.2
  607.8 35.6 %reduce-scatter.37.cloned.1.call-done = bf16[6,50,1024]{2,1,0:T(8,128)(2,1)} async-done(((bf16[24,50,1024]{2,1,0:T(8,128)(2,1)}), bf16[6,50,1024]{2,1,0:T(8,128)(2,1)}) %reduce-scatter.37.cloned.1.call-update) | async-done | bytes 614416 | tf_op jit(solution)/shard_map/reduce_scatter | solution.py:44
  650.1 6.1 bitcast_convert_fusion.2
  658.9 4.6 fusion.92
  665.6 6.5 bitcast_convert_fusion.3
  672.1 3.9 copy.160
  676.5 7.6 bitcast_convert_fusion.4
  684.2 6.5 bitcast_convert_fusion.5
  690.9 3.8 fusion.95
  695.7 5.6 bitcast_convert_fusion.6
  701.5 3.0 convolution_convert_fusion.10
  712.5 3.3 multiply_reduce_fusion
  720.5 3.2 reshape.309
  728.6 3.8 bitcast_convert_fusion.7
  732.7 6.1 bitcast_convert_fusion
  738.9 9.3 reduce-scatter.55.cloned.1.call-done
  749.6 63.6 %reduce-scatter.51.cloned.1.call-done = bf16[128,256]{1,0:T(8,128)(2,1)} async-done(((bf16[1024,256]{1,0:T(8,128)(2,1)}), bf16[128,256]{1,0:T(8,128)(2,1)}) %reduce-scatter.51.cloned.1.call-update) | async-done | bytes 65552
  814.2 69.2 %reduce-scatter.53.cloned.1.call-done = bf16[128,1024]{1,0:T(8,128)(2,1)} async-done(((bf16[1024,1024]{1,0:T(8,128)(2,1)}), bf16[128,1024]{1,0:T(8,128)(2,1)}) %reduce-scatter.53.cloned.1.call-update) | async-done | bytes 262160
  885.7 68.2 %reduce-scatter.47.cloned.1.call-done = bf16[128,1024]{1,0:T(8,128)(2,1)} async-done(((bf16[1024,1024]{1,0:T(8,128)(2,1)}), bf16[128,1024]{1,0:T(8,128)(2,1)}) %reduce-scatter.47.cloned.1.call-update) | async-done | bytes 262160 | tf_op jit(solution)/shard_map/reduce_scatter | solution.py:50
  953.9 70.3 %reduce-scatter.45.cloned.1.call-done = bf16[128,1024]{1,0:T(8,128)(2,1)} async-done(((bf16[1024,1024]{1,0:T(8,128)(2,1)}), bf16[128,1024]{1,0:T(8,128)(2,1)}) %reduce-scatter.45.cloned.1.call-update) | async-done | bytes 262160 | tf_op jit(solution)/shard_map/reduce_scatter | solution.py:50
  1027.9 60.6 %reduce-scatter.49.cloned.1.call-done = bf16[128,256]{1,0:T(8,128)(2,1)} async-done(((bf16[1024,256]{1,0:T(8,128)(2,1)}), bf16[128,256]{1,0:T(8,128)(2,1)}) %reduce-scatter.49.cloned.1.call-update) | async-done | bytes 65552
  1090.2 66.7 %reduce-scatter.43.cloned.1.call-done = bf16[128,3,256]{2,0,1:T(8,128)(2,1)} async-done(((bf16[1024,3,256]{2,0,1:T(8,128)(2,1)}), bf16[128,3,256]{2,0,1:T(8,128)(2,1)}) %reduce-scatter.43.cloned.1.call-update) | async-done | bytes 196624 | tf_op jit(solution)/shard_map/reduce_scatter | solution.py:50
  1156.9 68.0 %reduce-scatter.41.cloned.1.call-done = bf16[128,3,256]{2,0,1:T(8,128)(2,1)} async-done(((bf16[1024,3,256]{2,0,1:T(8,128)(2,1)}), bf16[128,3,256]{2,0,1:T(8,128)(2,1)}) %reduce-scatter.41.cloned.1.call-update) | async-done | bytes 196624 | tf_op jit(solution)/shard_map/reduce_scatter | solution.py:50
  1227.0 34.9 %reduce-scatter.39.cloned.1.call-done = bf16[6,50,1024]{2,1,0:T(8,128)(2,1)} async-done(((bf16[24,50,1024]{2,1,0:T(8,128)(2,1)}), bf16[6,50,1024]{2,1,0:T(8,128)(2,1)}) %reduce-scatter.39.cloned.1.call-update) | async-done | bytes 614416 | tf_op jit(solution)/shard_map/reduce_scatter | solution.py:44
  1266.7 4.6 fusion.82
  1271.3 120.0 %all-reduce.4.cloned.1.call-done = (f32[2,2,1024]{2,1,0:T(2,128)}, f32[2,4,1024]{2,1,0:T(4,128)}, f32[2,2,1024]{2,1,0:T(2,128)}, f32[2,4096]{1,0:T(2,128)}) async-done(((f32[2,2,1024]{2,1,0:T(2,128)}, f32[2,4,1024]{2,1,0:T(4,128)}, f32[2,2,1024]{2,1,0:T(2,128)}, f32[2,4096]{1,0:T(2,128)}), (f32[2,2,1024]{2,1,0:T(2,128)}, f32[2,4,1024]{2,1,0:T(4,128)}, f32[2,2,1024]{2,1,0:T(2,128)}, ...) | async-done | bytes 98320 | tf_op jit(solution)/shard_map/psum | solution.py:254
  (380 shorter events, 148.7 us)
Async XLA Ops:
  7.2 33.8 %all-gather.9.cloned.1.call-start = ((), (), s32[]{:S(2)}) async-start(), calls=%async_computation.16 | async-start | bytes 3440640 | tf_op jit(solution)/shard_map/all_gather | solution.py:28
  9.5 95.8 %copy-start.4 = (f32[6,50,1024]{2,1,0:T(8,128)}, f32[6,50,1024]{2,1,0:T(8,128)S(1)}, u32[]{:S(2)}) copy-start(f32[6,50,1024]{2,1,0:T(8,128)S(1)} %get-tuple-element.77) | copy-start | bytes 3686404
  9.5 36.1 %copy-start.52 = (f32[6,50]{1,0:T(8,128)}, f32[6,50]{1,0:T(8,128)S(1)}, u32[]{:S(2)}) copy-start(f32[6,50]{1,0:T(8,128)S(1)} %broadcast_multiply_fusion.3) | copy-start | bytes 3604
  10.6 35.0 %copy-start.61 = (f32[6,50]{1,0:T(8,128)}, f32[6,50]{1,0:T(8,128)S(1)}, u32[]{:S(2)}) copy-start(f32[6,50]{1,0:T(8,128)S(1)} %fusion.141) | copy-start | bytes 3604
  10.7 35.0 %copy-start.57 = (f32[1,1,1024]{2,1,0:T(1,128)}, f32[1,1,1024]{2,1,0:T(1,128)S(1)}, u32[]{:S(2)}) copy-start(f32[1,1,1024]{2,1,0:T(1,128)S(1)} %get-tuple-element.72) | copy-start | bytes 12292
  10.7 637.3 %copy-start.54 = (f32[1,1,1024]{2,1,0:T(1,128)}, f32[1,1,1024]{2,1,0:T(1,128)S(1)}, u32[]{:S(2)}) copy-start(f32[1,1,1024]{2,1,0:T(1,128)S(1)} %get-tuple-element.71) | copy-start | bytes 12292
  11.8 93.5 %reduce-scatter.25.cloned.1.call-start = ((), (), s32[]{:S(2)}) async-start(), calls=%async_computation.17 | async-start | bytes 3440640 | tf_op jit(solution)/shard_map/reduce_scatter | solution.py:34
  69.7 64.9 %all-gather.11.cloned.1.call-start = ((), (), s32[]{:S(2)}) async-start(), calls=%async_computation.18 | async-start | bytes 3440640 | tf_op jit(solution)/shard_map/all_gather | solution.py:28
  106.7 541.3 %copy-start.2 = (f32[6,50,1024]{2,1,0:T(8,128)}, f32[6,50,1024]{2,1,0:T(8,128)S(1)}, u32[]{:S(2)}) copy-start(f32[6,50,1024]{2,1,0:T(8,128)S(1)} %get-tuple-element.56) | copy-start | bytes 3686404
  106.7 541.3 %copy-start.50 = (f32[6,50]{1,0:T(8,128)}, f32[6,50]{1,0:T(8,128)S(1)}, u32[]{:S(2)}) copy-start(f32[6,50]{1,0:T(8,128)S(1)} %broadcast_multiply_fusion.2) | copy-start | bytes 3604
  107.0 541.0 %copy-start.59 = (f32[6,50]{1,0:T(8,128)}, f32[6,50]{1,0:T(8,128)S(1)}, u32[]{:S(2)}) copy-start(f32[6,50]{1,0:T(8,128)S(1)} %fusion.142) | copy-start | bytes 3604
  108.2 88.5 %reduce-scatter.27.cloned.1.call-start = ((), (), s32[]{:S(2)}) async-start(), calls=%async_computation.19 | async-start | bytes 3440640 | tf_op jit(solution)/shard_map/reduce_scatter | solution.py:34
  109.0 32.7 %copy-start.83 = (f32[1,1024]{1,0:T(1,128)}, f32[1,1024]{1,0:T(1,128)S(1)}, u32[]{:S(2)}) copy-start(f32[1,1024]{1,0:T(1,128)S(1)} %get-tuple-element.75) | copy-start | bytes 12292
  141.8 14.8 %copy-start.91 = (bf16[2,1024,1024]{2,1,0:T(8,128)(2,1)S(1)}, bf16[2,1024,1024]{2,1,0:T(8,128)(2,1)}, u32[]{:S(2)}) copy-start(bf16[2,1024,1024]{2,1,0:T(8,128)(2,1)} %param.22) | copy-start | bytes 12582916
  161.0 64.9 %all-gather.13.cloned.1.call-start = ((), (), s32[]{:S(2)}) async-start(), calls=%async_computation.20 | async-start | bytes 3440640 | tf_op jit(solution)/shard_map/all_gather | solution.py:28
  199.5 97.4 %reduce-scatter.29.cloned.1.call-start = ((), (), s32[]{:S(2)}) async-start(), calls=%async_computation.21 | async-start | bytes 3440640 | tf_op jit(solution)/shard_map/reduce_scatter | solution.py:34
  261.3 65.7 %all-gather.15.cloned.1.call-start = ((), (), s32[]{:S(2)}) async-start(), calls=%async_computation.22 | async-start | bytes 3440640 | tf_op jit(solution)/shard_map/all_gather | solution.py:28
  300.5 55.0 %all-gather.17.cloned.1.call-start = ((), (), s32[]{:S(2)}) async-start(), calls=%async_computation.24 | async-start | bytes 3440640 | tf_op jit(solution)/shard_map/all_gather | solution.py:40
  303.0 105.6 %reduce-scatter.33.cloned.1.call-start = ((), (), s32[]{:S(2)}) async-start(), calls=%async_computation.25 | async-start | bytes 3440640 | tf_op jit(solution)/shard_map/reduce_scatter | solution.py:44
  372.9 70.5 %all-gather.19.cloned.1.call-start = ((), (), s32[]{:S(2)}) async-start(), calls=%async_computation.26 | async-start | bytes 3440640 | tf_op jit(solution)/shard_map/all_gather | solution.py:40
  416.9 104.2 %reduce-scatter.35.cloned.1.call-start = ((), (), s32[]{:S(2)}) async-start(), calls=%async_computation.27 | async-start | bytes 3440640 | tf_op jit(solution)/shard_map/reduce_scatter | solution.py:44
  485.5 73.7 %reduce-scatter.31.cloned.1.call-start = ((), (), s32[]{:S(2)}) async-start(), calls=%async_computation.23 | async-start | bytes 3440640 | tf_op jit(solution)/shard_map/reduce_scatter | solution.py:34
  492.6 97.6 %all-gather.21.cloned.1.call-start = ((), (), s32[]{:S(2)}) async-start(), calls=%async_computation.28 | async-start | bytes 3440640 | tf_op jit(solution)/shard_map/all_gather | solution.py:40
  559.2 31.0 %copy-start.84 = (f32[1,1024]{1,0:T(1,128)S(1)}, f32[1,1024]{1,0:T(1,128)}, u32[]{:S(2)}) copy-start(f32[1,1024]{1,0:T(1,128)} %copy-done.83) | copy-start | bytes 12292
  563.8 79.6 %reduce-scatter.37.cloned.1.call-start = ((), (), s32[]{:S(2)}) async-start(), calls=%async_computation.29 | async-start | bytes 3440640 | tf_op jit(solution)/shard_map/reduce_scatter | solution.py:44
  607.8 40.3 %copy-start.16 = (f32[6,50,1024]{2,1,0:T(8,128)S(1)}, f32[6,50,1024]{2,1,0:T(8,128)}, u32[]{:S(2)}) copy-start(f32[6,50,1024]{2,1,0:T(8,128)} %get-tuple-element.42) | copy-start | bytes 3686404
  607.8 83.1 %all-gather.23.cloned.1.call-start = ((), (), s32[]{:S(2)}) async-start(), calls=%async_computation.30 | async-start | bytes 3440640 | tf_op jit(solution)/shard_map/all_gather | solution.py:40
  650.1 98.1 %reduce-scatter.55.cloned.1.call-start = ((), (), s32[]{:S(2)}) async-start(), calls=%async_computation.39 | async-start | bytes 2359296
  658.8 154.4 %reduce-scatter.51.cloned.1.call-start = ((), (), s32[]{:S(2)}) async-start(), calls=%async_computation.37 | async-start | bytes 589824
  665.6 217.9 %reduce-scatter.53.cloned.1.call-start = ((), (), s32[]{:S(2)}) async-start(), calls=%async_computation.38 | async-start | bytes 2359296
  676.1 277.8 %reduce-scatter.47.cloned.1.call-start = ((), (), s32[]{:S(2)}) async-start(), calls=%async_computation.35 | async-start | bytes 2359296 | tf_op jit(solution)/shard_map/reduce_scatter | solution.py:50
  684.2 340.0 %reduce-scatter.45.cloned.1.call-start = ((), (), s32[]{:S(2)}) async-start(), calls=%async_computation.34 | async-start | bytes 2359296 | tf_op jit(solution)/shard_map/reduce_scatter | solution.py:50
  690.8 397.7 %reduce-scatter.49.cloned.1.call-start = ((), (), s32[]{:S(2)}) async-start(), calls=%async_computation.36 | async-start | bytes 589824
  695.7 461.2 %reduce-scatter.43.cloned.1.call-start = ((), (), s32[]{:S(2)}) async-start(), calls=%async_computation.33 | async-start | bytes 1769472 | tf_op jit(solution)/shard_map/reduce_scatter | solution.py:50
  701.4 523.4 %reduce-scatter.41.cloned.1.call-start = ((), (), s32[]{:S(2)}) async-start(), calls=%async_computation.32 | async-start | bytes 1769472 | tf_op jit(solution)/shard_map/reduce_scatter | solution.py:50
  732.4 529.4 %reduce-scatter.39.cloned.1.call-start = ((), (), s32[]{:S(2)}) async-start(), calls=%async_computation.31 | async-start | bytes 3440640 | tf_op jit(solution)/shard_map/reduce_scatter | solution.py:44
  738.8 75.4 %copy-start.88 = (f32[1024]{0:T(1024)S(1)}, f32[1024]{0:T(1024)}, u32[]{:S(2)}) copy-start(f32[1024]{0:T(1024)} %get-tuple-element.88) | copy-start | bytes 12292
  738.8 75.4 %copy-start.89 = (f32[1024]{0:T(1024)S(1)}, f32[1024]{0:T(1024)}, u32[]{:S(2)}) copy-start(f32[1024]{0:T(1024)} %get-tuple-element.90) | copy-start | bytes 12292
  738.8 652.5 %all-reduce.4.cloned.1.call-start = ((), (), s32[]{:S(2)}) async-start(), calls=%async_computation.40 | async-start | bytes 196608 | tf_op jit(solution)/shard_map/psum | solution.py:254
  814.2 275.9 %copy-start.56 = (f32[2,4096]{1,0:T(2,128)}, f32[2,4096]{1,0:T(2,128)S(1)}, u32[]{:S(2)}) copy-start(f32[2,4096]{1,0:T(2,128)S(1)} %maximum_dynamic-update-slice_fusion) | copy-start | bytes 98308
  884.6 377.2 %copy-start.5 = (f32[6,50,1024]{2,1,0:T(8,128)S(1)}, f32[6,50,1024]{2,1,0:T(8,128)}, u32[]{:S(2)}) copy-start(f32[6,50,1024]{2,1,0:T(8,128)} %copy-done.4) | copy-start | bytes 3686404
  884.6 377.2 %copy-start.53 = (f32[6,50]{1,0:T(8,128)S(1)}, f32[6,50]{1,0:T(8,128)}, u32[]{:S(2)}) copy-start(f32[6,50]{1,0:T(8,128)} %copy-done.52) | copy-start | bytes 3604
  884.6 377.2 %copy-start.58 = (f32[1,1,1024]{2,1,0:T(1,128)S(1)}, f32[1,1,1024]{2,1,0:T(1,128)}, u32[]{:S(2)}) copy-start(f32[1,1,1024]{2,1,0:T(1,128)} %copy-done.57) | copy-start | bytes 12292
  1026.2 237.1 %copy-start.67 = (f32[6,50]{1,0:T(8,128)S(1)}, f32[6,50]{1,0:T(8,128)}, u32[]{:S(2)}) copy-start(f32[6,50]{1,0:T(8,128)} %copy-done.66) | copy-start | bytes 3604
  1026.2 237.1 %copy-start.62 = (f32[6,50]{1,0:T(8,128)S(1)}, f32[6,50]{1,0:T(8,128)}, u32[]{:S(2)}) copy-start(f32[6,50]{1,0:T(8,128)} %copy-done.61) | copy-start | bytes 3604
  1027.9 237.3 %copy-start.63 = (f32[2,2,1024]{2,1,0:T(2,128)}, f32[2,2,1024]{2,1,0:T(2,128)S(1)}, u32[]{:S(2)}) copy-start(f32[2,2,1024]{2,1,0:T(2,128)S(1)} %maximum_dynamic-update-slice_fusion.1) | copy-start | bytes 49156
  1090.2 175.0 %copy-start.72 = (f32[1024]{0:T(1024)S(1)}, f32[1024]{0:T(1024)}, u32[]{:S(2)}) copy-start(f32[1024]{0:T(1024)} %get-tuple-element.45) | copy-start | bytes 12292
  1090.2 175.0 %copy-start.73 = (f32[1024]{0:T(1024)S(1)}, f32[1024]{0:T(1024)}, u32[]{:S(2)}) copy-start(f32[1024]{0:T(1024)} %get-tuple-element.28) | copy-start | bytes 12292
  1090.2 175.0 %copy-start.74 = (f32[1024]{0:T(1024)S(1)}, f32[1024]{0:T(1024)}, u32[]{:S(2)}) copy-start(f32[1024]{0:T(1024)} %get-tuple-element.43) | copy-start | bytes 12292
  1090.2 175.0 %copy-start.75 = (f32[1024]{0:T(1024)S(1)}, f32[1024]{0:T(1024)}, u32[]{:S(2)}) copy-start(f32[1024]{0:T(1024)} %get-tuple-element.26) | copy-start | bytes 12292
  1090.2 175.0 %copy-start.76 = (f32[1024]{0:T(1024)S(1)}, f32[1024]{0:T(1024)}, u32[]{:S(2)}) copy-start(f32[1024]{0:T(1024)} %get-tuple-element.40) | copy-start | bytes 12292
  1090.2 175.0 %copy-start.77 = (f32[1024]{0:T(1024)S(1)}, f32[1024]{0:T(1024)}, u32[]{:S(2)}) copy-start(f32[1024]{0:T(1024)} %get-tuple-element.24) | copy-start | bytes 12292
  1090.2 175.0 %copy-start.82 = (f32[1024]{0:T(1024)S(1)}, f32[1024]{0:T(1024)}, u32[]{:S(2)}) copy-start(f32[1024]{0:T(1024)} %get-tuple-element.38) | copy-start | bytes 12292
  1224.8 41.1 %copy-start.78 = (f32[1024]{0:T(1024)S(1)}, f32[1024]{0:T(1024)}, u32[]{:S(2)}) copy-start(f32[1024]{0:T(1024)} %get-tuple-element.20) | copy-start | bytes 12292
  1224.8 41.1 %copy-start.79 = (f32[1024]{0:T(1024)S(1)}, f32[1024]{0:T(1024)}, u32[]{:S(2)}) copy-start(f32[1024]{0:T(1024)} %get-tuple-element.18) | copy-start | bytes 12292
  1224.8 41.1 %copy-start.80 = (f32[1024]{0:T(1024)S(1)}, f32[1024]{0:T(1024)}, u32[]{:S(2)}) copy-start(f32[1024]{0:T(1024)} %get-tuple-element.16) | copy-start | bytes 12292
  1224.8 41.7 %copy-start.3 = (f32[6,50,1024]{2,1,0:T(8,128)S(1)}, f32[6,50,1024]{2,1,0:T(8,128)}, u32[]{:S(2)}) copy-start(f32[6,50,1024]{2,1,0:T(8,128)} %copy-done.2) | copy-start | bytes 3686404
  1224.8 41.7 %copy-start.51 = (f32[6,50]{1,0:T(8,128)S(1)}, f32[6,50]{1,0:T(8,128)}, u32[]{:S(2)}) copy-start(f32[6,50]{1,0:T(8,128)} %copy-done.50) | copy-start | bytes 3604
  1224.9 41.7 %copy-start.55 = (f32[1,1,1024]{2,1,0:T(1,128)S(1)}, f32[1,1,1024]{2,1,0:T(1,128)}, u32[]{:S(2)}) copy-start(f32[1,1,1024]{2,1,0:T(1,128)} %copy-done.54) | copy-start | bytes 12292
  1224.9 41.7 %copy-start.60 = (f32[6,50]{1,0:T(8,128)S(1)}, f32[6,50]{1,0:T(8,128)}, u32[]{:S(2)}) copy-start(f32[6,50]{1,0:T(8,128)} %copy-done.59) | copy-start | bytes 3604
  1224.9 41.7 %copy-start.65 = (f32[6,50]{1,0:T(8,128)S(1)}, f32[6,50]{1,0:T(8,128)}, u32[]{:S(2)}) copy-start(f32[6,50]{1,0:T(8,128)} %copy-done.64) | copy-start | bytes 3604
  1224.9 41.7 %copy-start.69 = (f32[6,50]{1,0:T(8,128)S(1)}, f32[6,50]{1,0:T(8,128)}, u32[]{:S(2)}) copy-start(f32[6,50]{1,0:T(8,128)} %copy-done.68) | copy-start | bytes 3604
  1224.9 41.7 %copy-start.71 = (s32[6,50]{1,0:T(8,128)S(1)}, s32[6,50]{1,0:T(8,128)}, u32[]{:S(2)}) copy-start(s32[6,50]{1,0:T(8,128)} %param.13) | copy-start | bytes 3604
  1266.6 130.1 %copy-start.1 = (bf16[6,50,1024]{2,1,0:T(8,128)(2,1)S(1)}, bf16[6,50,1024]{2,1,0:T(8,128)(2,1)}, u32[]{:S(2)}) copy-start(bf16[6,50,1024]{2,1,0:T(8,128)(2,1)} %param.12) | copy-start | bytes 1843204
  (61 other events, 239.3 us)
Sparse Core Ops, SparseCore 0:
  12.0 28.9 all-gather.8
  69.8 35.4 reduce-scatter.24
  108.3 26.2 all-gather.10
  161.1 35.4 reduce-scatter.26
  199.6 26.2 all-gather.12
  261.4 35.4 reduce-scatter.28
  300.6 26.2 all-gather.14
  329.2 26.2 all-gather.16
  373.0 35.4 reduce-scatter.32
  417.0 26.3 all-gather.18
  485.6 35.4 reduce-scatter.34
  523.7 35.4 reduce-scatter.30
  563.9 26.2 all-gather.20
  607.9 35.4 reduce-scatter.36
  650.2 26.2 all-gather.22
  680.3 67.8 reduce-scatter.54
  752.3 60.8 reduce-scatter.50
  816.6 66.8 reduce-scatter.52
  887.0 66.8 reduce-scatter.46
  957.3 66.8 reduce-scatter.44
  1027.5 60.9 reduce-scatter.48
  1092.3 64.5 reduce-scatter.42
  1160.3 64.4 reduce-scatter.40
  1227.4 34.3 reduce-scatter.38
  1269.1 122.1 all-reduce.3

commit v2 on v1

v2 whole, which is shorter than its diff:
```python
from functools import partial

import jax
import jax.numpy as jnp
from jax import lax
from jax.experimental import pallas as pl
from jax.experimental.pallas import tpu as pltpu
from jax.sharding import PartitionSpec as P

D = 1024
HEAD = 64
FF = 4096
LAYERS = 2
PATCHES = 50
EPS = 1e-06
HIGHEST = lax.Precision.HIGHEST
F32 = jnp.float32
BF16 = jnp.bfloat16

GROUPS = 2
ROWS = 160
LIVE = 150
COLS = 128
SCALE = HEAD ** (-0.5)


def dot(a, b, lhs=1, rhs=0):
    return lax.dot_general(a, b, (((lhs,), (rhs,)), ((), ())), preferred_element_type=F32)


def remote(src, dst, send, recv, peer):
    return pltpu.make_async_remote_copy(
        src_ref=src,
        dst_ref=dst,
        send_sem=send,
        recv_sem=recv,
        device_id={"tensor": peer},
        device_id_type=pl.DeviceIdType.MESH,
    )


def norm_parts(values):
    average = jnp.mean(values, axis=-1, keepdims=True)
    centred = values - average
    variance = jnp.mean(centred * centred, axis=-1, keepdims=True)
    scale = lax.rsqrt(variance + EPS)
    return centred * scale, scale


def head_mask(h, width):
    lane = lax.broadcasted_iota(jnp.int32, (1, width), 1)
    return (lane // HEAD == h).astype(F32).astype(BF16)


class Exchange:
    def __init__(self, x_own, gath, part, bufs, sems):
        self.x_own, self.gath, self.part = x_own, gath, part
        self.out_po, self.out_pd, self.out_y, self.in_po, self.in_pd, self.in_y = bufs
        self.sem = sems
        me = lax.axis_index("tensor")
        self.me = me
        self.mate = me + 1 - 2 * (me % 2)
        self.far = (me + 2) % 4
        self.diag = (self.mate + 2) % 4

    def barrier(self):
        sem = pltpu.get_barrier_semaphore()
        for peer in (self.mate, self.far):
            pl.semaphore_signal(
                sem, inc=1, device_id={"tensor": peer}, device_id_type=pl.DeviceIdType.MESH
            )
        pl.semaphore_wait(sem, 2)

    def copy(self, kind, g):
        s = self.sem
        own = GROUPS * self.me + g
        if kind == 0:
            src, dst, peer = self.x_own.at[g], self.gath.at[own], self.far
        elif kind == 1:
            src, dst, peer = self.x_own.at[g], self.gath.at[own], self.mate
        elif kind == 2:
            slot = GROUPS * self.far + g
            src, dst, peer = self.gath.at[slot], self.gath.at[slot], self.mate
        elif kind == 3:
            src, dst, peer = self.out_po.at[g], self.in_po.at[g], self.mate
        elif kind == 4:
            src, dst, peer = self.out_pd.at[g], self.in_pd.at[g], self.mate
        else:
            src, dst, peer = self.out_y.at[g], self.in_y.at[g], self.far
        return remote(src, dst, s.at[0, kind, g], s.at[1, kind, g], peer)

    def local(self, g):
        return pltpu.make_async_copy(
            self.x_own.at[g], self.gath.at[GROUPS * self.me + g], self.sem.at[0, 6, g]
        )

    def begin(self):
        self.barrier()
        for g in range(GROUPS):
            self.copy(0, g).start()
            self.copy(1, g).start()
            self.local(g).start()

    def slot(self, i):
        owner = jnp.where(
            i < 2, self.me, jnp.where(i < 4, self.mate, jnp.where(i % 2 == 0, self.far, self.diag))
        )
        g = jnp.where(i < 4, i % 2, (i - 4) // 2)
        return GROUPS * owner + g

    def before(self, i):
        for g in range(GROUPS):

            @pl.when(i == g)
            def _():
                self.local(g).wait()

            @pl.when(i == 2 + g)
            def _():
                self.copy(1, g).wait_recv()

            @pl.when(i == 4 + 2 * g)
            def _():
                self.copy(0, g).wait_recv()
                self.copy(2, g).start()

            @pl.when(i == 5 + 2 * g)
            def _():
                self.copy(2, g).wait_recv()

    def after(self, i):
        for g in range(GROUPS):

            @pl.when(i == 2 + g)
            def _():
                self.out_po[g] = self.part[2 + g].astype(BF16)
                self.copy(3, g).start()

            @pl.when(i == 5 + 2 * g)
            def _():
                self.out_pd[g] = self.part[5 + 2 * g].astype(BF16)
                self.copy(4, g).start()
                self.copy(4, g).wait_recv()
                self.out_y[g] = (self.part[4 + 2 * g] + self.in_pd[g].astype(F32)).astype(BF16)
                self.copy(5, g).start()

    def total(self, g):
        self.copy(3, g).wait_recv()
        self.copy(5, g).wait_recv()
        return self.part[g] + self.in_po[g].astype(F32) + self.in_y[g].astype(F32)

    def end(self):
        for g in range(GROUPS):
            for kind in range(6):
                self.copy(kind, g).wait_send()


def exchange_scratch():
    return [
        pltpu.VMEM((8, ROWS, D), BF16),
        pltpu.VMEM((8, ROWS, D), F32),
    ] + [pltpu.VMEM((GROUPS, ROWS, D), BF16)] * 6 + [pltpu.SemaphoreType.DMA((2, 7, GROUPS))]


class Moves:
    def __init__(self, sems):
        self.sems = sems

    def load(self, n, src, dst):
        return pltpu.make_async_copy(src, dst, self.sems.at[n])


def keep_pad(old, new):
    row = lax.broadcasted_iota(jnp.int32, (ROWS, D), 0)
    return jnp.where(row >= LIVE, old.astype(F32), new)


def attend_kernel(
    x_own, norm2, shift_a, shift_n, bias, resid_h, wqkv_h, wout_h,
    gath_h, qkv_h, prob_h, att_h, middle, next_own,
    gath, part, out_po, out_pd, out_y, in_po, in_pd, in_y, ex_sem,
    resid, wqkv, wout, qkv, prob, att, load_sem, save_sem,
):
    ex = Exchange(x_own, gath, part, (out_po, out_pd, out_y, in_po, in_pd, in_y), ex_sem)
    width = wout.shape[0]
    loads = Moves(load_sem)
    for n, pair in enumerate(((wqkv_h, wqkv), (wout_h, wout), (resid_h, resid))):
        loads.load(n, *pair).start()
    ex.begin()
    loads.load(0, wqkv_h, wqkv).wait()
    loads.load(1, wout_h, wout).wait()
    pairs = ((gath, gath_h), (qkv, qkv_h), (prob, prob_h), (att, att_h))

    def saves(slot):
        return [
            pltpu.make_async_copy(a.at[slot], b.at[slot], save_sem.at[n, slot])
            for n, (a, b) in enumerate(pairs)
        ]

    def step(i, _):
        ex.before(i)
        slot = ex.slot(i)
        x = gath[slot]
        triple = dot(x, wqkv[...])
        q = (triple[:, :width] + bias[0:1]).astype(BF16)
        k = triple[:, width : 2 * width].astype(BF16)
        v = (triple[:, 2 * width :] + bias[1:2]).astype(BF16)
        qkv[slot, :, 0:width] = q
        qkv[slot, :, width : 2 * width] = k
        qkv[slot, :, 2 * width :] = v
        counts = gath[slot, ROWS - 16 : ROWS, 0:256][:, 0:ROWS].astype(F32)
        lane = lax.broadcasted_iota(jnp.int32, (1, ROWS), 1)
        image = lane // PATCHES
        count = jnp.where(
            image == 0, counts[6:7], jnp.where(image == 1, counts[7:8], counts[8:9])
        )
        fits = (lane - image * PATCHES).astype(F32) < count
        row = lax.broadcasted_iota(jnp.int32, (ROWS, ROWS), 0)
        col = lax.broadcasted_iota(jnp.int32, (ROWS, ROWS), 1)
        same = jnp.minimum(row // PATCHES, 2) == col // PATCHES
        veil = jnp.where(same, 0.0, -1e30) + jnp.where(fits, 0.0, -1e30)
        mixed = jnp.zeros((ROWS, width), F32)
        for h in range(width // HEAD):
            mask = head_mask(h, width)
            scores = dot(q * mask, k, 1, 1) * SCALE + veil
            peak = jnp.max(scores, axis=-1, keepdims=True)
            raised = jnp.exp(scores - peak)
            weight = raised * (1.0 / jnp.sum(raised, axis=-1, keepdims=True))
            rounded = weight.astype(BF16)
            prob[slot, h * ROWS : (h + 1) * ROWS] = rounded
            mixed = mixed + dot(rounded, v * mask)
        mixed = mixed.astype(BF16)
        att[slot] = mixed
        part[i] = dot(mixed, wout[...])
        for copy in saves(slot):
            copy.start()
        ex.after(i)
        return 0

    lax.fori_loop(0, 8, step, 0)
    loads.load(2, resid_h, resid).wait()
    for g in range(GROUPS):
        mid = resid[g] + ex.total(g) + shift_a[...]
        middle[g] = mid
        unit, _ = norm_parts(mid)
        next_own[g] = keep_pad(x_own[g], unit * norm2[...] + shift_n[...]).astype(BF16)
    ex.end()

    def drain(slot, _):
        for copy in saves(slot):
            copy.wait()
        return 0

    lax.fori_loop(0, 8, drain, 0)


def erf_parts(pre):
    cdf = 0.5 * (1.0 + lax.erf(pre * (0.5 ** 0.5)))
    pdf = jnp.exp(-0.5 * pre * pre) * 0.3989422804014327
    return cdf, pdf


def mlp_kernel(
    x_own, gain_n, shift_a, shift_n, bias, middle_h, w1_h, w2_h,
    gath_h, act_h, slope_h, resid_out, next_own,
    gath, part, out_po, out_pd, out_y, in_po, in_pd, in_y, ex_sem,
    middle, w1, w2, act, slope, load_sem, save_sem,
):
    ex = Exchange(x_own, gath, part, (out_po, out_pd, out_y, in_po, in_pd, in_y), ex_sem)
    hidden = w1.shape[1]
    loads = Moves(load_sem)
    for n, pair in enumerate(((w1_h, w1), (w2_h, w2), (middle_h, middle))):
        loads.load(n, *pair).start()
    ex.begin()
    loads.load(0, w1_h, w1).wait()
    loads.load(1, w2_h, w2).wait()
    pairs = ((gath, gath_h), (act, act_h), (slope, slope_h))

    def saves(slot):
        return [
            pltpu.make_async_copy(a.at[slot], b.at[slot], save_sem.at[n, slot])
            for n, (a, b) in enumerate(pairs)
        ]

    def step(i, _):
        ex.before(i)
        slot = ex.slot(i)
        x = gath[slot]
        for block in range(hidden // 256):
            at = slice(block * 256, block * 256 + 256)
            pre = dot(x, w1[:, at]) + bias[:, at]
            cdf, pdf = erf_parts(pre)
            act[slot, :, at] = (pre * cdf).astype(BF16)
            slope[slot, :, at] = (cdf + pre * pdf).astype(BF16)
        part[i] = dot(act[slot], w2[...])
        for copy in saves(slot):
            copy.start()
        ex.after(i)
        return 0

    lax.fori_loop(0, 8, step, 0)
    loads.load(2, middle_h, middle).wait()
    for g in range(GROUPS):
        res = middle[g] + ex.total(g) + shift_a[...]
        resid_out[g] = res
        unit, _ = norm_parts(res)
        next_own[g] = keep_pad(x_own[g], unit * gain_n[...] + shift_n[...]).astype(BF16)
    ex.end()

    def drain(slot, _):
        for copy in saves(slot):
            copy.wait()
        return 0

    lax.fori_loop(0, 8, drain, 0)


VM = pl.BlockSpec(memory_space=pltpu.VMEM)
HB = pl.BlockSpec(memory_space=pl.ANY)


def sds(shape, dtype):
    return jax.ShapeDtypeStruct(shape, dtype)


def params(n):
    return pltpu.CompilerParams(
        collective_id=n, has_side_effects=True, vmem_limit_bytes=60 * 1024 * 1024
    )


def attend_half(x_own, gain, shift_a, shift_n, bias, resid, wqkv, wout):
    width = wout.shape[0]
    heads = width // HEAD
    return pl.pallas_call(
        attend_kernel,
        out_shape=(
            sds((8, ROWS, D), BF16),
            sds((8, ROWS, 3 * width), BF16),
            sds((8, heads * ROWS, ROWS), BF16),
            sds((8, ROWS, width), BF16),
            sds((GROUPS, ROWS, D), F32),
            sds((GROUPS, ROWS, D), BF16),
        ),
        in_specs=[VM] * 5 + [HB] * 3,
        out_specs=(HB, HB, HB, HB, VM, VM),
        scratch_shapes=exchange_scratch()
        + [
            pltpu.VMEM((GROUPS, ROWS, D), F32),
            pltpu.VMEM((D, 3 * width), BF16),
            pltpu.VMEM((width, D), BF16),
            pltpu.VMEM((8, ROWS, 3 * width), BF16),
            pltpu.VMEM((8, heads * ROWS, ROWS), BF16),
            pltpu.VMEM((8, ROWS, width), BF16),
            pltpu.SemaphoreType.DMA((3,)),
            pltpu.SemaphoreType.DMA((4, 8)),
        ],
        compiler_params=params(1),
    )(x_own, gain, shift_a, shift_n, bias, resid, wqkv, wout)


def mlp_half(x_own, gain, shift_a, shift_n, bias, middle, w1, w2):
    hidden = w1.shape[1]
    return pl.pallas_call(
        mlp_kernel,
        out_shape=(
            sds((8, ROWS, D), BF16),
            sds((8, ROWS, hidden), BF16),
            sds((8, ROWS, hidden), BF16),
            sds((GROUPS, ROWS, D), F32),
            sds((GROUPS, ROWS, D), BF16),
        ),
        in_specs=[VM] * 5 + [HB] * 3,
        out_specs=(HB, HB, HB, VM, VM),
        scratch_shapes=exchange_scratch()
        + [
            pltpu.VMEM((GROUPS, ROWS, D), F32),
            pltpu.VMEM((D, hidden), BF16),
            pltpu.VMEM((hidden, D), BF16),
            pltpu.VMEM((8, ROWS, hidden), BF16),
            pltpu.VMEM((8, ROWS, hidden), BF16),
            pltpu.SemaphoreType.DMA((3,)),
            pltpu.SemaphoreType.DMA((3, 8)),
        ],
        compiler_params=params(2),
    )(x_own, gain, shift_a, shift_n, bias, middle, w1, w2)


def column_sums(values):
    return jnp.sum(values, axis=0, keepdims=True)


def back_through_norm(ex, g, gradient, source, gain, grad_out, next_own, sums):
    moved = ex.total(g)
    unit, scale = norm_parts(source[g])
    scaled = moved * gain[...]
    lean = jnp.mean(scaled, axis=-1, keepdims=True)
    tilt = jnp.mean(scaled * unit, axis=-1, keepdims=True)
    grad = gradient[g] + scale * (scaled - lean - unit * tilt)
    rounded = grad.astype(BF16)
    grad_out[g] = grad
    next_own[g] = rounded
    rows = (column_sums(moved * unit), column_sums(moved), column_sums(rounded.astype(F32)))
    for n, row in enumerate(rows):
        sums[n : n + 1] = row if g == 0 else sums[n : n + 1] + row


def weight_blocks(left, right, rows_out, cols_left, cols_right, cols_out, copies):
    flat = 8 * ROWS

    def block(n, _):
        at = pl.ds(pl.multiple_of(n * 256, 256), 256)
        some = left[:, :, at].reshape(flat, 256)
        rows_out[at, :] = dot(some, right[...].reshape(flat, right.shape[-1]), 0, 0).astype(BF16)
        some = cols_right[:, :, at].reshape(flat, 256)
        wide = dot(cols_left[...].reshape(flat, cols_left.shape[-1]), some, 0, 0).astype(BF16)
        cols_out[2 * n] = wide[:, :COLS]
        cols_out[2 * n + 1] = wide[:, COLS:]
        for copy in copies(n):
            copy.start()
        return 0

    lax.fori_loop(0, D // 256, block, 0)


def weight_copies(rows_out, rows_h, cols_out, cols_h, sems):
    def copies(n):
        at = pl.ds(pl.multiple_of(n * 256, 256), 256)
        two = pl.ds(2 * n, 2)
        return (
            pltpu.make_async_copy(rows_out.at[at], rows_h.at[at], sems.at[0, n]),
            pltpu.make_async_copy(cols_out.at[two], cols_h.at[two], sems.at[1, n]),
        )

    return copies


def drain_weights(copies):
    def drain(n, _):
        for copy in copies(n):
            copy.wait()
        return 0

    lax.fori_loop(0, D // 256, drain, 0)


def mlp_back_kernel(
    x_own, gain, gradient_h, middle_h, w1_h, w2_h, act_h, slope_h, norm_h,
    grad_out, next_own, sums, bias_sum, rows_h, cols_h,
    gath, part, out_po, out_pd, out_y, in_po, in_pd, in_y, ex_sem,
    gradient, middle, w1, w2, act, slope, norm, pre, rows_out, cols_out, load_sem, save_sem,
):
    ex = Exchange(x_own, gath, part, (out_po, out_pd, out_y, in_po, in_pd, in_y), ex_sem)
    hidden = w1.shape[1]
    loads = [
        pltpu.make_async_copy(a, b, load_sem.at[n])
        for n, (a, b) in enumerate(
            (
                (w2_h, w2),
                (slope_h, slope),
                (w1_h, w1),
                (act_h, act),
                (norm_h, norm),
                (gradient_h, gradient),
                (middle_h, middle),
            )
        )
    ]
    for copy in loads:
        copy.start()
    ex.begin()
    for copy in loads[:3]:
        copy.wait()

    def step(i, _):
        ex.before(i)
        slot = ex.slot(i)
        grad = gath[slot]
        for block in range(hidden // 256):
            at = slice(block * 256, block * 256 + 256)
            d_act = dot(grad, w2[at, :], 1, 1)
            pre[slot, :, at] = (d_act * slope[slot, :, at].astype(F32)).astype(BF16)
        part[i] = dot(pre[slot], w1[...], 1, 1)
        ex.after(i)
        return 0

    lax.fori_loop(0, 8, step, 0)
    for copy in loads[3:]:
        copy.wait()
    copies = weight_copies(rows_out, rows_h, cols_out, cols_h, save_sem)
    weight_blocks(norm, pre, rows_out, act, gath, cols_out, copies)
    ones = jnp.ones((8, 8 * ROWS), BF16)
    bias_sum[...] = dot(ones, pre[...].reshape(8 * ROWS, hidden))
    for g in range(GROUPS):
        back_through_norm(ex, g, gradient, middle, gain, grad_out, next_own, sums)
    ex.end()
    drain_weights(copies)


def attend_back_kernel(
    x_own, gain, gradient_h, resid_h, wqkv_h, wout_h, qkv_h, prob_h, att_h, norm_h,
    grad_out, next_own, sums, bias_sum, rows_h, cols_h,
    gath, part, out_po, out_pd, out_y, in_po, in_pd, in_y, ex_sem,
    gradient, resid, wqkv, wout, qkv, prob, att, norm, triple, rows_out, cols_out,
    load_sem, save_sem,
):
    ex = Exchange(x_own, gath, part, (out_po, out_pd, out_y, in_po, in_pd, in_y), ex_sem)
    width = wout.shape[0]
    loads = [
        pltpu.make_async_copy(a, b, load_sem.at[n])
        for n, (a, b) in enumerate(
            (
                (wout_h, wout),
                (qkv_h, qkv),
                (prob_h, prob),
                (wqkv_h, wqkv),
                (att_h, att),
                (norm_h, norm),
                (gradient_h, gradient),
                (resid_h, resid),
            )
        )
    ]
    for copy in loads:
        copy.start()
    ex.begin()
    for copy in loads[:4]:
        copy.wait()

    def step(i, _):
        ex.before(i)
        slot = ex.slot(i)
        grad = gath[slot]
        d_att = dot(grad, wout[...], 1, 1).astype(BF16)
        q = qkv[slot, :, 0:width]
        k = qkv[slot, :, width : 2 * width]
        v = qkv[slot, :, 2 * width :]
        d_q = jnp.zeros((ROWS, width), F32)
        d_k = jnp.zeros((ROWS, width), F32)
        d_v = jnp.zeros((ROWS, width), F32)
        for h in range(width // HEAD):
            mask = head_mask(h, width)
            d_one = d_att * mask
            rounded = prob[slot, h * ROWS : (h + 1) * ROWS]
            weight = rounded.astype(F32)
            d_prob = dot(d_one, v, 1, 1)
            centre = jnp.sum(weight * d_prob, axis=-1, keepdims=True)
            d_scores = (weight * (d_prob - centre)).astype(BF16)
            d_q = d_q + dot(d_scores, k * mask)
            d_k = d_k + dot(d_scores, q * mask, 0, 0)
            d_v = d_v + dot(rounded, d_one, 0, 0)
        triple[slot, :, 0:width] = (d_q * SCALE).astype(BF16)
        triple[slot, :, width : 2 * width] = (d_k * SCALE).astype(BF16)
        triple[slot, :, 2 * width :] = d_v.astype(BF16)
        part[i] = dot(triple[slot], wqkv[...], 1, 1)
        ex.after(i)
        return 0

    lax.fori_loop(0, 8, step, 0)
    for copy in loads[4:]:
        copy.wait()
    copies = weight_copies(rows_out, rows_h, cols_out, cols_h, save_sem)
    weight_blocks(norm, triple, rows_out, att, gath, cols_out, copies)
    ones = jnp.ones((8, 8 * ROWS), BF16)
    bias_sum[...] = dot(ones, triple[...].reshape(8 * ROWS, 3 * width))
    for g in range(GROUPS):
        back_through_norm(ex, g, gradient, resid, gain, grad_out, next_own, sums)
    ex.end()
    drain_weights(copies)


def back_outs(rows, cols):
    return (
        sds((GROUPS, ROWS, D), F32),
        sds((GROUPS, ROWS, D), BF16),
        sds((8, D), F32),
        sds((8, rows), F32),
        sds((D, rows), BF16),
        sds((D // COLS, cols, COLS), BF16),
    )


def back_scratch(rows, cols, loads):
    return [
        pltpu.VMEM((D, rows), BF16),
        pltpu.VMEM((D // COLS, cols, COLS), BF16),
        pltpu.SemaphoreType.DMA((loads,)),
        pltpu.SemaphoreType.DMA((2, D // 256)),
    ]


def mlp_back(x_own, gain, gradient, middle, w1, w2, act, slope, norm):
    hidden = w1.shape[1]
    wide = pltpu.VMEM((8, ROWS, hidden), BF16)
    return pl.pallas_call(
        mlp_back_kernel,
        out_shape=back_outs(hidden, hidden),
        in_specs=[VM] * 2 + [HB] * 7,
        out_specs=(VM, VM, VM, VM, HB, HB),
        scratch_shapes=exchange_scratch()
        + [
            pltpu.VMEM((GROUPS, ROWS, D), F32),
            pltpu.VMEM((GROUPS, ROWS, D), F32),
            pltpu.VMEM((D, hidden), BF16),
            pltpu.VMEM((hidden, D), BF16),
            wide,
            wide,
            pltpu.VMEM((8, ROWS, D), BF16),
            wide,
        ]
        + back_scratch(hidden, hidden, 7),
        compiler_params=params(3),
    )(x_own, gain, gradient, middle, w1, w2, act, slope, norm)


def attend_back(x_own, gain, gradient, resid, wqkv, wout, qkv, prob, att, norm):
    width = wout.shape[0]
    heads = width // HEAD
    return pl.pallas_call(
        attend_back_kernel,
        out_shape=back_outs(3 * width, width),
        in_specs=[VM] * 2 + [HB] * 8,
        out_specs=(VM, VM, VM, VM, HB, HB),
        scratch_shapes=exchange_scratch()
        + [
            pltpu.VMEM((GROUPS, ROWS, D), F32),
            pltpu.VMEM((GROUPS, ROWS, D), F32),
            pltpu.VMEM((D, 3 * width), BF16),
            pltpu.VMEM((width, D), BF16),
            pltpu.VMEM((8, ROWS, 3 * width), BF16),
            pltpu.VMEM((8, heads * ROWS, ROWS), BF16),
            pltpu.VMEM((8, ROWS, width), BF16),
            pltpu.VMEM((8, ROWS, D), BF16),
            pltpu.VMEM((8, ROWS, 3 * width), BF16),
        ]
        + back_scratch(3 * width, width, 8),
        compiler_params=params(4),
    )(x_own, gain, gradient, resid, wqkv, wout, qkv, prob, att, norm)


def to_groups(array, dtype):
    images = array.shape[0] // GROUPS
    rows = array.reshape(GROUPS, images * PATCHES, D)
    return jnp.pad(rows, ((0, 0), (0, ROWS - images * PATCHES), (0, 0))).astype(dtype)


def from_groups(array):
    return array[:, :LIVE].reshape(GROUPS * (LIVE // PATCHES), PATCHES, D)


def collect_weight(partial_grad, split_dim):
    return lax.psum_scatter(
        partial_grad, "dp", scatter_dimension=split_dim, tiled=True
    ).astype(F32)


def join_columns(blocks):
    return jnp.transpose(blocks, (1, 0, 2)).reshape(blocks.shape[1], -1)


def local(
    patches,
    keep_index,
    kept_count,
    norm_gain,
    shifts,
    w_qkv,
    bias_qv,
    w_out,
    w_fc1,
    bias_fc1,
    w_fc2,
    cotangent,
):
    width = w_qkv.shape[-1]
    hidden = w_fc1.shape[-1]
    slot_ids = jnp.arange(PATCHES, dtype=jnp.int32)
    selector = (keep_index[:, :, None] == slot_ids[None, None, :]).astype(BF16)
    tokens = jnp.einsum("bsp,bpd->bsd", selector, patches, preferred_element_type=F32)
    resid = to_groups(tokens, F32)
    unit, _ = norm_parts(resid)
    own = unit * norm_gain[0, 0] + shifts[0, 0]
    per = kept_count.shape[0] // GROUPS
    pad_row = jnp.arange(ROWS) - LIVE
    counts = kept_count.reshape(GROUPS, per).astype(F32)
    counts = jnp.pad(counts, ((0, 0), (LIVE, ROWS - LIVE - per)))
    own = jnp.where(pad_row[None, :, None] >= 0, counts[:, :, None], own).astype(BF16)

    def row(array):
        return array.reshape(1, -1)

    stored = []
    for n in range(LAYERS):
        wqkv = w_qkv[n].reshape(D, 3 * width)
        gath, qkv, prob, att, middle, own = attend_half(
            own, row(norm_gain[n, 1]), row(shifts[n, 2]), row(shifts[n, 1]),
            bias_qv[n], resid, wqkv, w_out[n],
        )
        after = min(n + 1, LAYERS - 1)
        gath_mlp, act, slope, resid_out, own = mlp_half(
            own, row(norm_gain[after, 0]), row(shifts[n, 3]), row(shifts[after, 0]),
            row(bias_fc1[n]), middle, w_fc1[n], w_fc2[n],
        )
        stored.append((resid, wqkv, gath, qkv, prob, att, middle, gath_mlp, act, slope))
        resid = resid_out
    own_mask = (slot_ids[None, :] < kept_count[:, None]).astype(F32)[:, :, None]
    layer_out = from_groups(resid) * own_mask
    start = cotangent.astype(F32) * own_mask
    gradient = to_groups(start, F32)
    own = gradient.astype(BF16)
    shift_last = jnp.sum(start, axis=(0, 1))
    gain_terms, shift_terms, bias_qv_terms, bias_fc1_terms, weight_terms = [], [], [], [], []
    for n in reversed(range(LAYERS)):
        resid, wqkv, gath, qkv, prob, att, middle, gath_mlp, act, slope = stored[n]
        gradient, own, sums, fc1_sum, d_fc1, d_fc2 = mlp_back(
            own, row(norm_gain[n, 1]), gradient, middle, w_fc1[n], w_fc2[n], act, slope, gath_mlp
        )
        gradient, own, sums_a, qkv_sum, d_qkv, d_out = attend_back(
            own, row(norm_gain[n, 0]), gradient, resid, wqkv, w_out[n], qkv, prob, att, gath
        )
        gain_terms.insert(0, jnp.stack([sums_a[0], sums[0]]))
        shift_terms.insert(0, jnp.stack([sums_a[1], sums[1], sums[2], shift_last]))
        shift_last = sums_a[2]
        bias_fc1_terms.insert(0, fc1_sum[0])
        bias_qv_terms.insert(0, jnp.stack([qkv_sum[0, :width], qkv_sum[0, 2 * width :]]))
        weight_terms.insert(
            0,
            (
                collect_weight(d_qkv.reshape(D, 3, width), 0),
                collect_weight(join_columns(d_out), 1),
                collect_weight(d_fc1, 0),
                collect_weight(join_columns(d_fc2), 1),
            ),
        )
    grad_qkv, grad_out, grad_fc1, grad_fc2 = (
        jnp.stack([entry[k] for entry in weight_terms]) for k in range(4)
    )
    offset_at = lax.axis_index("tensor") * width
    hidden_at = lax.axis_index("tensor") * hidden
    zero_at = offset_at * 0
    qv_full = lax.dynamic_update_slice(
        jnp.zeros((LAYERS, 2, D), F32), jnp.stack(bias_qv_terms), (zero_at, zero_at, offset_at)
    )
    fc1_full = lax.dynamic_update_slice(
        jnp.zeros((LAYERS, FF), F32), jnp.stack(bias_fc1_terms), (zero_at, hidden_at)
    )
    grad_gain, grad_shifts, grad_bias_qv, grad_bias_fc1 = lax.psum(
        (jnp.stack(gain_terms), jnp.stack(shift_terms), qv_full, fc1_full), ("dp", "tensor")
    )
    grad_patches = jnp.einsum(
        "bsp,bsd->bpd", selector.astype(F32), from_groups(gradient), precision=HIGHEST
    )
    return (
        layer_out,
        grad_patches,
        grad_gain,
        grad_shifts,
        grad_qkv,
        grad_bias_qv,
        grad_out,
        grad_fc1,
        grad_bias_fc1,
        grad_fc2,
    )


def solution(mesh):
    in_specs = (
        P(("dp", "tensor"), None, None),
        P(("dp", "tensor"), None),
        P(("dp", "tensor")),
        P(),
        P(),
        P(None, None, None, "tensor"),
        P(None, None, "tensor"),
        P(None, "tensor", None),
        P(None, None, "tensor"),
        P(None, "tensor"),
        P(None, "tensor", None),
        P(("dp", "tensor"), None, None),
    )
    out_specs = (
        P(("dp", "tensor"), None, None),
        P(("dp", "tensor"), None, None),
        P(),
        P(),
        P(None, "dp", None, "tensor"),
        P(),
        P(None, "tensor", "dp"),
        P(None, "dp", "tensor"),
        P(),
        P(None, "tensor", "dp"),
    )
    return jax.shard_map(local, mesh=mesh, in_specs=in_specs, out_specs=out_specs, check_vma=False)
```

time: 1420 us -> 883 us (0.62); the launches traced: 1400 us -> 881 us
  waiting for transfers between devices: 1030 us -> 517 us
  Pallas kernels: 0 us -> 279 us
  matrix products: 164 us -> 2.98 us
  other arithmetic: 89.3 us -> 10.9 us
  local copies, waits for them, and re-layouts: 99.4 us -> 55 us
    pallas_call x0 -> x8, Pallas kernels: none -> 279 us  [the longest x2 71 us: attend_back(): pl.pallas_call(attend_back_kernel, out_shape=back_outs(3 * width, width),...]
    reduce_scatter x12 -> x6, waiting for transfers between devices: 547 us -> 382 us  [collect_weight(): lax.psum_scatter(partial_grad, 'dp', scatter_dimension=split_dim, tiled=T...]
    dot_general x38 -> x2, matrix products: 164 us -> 2.98 us  [the longest x1 1.89 us: local(): jnp.einsum('bsp,bsd->bpd', selector.astype(F32), from_groups(gradient), p...]
    all_gather x8 -> x0, waiting for transfers between devices: 155 us -> none  [the longest x4 96.1 us: spread(): lax.all_gather(rows, 'tensor', axis=0, tiled=True)]
    psum x1, waiting for transfers between devices: 120 us -> 0.01 us  [local(): lax.psum((jnp.stack(gain_terms), jnp.stack(shift_terms), qv_full, fc1_ful...]
    unnamed x29 -> x11, waiting for transfers between devices: 203 us -> 135 us
    convert_element_type x13 -> x3, other arithmetic: 43.7 us -> 2.59 us  [the longest x1 1.15 us: local(): jnp.where(pad_row[None, :, None] >= 0, counts[:, :, None], own).astype(BF16)]
    reduce_sum x23 -> x2, other arithmetic: 38.1 us -> 1.61 us  [the longest x1 1.34 us: local(): shift_last = jnp.sum(start, axis=(0, 1))]
  transfers between devices with their start and end apart: 25 -> 9, of which waited for: 24 -> 8; matrix products, arithmetic and copies ran while one was open for 10% -> 3% of each run, Pallas kernels for 0% -> 0%
where the time goes in v2:
time: 883 us; the launch traced here: 881 us
  waiting for transfers between devices  517 us (59%)
  Pallas kernels  279 us (32%)
  local copies, waits for them, and re-layouts  55 us (6%)
  between operations  15.9 us (2%)
  other arithmetic  10.9 us (1%)
    reduce_scatter x6, waiting for transfers between devices, collect_weight(): lax.psum_scatter(partial_grad, 'dp', scatter_dimension=split_dim, tiled=T...  382 us
    unnamed x11, waiting for transfers between devices  135 us
    pallas_call x2, Pallas kernels, attend_back(): pl.pallas_call(attend_back_kernel, out_shape=back_outs(3 * width, width),...  71 us
    pallas_call x2, Pallas kernels, attend_half(): pl.pallas_call(attend_kernel, out_shape=(sds((8, ROWS, D), BF16), sds((8,...  70.3 us
    pallas_call x2, Pallas kernels, mlp_back(): pl.pallas_call(mlp_back_kernel, out_shape=back_outs(hidden, hidden), in_s...  69.8 us
    pallas_call x2, Pallas kernels, mlp_half(): pl.pallas_call(mlp_kernel, out_shape=(sds((8, ROWS, D), BF16), sds((8, RO...  67.8 us
  transfers between devices with their start and end apart: 9, of which 8 were waited for; matrix products, arithmetic and copies ran while one was open for 3% of the time, Pallas kernels for 0%

profile of v2, /device:TPU:0, one launch (start us, length us, event | category | flops | bytes accessed | tf_op | source)
XLA Modules:
  0.0 881.2 jit_solution(13216200456972223405)
XLA Ops:
  8.1 0.7 convert_element_type.37
  8.8 0.7 fusion.5
  9.5 1.1 fusion.2
  10.8 1.1 fusion.7
  12.3 3.7 fusion.6
  16.0 1.7 copy.68
  17.7 1.6 copy.45.wqkv_h
  19.3 2.3 slice_bitcast_fusion.4
  22.8 1.7 copy.69
  24.6 1.6 copy.47.wqkv_h
  26.9 6.0 slice_bitcast_fusion
  32.9 1.2 select_convert_fusion.x_own
  34.0 36.1 %shard_map.195 = (bf16[8,160,1024]{2,1,0:T(8,128)(2,1)}, bf16[8,160,768]{2,1,0:T(8,128)(2,1)}, bf16[8,640,160]{2,1,0:T(8,128)(2,1)}, bf16[8,160,256]{2,1,0:T(8,1...) custom-call(bf16[2,160,1024]{2,1,0:T(8,128)(2,1)} %select_convert_fusion.x_own, ...), custom_call_target="tpu_custom_call" | custom-call | tf_op jit(solution)/shard_map/pallas_call | solution.py:335
  70.1 33.8 %shard_map.196 = (bf16[8,160,1024]{2,1,0:T(8,128)(2,1)}, bf16[8,160,1024]{2,1,0:T(8,128)(2,1)}, bf16[8,160,1024]{2,1,0:T(8,128)(2,1)}, f32[2,160,1024]{2,1,0:T(8,128)}, bf16[2,160,1024]{2,1,0:T(8,128)(2,1)}) custom-call(bf16[2,160,1024]{2,1,0:T(8,128)(2,1)} %get-tuple-element.54.x_own, f32[1,1024]{1,0:T(1,128)} %get-tuple-element.161.gain_n.gain, ...), custom_call_target="tpu_custom_call" | custom-call | tf_op jit(solution)/shard_map/pallas_call | solution.py:364
  104.0 34.2 %shard_map.197 = (bf16[8,160,1024]{2,1,0:T(8,128)(2,1)}, bf16[8,160,768]{2,1,0:T(8,128)(2,1)}, bf16[8,640,160]{2,1,0:T(8,128)(2,1)}, bf16[8,160,256]{2,1,0:T(8,1...) custom-call(bf16[2,160,1024]{2,1,0:T(8,128)(2,1)} %get-tuple-element.56.x_own, ...), custom_call_target="tpu_custom_call" | custom-call | tf_op jit(solution)/shard_map/pallas_call | solution.py:335
  138.2 34.0 %shard_map.198 = (bf16[8,160,1024]{2,1,0:T(8,128)(2,1)}, bf16[8,160,1024]{2,1,0:T(8,128)(2,1)}, bf16[8,160,1024]{2,1,0:T(8,128)(2,1)}, f32[2,160,1024]{2,1,0:T(8,128)}, bf16[2,160,1024]{2,1,0:T(8,128)(2,1)}) custom-call(bf16[2,160,1024]{2,1,0:T(8,128)(2,1)} %get-tuple-element.58.x_own, f32[1,1024]{1,0:T(1,128)} %get-tuple-element.161.gain_n.gain, ...), custom_call_target="tpu_custom_call" | custom-call | tf_op jit(solution)/shard_map/pallas_call | solution.py:364
  172.1 1.4 slice.163
  173.7 0.9 copy-done.5
  174.6 1.3 fusion
  176.1 1.2 pad.13.gradient_h
  177.3 0.9 pad.78.x_own
  178.2 34.9 %shard_map.199 = (f32[2,160,1024]{2,1,0:T(8,128)}, bf16[2,160,1024]{2,1,0:T(8,128)(2,1)}, f32[8,1024]{1,0:T(8,128)}, f32[8,1024]{1,0:T(8,128)}, bf16[1024,1024]{...) custom-call(bf16[2,160,1024]{2,1,0:T(8,128)(2,1)} %pad.78.x_own, f32[1,1024]{1,0:T(1,128)} %get-tuple-element.162.norm2.gain, ...), custom_call_target="tpu_custom_call" | custom-call | tf_op jit(solution)/shard_map/pallas_call | solution.py:595
  213.1 35.5 %shard_map.200 = (f32[2,160,1024]{2,1,0:T(8,128)}, bf16[2,160,1024]{2,1,0:T(8,128)(2,1)}, f32[8,1024]{1,0:T(8,128)}, f32[8,768]{1,0:T(8,128)}, bf16[1024,768]{1,0:T(8,128)(2,1)}, /*index=5*/bf16[8,256,128]{2,1,0:T(8,128)(2,1)}) custom-call(bf16[2,160,1024]{2,1,0:T(8,128)(2,1)} %get-tuple-element.64.x_own, f32[1,1024]{1,0:T(1,128)} %get-tuple-element.161.gain_n.gain, ...), custom_call_target="tpu_custom_call" | custom-call | tf_op jit(solution)/shard_map/pallas_call | solution.py:619
  248.6 34.9 %shard_map.201 = (f32[2,160,1024]{2,1,0:T(8,128)}, bf16[2,160,1024]{2,1,0:T(8,128)(2,1)}, f32[8,1024]{1,0:T(8,128)}, f32[8,1024]{1,0:T(8,128)}, bf16[1024,1024]{...) custom-call(bf16[2,160,1024]{2,1,0:T(8,128)(2,1)} %get-tuple-element.70.x_own, f32[1,1024]{1,0:T(1,128)} %get-tuple-element.164.norm2.gain, ...), custom_call_target="tpu_custom_call" | custom-call | tf_op jit(solution)/shard_map/pallas_call | solution.py:595
  283.5 35.5 %shard_map.202 = (f32[2,160,1024]{2,1,0:T(8,128)}, bf16[2,160,1024]{2,1,0:T(8,128)(2,1)}, f32[8,1024]{1,0:T(8,128)}, f32[8,768]{1,0:T(8,128)}, bf16[1024,768]{1,0:T(8,128)(2,1)}, /*index=5*/bf16[8,256,128]{2,1,0:T(8,128)(2,1)}) custom-call(bf16[2,160,1024]{2,1,0:T(8,128)(2,1)} %get-tuple-element.75.x_own, f32[1,1024]{1,0:T(1,128)} %get-tuple-element.165.gain, ...), custom_call_target="tpu_custom_call" | custom-call | tf_op jit(solution)/shard_map/pallas_call | solution.py:619
  319.1 2.1 copy.52
  321.2 1.0 copy.53
  322.3 0.7 reduce-scatter.25.cloned.1.call-update
  323.9 2.6 copy.54
  326.6 1.5 copy-done.2
  328.1 2.6 copy.55
  330.8 0.7 reduce-scatter.17.cloned.1.call-update
  331.6 0.7 reduce-scatter.19.cloned.1.call-update
  332.3 0.8 slice.170
  333.1 0.8 slice.166
  333.9 0.8 slice.173
  334.6 0.8 slice.168
  335.4 0.8 slice.178
  336.1 0.8 slice.179
  336.9 0.7 fusion.10
  337.6 0.7 fusion.11
  338.4 0.8 fusion.8
  339.3 0.9 fusion.9
  342.4 1.9 fusion.1
  344.3 40.0 %reduce-scatter.13.cloned.1.call-done = bf16[256,128]{0,1:T(8,128)(2,1)} async-done(((bf16[256,1024]{0,1:T(8,128)(2,1)}), bf16[256,128]{0,1:T(8,128)(2,1)}) %reduce-scatter.13.cloned.1.call-update) | async-done | bytes 65552 | tf_op jit(solution)/shard_map/reduce_scatter | solution.py:652
  384.3 65.3 %reduce-scatter.15.cloned.1.call-done = bf16[256,128]{0,1:T(8,128)(2,1)} async-done(((bf16[256,1024]{0,1:T(8,128)(2,1)}), bf16[256,128]{0,1:T(8,128)(2,1)}) %reduce-scatter.15.cloned.1.call-update) | async-done | bytes 65552 | tf_op jit(solution)/shard_map/reduce_scatter | solution.py:652
  449.6 0.9 maximum_convert_fusion.3
  450.5 0.8 copy.57
  451.3 65.6 %reduce-scatter.25.cloned.1.call-done = bf16[128,768]{1,0:T(8,128)(2,1)} async-done(((bf16[1024,768]{1,0:T(8,128)(2,1)}), bf16[128,768]{1,0:T(8,128)(2,1)}) %reduce-scatter.25.cloned.1.call-update) | async-done | bytes 196624
  516.9 1.1 copy.65
  518.0 66.4 %reduce-scatter.27.cloned.1.call-done = bf16[128,768]{1,0:T(8,128)(2,1)} async-done(((bf16[1024,768]{1,0:T(8,128)(2,1)}), bf16[128,768]{1,0:T(8,128)(2,1)}) %reduce-scatter.27.cloned.1.call-update) | async-done | bytes 196624
  584.4 1.1 copy.67
  585.6 1.1 copy.56
  586.7 67.7 %reduce-scatter.21.cloned.1.call-done = bf16[1024,128]{0,1:T(8,128)(2,1)} async-done(((bf16[1024,1024]{0,1:T(8,128)(2,1)}), bf16[1024,128]{0,1:T(8,128)(2,1)}) %reduce-scatter.21.cloned.1.call-update) | async-done | bytes 262160 | tf_op jit(solution)/shard_map/reduce_scatter | solution.py:652
  654.4 70.1 %reduce-scatter.23.cloned.1.call-done = bf16[1024,128]{0,1:T(8,128)(2,1)} async-done(((bf16[1024,1024]{0,1:T(8,128)(2,1)}), bf16[1024,128]{0,1:T(8,128)(2,1)}) %reduce-scatter.23.cloned.1.call-update) | async-done | bytes 262160 | tf_op jit(solution)/shard_map/reduce_scatter | solution.py:652
  724.5 1.1 maximum_convert_fusion.1
  725.6 69.1 %reduce-scatter.17.cloned.1.call-done = bf16[128,1024]{1,0:T(8,128)(2,1)} async-done(((bf16[1024,1024]{1,0:T(8,128)(2,1)}), bf16[128,1024]{1,0:T(8,128)(2,1)}) %reduce-scatter.17.cloned.1.call-update) | async-done | bytes 262160 | tf_op jit(solution)/shard_map/reduce_scatter | solution.py:652
  794.7 70.2 %reduce-scatter.19.cloned.1.call-done = bf16[128,1024]{1,0:T(8,128)(2,1)} async-done(((bf16[1024,1024]{1,0:T(8,128)(2,1)}), bf16[128,1024]{1,0:T(8,128)(2,1)}) %reduce-scatter.19.cloned.1.call-update) | async-done | bytes 262160 | tf_op jit(solution)/shard_map/reduce_scatter | solution.py:652
  864.9 2.1 maximum_convert_fusion
  867.1 1.3 copy.58
  868.4 1.3 copy.76
  869.7 1.4 copy.77
  871.1 1.3 copy.78
  872.4 1.4 copy.79
  (69 shorter events, 6.3 us)
Async XLA Ops:
  8.0 1.5 copy-start
  8.0 376.2 %reduce-scatter.13.cloned.1.call-start = ((), (), s32[]{:S(2)}) async-start(), calls=%async_computation.8 | async-start | bytes 589824 | tf_op jit(solution)/shard_map/reduce_scatter | solution.py:652
  19.3 2.3 copy-start.13
  19.3 2.9 copy-start.12
  24.5 1.6 copy-start.9
  24.5 1.6 copy-start.11
  173.5 1.1 copy-start.5
  319.0 2.2 copy-start.6
  321.2 128.4 %reduce-scatter.15.cloned.1.call-start = ((), (), s32[]{:S(2)}) async-start(), calls=%async_computation.9 | async-start | bytes 589824 | tf_op jit(solution)/shard_map/reduce_scatter | solution.py:652
  322.3 194.6 %reduce-scatter.25.cloned.1.call-start = ((), (), s32[]{:S(2)}) async-start(), calls=%async_computation.14 | async-start | bytes 1769472
  322.3 1.6 copy-start.3
  323.0 261.4 %reduce-scatter.27.cloned.1.call-start = ((), (), s32[]{:S(2)}) async-start(), calls=%async_computation.15 | async-start | bytes 1769472
  323.6 330.8 %reduce-scatter.21.cloned.1.call-start = ((), (), s32[]{:S(2)}) async-start(), calls=%async_computation.12 | async-start | bytes 2359296 | tf_op jit(solution)/shard_map/reduce_scatter | solution.py:652
  326.5 1.6 copy-start.2
  326.5 398.0 %reduce-scatter.23.cloned.1.call-start = ((), (), s32[]{:S(2)}) async-start(), calls=%async_computation.13 | async-start | bytes 2359296 | tf_op jit(solution)/shard_map/reduce_scatter | solution.py:652
  330.8 464.0 %reduce-scatter.17.cloned.1.call-start = ((), (), s32[]{:S(2)}) async-start(), calls=%async_computation.10 | async-start | bytes 2359296 | tf_op jit(solution)/shard_map/reduce_scatter | solution.py:652
  331.5 10.0 %copy-start.4 = (f32[2,160,1024]{2,1,0:T(8,128)S(1)}, f32[2,160,1024]{2,1,0:T(8,128)}, u32[]{:S(2)}) copy-start(f32[2,160,1024]{2,1,0:T(8,128)} %get-tuple-element.81) | copy-start | bytes 3932164
  331.5 533.4 %reduce-scatter.19.cloned.1.call-start = ((), (), s32[]{:S(2)}) async-start(), calls=%async_computation.11 | async-start | bytes 2359296 | tf_op jit(solution)/shard_map/reduce_scatter | solution.py:652
  332.3 536.1 %all-reduce.6.cloned.1.call-start = ((), (), s32[]{:S(2)}) async-start(), calls=%async_computation.16 | async-start | bytes 196608 | tf_op jit(solution)/shard_map/psum | solution.py:747
  338.4 3.1 copy-start.8
  340.2 1.3 copy-start.7
  341.7 0.7 copy-start.10
  864.9 8.8 %copy-start.1 = (bf16[6,50,1024]{2,1,0:T(8,128)(2,1)S(1)}, bf16[6,50,1024]{2,1,0:T(8,128)(2,1)}, u32[]{:S(2)}) copy-start(bf16[6,50,1024]{2,1,0:T(8,128)(2,1)} %param.12) | copy-start | bytes 1843204
Sparse Core Ops, SparseCore 0:
  321.3 62.9 reduce-scatter.12
  388.6 60.9 reduce-scatter.14
  453.0 63.8 reduce-scatter.24
  520.6 63.7 reduce-scatter.26
  587.8 66.5 reduce-scatter.20
  657.8 66.6 reduce-scatter.22
  728.1 66.6 reduce-scatter.16
  798.3 66.6 reduce-scatter.18
Sparse Core Ops, SparseCore 1:
  341.6 123.6 all-reduce.5

commit v3 on v2

--- a/solution.py
+++ b/solution.py
@@ -411,11 +411,13 @@
     def block(n, _):
         at = pl.ds(pl.multiple_of(n * 256, 256), 256)
         some = left[:, :, at].reshape(flat, 256)
-        rows_out[at, :] = dot(some, right[...].reshape(flat, right.shape[-1]), 0, 0).astype(BF16)
+        tall = dot(some, right[...].reshape(flat, right.shape[-1]), 0, 0).astype(BF16)
+        rows_out[0, n] = tall[:COLS]
+        rows_out[1, n] = tall[COLS:]
         some = cols_right[:, :, at].reshape(flat, 256)
         wide = dot(cols_left[...].reshape(flat, cols_left.shape[-1]), some, 0, 0).astype(BF16)
-        cols_out[2 * n] = wide[:, :COLS]
-        cols_out[2 * n + 1] = wide[:, COLS:]
+        cols_out[0, n] = wide[:, :COLS]
+        cols_out[1, n] = wide[:, COLS:]
         for copy in copies(n):
             copy.start()
         return 0
@@ -425,12 +427,11 @@
 
 def weight_copies(rows_out, rows_h, cols_out, cols_h, sems):
     def copies(n):
-        at = pl.ds(pl.multiple_of(n * 256, 256), 256)
-        two = pl.ds(2 * n, 2)
-        return (
-            pltpu.make_async_copy(rows_out.at[at], rows_h.at[at], sems.at[0, n]),
-            pltpu.make_async_copy(cols_out.at[two], cols_h.at[two], sems.at[1, n]),
-        )
+        return [
+            pltpu.make_async_copy(a.at[half, n], b.at[half, n], sems.at[2 * kind + half, n])
+            for kind, (a, b) in enumerate(((rows_out, rows_h), (cols_out, cols_h)))
+            for half in range(2)
+        ]
 
     return copies
 
@@ -575,17 +576,17 @@
         sds((GROUPS, ROWS, D), BF16),
         sds((8, D), F32),
         sds((8, rows), F32),
-        sds((D, rows), BF16),
-        sds((D // COLS, cols, COLS), BF16),
+        sds((2, D // 256, COLS, rows), BF16),
+        sds((2, D // 256, cols, COLS), BF16),
     )
 
 
 def back_scratch(rows, cols, loads):
     return [
-        pltpu.VMEM((D, rows), BF16),
-        pltpu.VMEM((D // COLS, cols, COLS), BF16),
+        pltpu.VMEM((2, D // 256, COLS, rows), BF16),
+        pltpu.VMEM((2, D // 256, cols, COLS), BF16),
         pltpu.SemaphoreType.DMA((loads,)),
-        pltpu.SemaphoreType.DMA((2, D // 256)),
+        pltpu.SemaphoreType.DMA((4, D // 256)),
     ]
 
 
@@ -654,8 +655,166 @@
     ).astype(F32)
 
 
+def join_rows(blocks):
+    return jnp.transpose(blocks, (1, 0, 2, 3)).reshape(D, -1)
+
+
 def join_columns(blocks):
-    return jnp.transpose(blocks, (1, 0, 2)).reshape(blocks.shape[1], -1)
+    return jnp.transpose(blocks, (2, 1, 0, 3)).reshape(blocks.shape[2], -1)
+
+
+def to_peer(axis, src, dst, sems, n, peer):
+    return pltpu.make_async_remote_copy(
+        src_ref=src,
+        dst_ref=dst,
+        send_sem=sems.at[0, n],
+        recv_sem=sems.at[1, n],
+        device_id={axis: peer},
+        device_id_type=pl.DeviceIdType.MESH,
+    )
+
+
+def reduce_kernel(*refs):
+    count = 2 * 4
+    grads, small = refs[:count], refs[count]
+    outs, small_out = refs[count + 1 : 2 * count + 1], refs[2 * count + 1]
+    rest = refs[2 * count + 2 :]
+    keeps, halves = rest[:count], rest[count : 2 * count]
+    arrivals = rest[2 * count : 3 * count]
+    totals = rest[3 * count : 4 * count]
+    small_sum, small_in, small_z = rest[4 * count : 4 * count + 3]
+    load_sem, half_sem, z_sem, out_sem, small_sem = rest[4 * count + 3 :]
+    me = lax.axis_index("dp")
+    x, z = me % 2, me // 2
+    across = me + 1 - 2 * x
+    mine = lax.axis_index("tensor")
+
+    barrier = pltpu.get_barrier_semaphore()
+
+    def greet(axis, peer):
+        pl.semaphore_signal(
+            barrier, inc=1, device_id={axis: peer}, device_id_type=pl.DeviceIdType.MESH
+        )
+
+    greet("dp", across)
+    for d in range(1, 4):
+        greet("dp", 2 * ((z + d) % 4) + x)
+        greet("tensor", (mine + d) % 4)
+    pl.semaphore_wait(barrier, 7)
+
+    def half(n):
+        return to_peer("dp", grads[n].at[1 - x], halves[n], half_sem, n, across)
+
+    def keep(n):
+        return pltpu.make_async_copy(grads[n].at[x], keeps[n], load_sem.at[n])
+
+    def shard(n, d):
+        there = (z + d) % 4
+        return to_peer(
+            "dp", keeps[n].at[there], arrivals[n].at[d - 1], z_sem.at[n], d - 1, 2 * there + x
+        )
+
+    def store(n):
+        return pltpu.make_async_copy(totals[n], outs[n], out_sem.at[n])
+
+    small_x = to_peer("dp", small, small_in, small_sem, 0, across)
+    small_x.start()
+    for n in range(count):
+        half(n).start()
+        keep(n).start()
+
+    def small_over_z(d):
+        return to_peer(
+            "dp", small_sum, small_z.at[z], small_sem, d, 2 * ((z + d) % 4) + x
+        )
+
+    def small_over_tensor(d):
+        return to_peer(
+            "tensor", small_out.at[mine], small_out.at[mine], small_sem, 3 + d, (mine + d) % 4
+        )
+
+    small_x.wait_recv()
+    small_sum[...] = small[...] + small_in[...]
+    for d in range(1, 4):
+        small_over_z(d).start()
+    small_z[z] = small_sum[...]
+    for d in range(1, 4):
+        small_over_z(d).wait_recv()
+    small_out[mine] = small_z[0] + small_z[1] + small_z[2] + small_z[3]
+    for d in range(1, 4):
+        small_over_tensor(d).start()
+
+    for n in range(count):
+        keep(n).wait()
+        half(n).wait_recv()
+        rows = keeps[n].shape[1]
+
+        def fold(i, _, n=n, rows=rows):
+            at = pl.ds(pl.multiple_of(i * 128, 128), 128)
+            for j in range(4):
+                keeps[n][j, at, :] = (
+                    keeps[n][j, at, :].astype(F32) + halves[n][j, at, :].astype(F32)
+                ).astype(BF16)
+            return 0
+
+        lax.fori_loop(0, rows // 128, fold, 0)
+        for d in range(1, 4):
+            shard(n, d).start()
+    for n in range(count):
+        for d in range(1, 4):
+            shard(n, d).wait_recv()
+        rows = keeps[n].shape[1]
+
+        def add(i, _, n=n, rows=rows):
+            at = pl.ds(pl.multiple_of(i * 128, 128), 128)
+            total = keeps[n][z, at, :].astype(F32)
+            for j in range(3):
+                total = total + arrivals[n][j, at, :].astype(F32)
+            totals[n][at, :] = total
+            return 0
+
+        lax.fori_loop(0, rows // 128, add, 0)
+        store(n).start()
+    for d in range(1, 4):
+        small_over_tensor(d).wait_recv()
+    small_x.wait_send()
+    for d in range(1, 4):
+        small_over_z(d).wait_send()
+        small_over_tensor(d).wait_send()
+    for n in range(count):
+        half(n).wait_send()
+        for d in range(1, 4):
+            shard(n, d).wait_send()
+        store(n).wait()
+
+
+def reduce_all(grads, small):
+    shapes = [g.shape[2:] for g in grads]
+    count = len(grads)
+    small_shape = small.shape
+    dma = pltpu.SemaphoreType.DMA
+    results = pl.pallas_call(
+        reduce_kernel,
+        out_shape=[sds(s, F32) for s in shapes] + [sds((4,) + small_shape, F32)],
+        in_specs=[HB] * count + [VM],
+        out_specs=[HB] * count + [VM],
+        scratch_shapes=[pltpu.VMEM((4,) + s, BF16) for s in shapes]
+        + [pltpu.VMEM((4,) + s, BF16) for s in shapes]
+        + [pltpu.VMEM((3,) + s, BF16) for s in shapes]
+        + [pltpu.VMEM(s, F32) for s in shapes]
+        + [
+            pltpu.VMEM(small_shape, F32),
+            pltpu.VMEM(small_shape, F32),
+            pltpu.VMEM((4,) + small_shape, F32),
+            dma((count,)),
+            dma((2, count)),
+            dma((count, 2, 3)),
+            dma((count,)),
+            dma((2, 7)),
+        ],
+        compiler_params=params(5),
+    )(*grads, small)
+    return results[:-1], results[-1]
 
 
 def local(
@@ -674,6 +833,7 @@
 ):
     width = w_qkv.shape[-1]
     hidden = w_fc1.shape[-1]
+    dp_size = lax.axis_size("dp")
     slot_ids = jnp.arange(PATCHES, dtype=jnp.int32)
     selector = (keep_index[:, :, None] == slot_ids[None, None, :]).astype(BF16)
     tokens = jnp.einsum("bsp,bpd->bsd", selector, patches, preferred_element_type=F32)
@@ -723,30 +883,47 @@
         shift_last = sums_a[2]
         bias_fc1_terms.insert(0, fc1_sum[0])
         bias_qv_terms.insert(0, jnp.stack([qkv_sum[0, :width], qkv_sum[0, 2 * width :]]))
-        weight_terms.insert(
-            0,
-            (
-                collect_weight(d_qkv.reshape(D, 3, width), 0),
-                collect_weight(join_columns(d_out), 1),
-                collect_weight(d_fc1, 0),
-                collect_weight(join_columns(d_fc2), 1),
-            ),
-        )
-    grad_qkv, grad_out, grad_fc1, grad_fc2 = (
-        jnp.stack([entry[k] for entry in weight_terms]) for k in range(4)
-    )
-    offset_at = lax.axis_index("tensor") * width
-    hidden_at = lax.axis_index("tensor") * hidden
-    zero_at = offset_at * 0
-    qv_full = lax.dynamic_update_slice(
-        jnp.zeros((LAYERS, 2, D), F32), jnp.stack(bias_qv_terms), (zero_at, zero_at, offset_at)
-    )
-    fc1_full = lax.dynamic_update_slice(
-        jnp.zeros((LAYERS, FF), F32), jnp.stack(bias_fc1_terms), (zero_at, hidden_at)
-    )
-    grad_gain, grad_shifts, grad_bias_qv, grad_bias_fc1 = lax.psum(
-        (jnp.stack(gain_terms), jnp.stack(shift_terms), qv_full, fc1_full), ("dp", "tensor")
-    )
+        weight_terms.insert(0, (d_qkv, d_out, d_fc1, d_fc2))
+    if dp_size == 8 and lax.axis_size("tensor") == 4 and 4 * width == D and hidden == D:
+        flat = [entry[k] for k in range(4) for entry in weight_terms]
+        lines = gain_terms + shift_terms + [row(line) for line in bias_fc1_terms]
+        lines = lines + [jnp.stack(bias_qv_terms).reshape(1, D), jnp.zeros((1, D), F32)]
+        totals, small = reduce_all(flat, jnp.concatenate(lines))
+        grad_qkv, grad_out, grad_fc1, grad_fc2 = (
+            jnp.stack([totals[LAYERS * k + n] for n in range(LAYERS)]) for k in range(4)
+        )
+        grad_qkv = grad_qkv.reshape(LAYERS, -1, 3, width)
+        summed = jnp.sum(small[:, :12], axis=0)
+        grad_gain = summed[:4].reshape(LAYERS, 2, D)
+        grad_shifts = summed[4:].reshape(LAYERS, 4, D)
+        grad_bias_fc1 = jnp.transpose(small[:, 12:14], (1, 0, 2)).reshape(LAYERS, FF)
+        quarters = small[:, 14].reshape(4, LAYERS, 2, width)
+        grad_bias_qv = jnp.transpose(quarters, (1, 2, 0, 3)).reshape(LAYERS, 2, D)
+    else:
+        grad_qkv, grad_out, grad_fc1, grad_fc2 = (
+            jnp.stack(
+                [
+                    collect_weight(join(entry[k]), split)
+                    for entry in weight_terms
+                ]
+            )
+            for k, (join, split) in enumerate(
+                ((join_rows, 0), (join_columns, 1), (join_rows, 0), (join_columns, 1))
+            )
+        )
+        grad_qkv = grad_qkv.reshape(LAYERS, -1, 3, width)
+        offset_at = lax.axis_index("tensor") * width
+        hidden_at = lax.axis_index("tensor") * hidden
+        zero_at = offset_at * 0
+        qv_full = lax.dynamic_update_slice(
+            jnp.zeros((LAYERS, 2, D), F32), jnp.stack(bias_qv_terms), (zero_at, zero_at, offset_at)
+        )
+        fc1_full = lax.dynamic_update_slice(
+            jnp.zeros((LAYERS, FF), F32), jnp.stack(bias_fc1_terms), (zero_at, hidden_at)
+        )
+        grad_gain, grad_shifts, grad_bias_qv, grad_bias_fc1 = lax.psum(
+            (jnp.stack(gain_terms), jnp.stack(shift_terms), qv_full, fc1_full), ("dp", "tensor")
+        )
     grad_patches = jnp.einsum(
         "bsp,bsd->bpd", selector.astype(F32), from_groups(gradient), precision=HIGHEST
     )

time: 883 us -> 499 us (0.57)
  waiting for transfers between devices: 517 us -> 0 us
  Pallas kernels: 279 us -> 443 us
  between operations: 15.9 us -> 0.97 us
  local copies, waits for them, and re-layouts: 55 us -> 40.1 us
    reduce_scatter x6 -> x0, waiting for transfers between devices: 382 us -> none  [collect_weight(): lax.psum_scatter(partial_grad, 'dp', scatter_dimension=split_dim, tiled=T...]
    pallas_call x0 -> x1, Pallas kernels: none -> 165 us  [reduce_all(): pl.pallas_call(reduce_kernel, out_shape=[sds(s, F32) for s in shapes] + [...]
    unnamed x11 -> x0, waiting for transfers between devices: 135 us -> none
    unnamed x39 -> x31, local copies, waits for them, and re-layouts: 17.6 us -> 5.19 us
  transfers between devices with their start and end apart: 9 -> 0, of which waited for: 8 -> 0; matrix products, arithmetic and copies ran while one was open for 3% -> 0% of each run, Pallas kernels for 0% -> 0%
where the time goes in v3:
time: 499 us; the launch traced here: 496 us
  Pallas kernels  443 us (89%)
  local copies, waits for them, and re-layouts  40.1 us (8%)
  other arithmetic  8.24 us (2%)
    pallas_call x1, Pallas kernels, reduce_all(): pl.pallas_call(reduce_kernel, out_shape=[sds(s, F32) for s in shapes] + [...  165 us
    pallas_call x2, Pallas kernels, attend_back(): pl.pallas_call(attend_back_kernel, out_shape=back_outs(3 * width, width),...  71.1 us
    pallas_call x2, Pallas kernels, attend_half(): pl.pallas_call(attend_kernel, out_shape=(sds((8, ROWS, D), BF16), sds((8,...  70.3 us
    pallas_call x2, Pallas kernels, mlp_back(): pl.pallas_call(mlp_back_kernel, out_shape=back_outs(hidden, hidden), in_s...  70.1 us
    pallas_call x2, Pallas kernels, mlp_half(): pl.pallas_call(mlp_kernel, out_shape=(sds((8, ROWS, D), BF16), sds((8, RO...  67.5 us

profile of v3, /device:TPU:0, one launch (start us, length us, event | category | flops | bytes accessed | tf_op | source)
XLA Modules:
  0.0 495.8 jit_solution(873715332351662637)
XLA Ops:
  0.6 0.0 copy-start
  0.7 1.6 slice_bitcast_fusion.6
  2.2 1.1 fusion.2
  3.3 0.1 reshape.96
  3.5 0.0 copy-start.13
  3.5 1.1 fusion.7
  4.6 0.3 multiply_reduce_fusion
  5.0 0.1 convert_element_type.30
  5.0 0.1 pad.11
  5.1 1.2 select_convert_fusion.x_own
  6.3 3.3 fusion.6
  9.5 1.7 copy.40
  11.3 1.6 copy.30.wqkv_h
  12.8 2.2 slice_bitcast_fusion.4
  15.1 0.6 slice_bitcast_fusion.16
  15.7 36.1 %shard_map.195 = (bf16[8,160,1024]{2,1,0:T(8,128)(2,1)}, bf16[8,160,768]{2,1,0:T(8,128)(2,1)}, bf16[8,640,160]{2,1,0:T(8,128)(2,1)}, bf16[8,160,256]{2,1,0:T(8,1...) custom-call(bf16[2,160,1024]{2,1,0:T(8,128)(2,1)} %select_convert_fusion.x_own, ...), custom_call_target="tpu_custom_call" | custom-call | tf_op jit(solution)/shard_map/pallas_call | solution.py:335
  51.8 0.0 copy-start.11
  51.8 6.0 %slice_bitcast_fusion = (bf16[1024,1024]{1,0:T(8,128)(2,1)}, bf16[1024,1024]{1,0:T(8,128)(2,1)}, bf16[1024,1024]{1,0:T(8,128)(2,1)}, bf16[1024,1024]{1,0:T(8,128)(2,1)}) fusion(bf16[2,1024,1024]{2,1,0:T(8,128)(2,1)} %param.22, bf16[2,1024,1024]{2,1,0:T(8,128)(2,1)} %param.20), kind=kLoop, calls=%fused_computation | loop fusion | bytes 16777216 | tf_op jit(solution)/shard_map/squeeze | solution.py:862
  57.8 0.6 fusion.12
  58.4 33.7 %shard_map.196 = (bf16[8,160,1024]{2,1,0:T(8,128)(2,1)}, bf16[8,160,1024]{2,1,0:T(8,128)(2,1)}, bf16[8,160,1024]{2,1,0:T(8,128)(2,1)}, f32[2,160,1024]{2,1,0:T(8,128)}, bf16[2,160,1024]{2,1,0:T(8,128)(2,1)}) custom-call(bf16[2,160,1024]{2,1,0:T(8,128)(2,1)} %get-tuple-element.63.x_own, f32[1,1024]{1,0:T(1,128)} %get-tuple-element.165.gain_n.gain, ...), custom_call_target="tpu_custom_call" | custom-call | tf_op jit(solution)/shard_map/pallas_call | solution.py:364
  92.1 0.9 copy.41
  93.0 1.6 copy.32.wqkv_h
  94.6 34.2 %shard_map.197 = (bf16[8,160,1024]{2,1,0:T(8,128)(2,1)}, bf16[8,160,768]{2,1,0:T(8,128)(2,1)}, bf16[8,640,160]{2,1,0:T(8,128)(2,1)}, bf16[8,160,256]{2,1,0:T(8,1...) custom-call(bf16[2,160,1024]{2,1,0:T(8,128)(2,1)} %get-tuple-element.65.x_own, ...), custom_call_target="tpu_custom_call" | custom-call | tf_op jit(solution)/shard_map/pallas_call | solution.py:335
  128.8 33.7 %shard_map.198 = (bf16[8,160,1024]{2,1,0:T(8,128)(2,1)}, bf16[8,160,1024]{2,1,0:T(8,128)(2,1)}, bf16[8,160,1024]{2,1,0:T(8,128)(2,1)}, f32[2,160,1024]{2,1,0:T(8,128)}, bf16[2,160,1024]{2,1,0:T(8,128)(2,1)}) custom-call(bf16[2,160,1024]{2,1,0:T(8,128)(2,1)} %get-tuple-element.67.x_own, f32[1,1024]{1,0:T(1,128)} %get-tuple-element.165.gain_n.gain, ...), custom_call_target="tpu_custom_call" | custom-call | tf_op jit(solution)/shard_map/pallas_call | solution.py:364
  162.5 1.4 slice.178
  163.9 0.1 reshape.97
  164.1 0.1 fusion.5
  164.1 0.9 copy-done.2
  165.0 1.3 fusion
  166.3 0.1 reshape.98
  166.5 1.2 pad.13.gradient_h
  167.7 0.9 pad.46.x_own
  168.6 35.0 %shard_map.199 = (f32[2,160,1024]{2,1,0:T(8,128)}, bf16[2,160,1024]{2,1,0:T(8,128)(2,1)}, f32[8,1024]{1,0:T(8,128)}, f32[8,1024]{1,0:T(8,128)}, bf16[2,4,128,102...) custom-call(bf16[2,160,1024]{2,1,0:T(8,128)(2,1)} %pad.46.x_own, f32[1,1024]{1,0:T(1,128)} %get-tuple-element.166.norm2.gain, ...), custom_call_target="tpu_custom_call" | custom-call | tf_op jit(solution)/shard_map/pallas_call | solution.py:596
  203.6 35.6 %shard_map.200 = (f32[2,160,1024]{2,1,0:T(8,128)}, bf16[2,160,1024]{2,1,0:T(8,128)(2,1)}, f32[8,1024]{1,0:T(8,128)}, f32[8,768]{1,0:T(8,128)}, bf16[2,4,128,768]...) custom-call(bf16[2,160,1024]{2,1,0:T(8,128)(2,1)} %get-tuple-element.73.x_own, ...), custom_call_target="tpu_custom_call" | custom-call | tf_op jit(solution)/shard_map/pallas_call | solution.py:620
  239.2 35.0 %shard_map.201 = (f32[2,160,1024]{2,1,0:T(8,128)}, bf16[2,160,1024]{2,1,0:T(8,128)(2,1)}, f32[8,1024]{1,0:T(8,128)}, f32[8,1024]{1,0:T(8,128)}, bf16[2,4,128,102...) custom-call(bf16[2,160,1024]{2,1,0:T(8,128)(2,1)} %get-tuple-element.79.x_own, ...), custom_call_target="tpu_custom_call" | custom-call | tf_op jit(solution)/shard_map/pallas_call | solution.py:596
  274.2 35.5 %shard_map.202 = (f32[2,160,1024]{2,1,0:T(8,128)}, bf16[2,160,1024]{2,1,0:T(8,128)(2,1)}, f32[8,1024]{1,0:T(8,128)}, f32[8,768]{1,0:T(8,128)}, bf16[2,4,128,768]...) custom-call(bf16[2,160,1024]{2,1,0:T(8,128)(2,1)} %get-tuple-element.84.x_own, f32[1,1024]{1,0:T(1,128)} %get-tuple-element.169.gain, ...), custom_call_target="tpu_custom_call" | custom-call | tf_op jit(solution)/shard_map/pallas_call | solution.py:620
  309.8 0.7 fusion.10
  310.5 0.7 fusion.11
  311.3 0.8 fusion.9
  312.1 0.8 slice.185
  312.9 0.8 slice.181
  313.6 0.8 slice.189
  314.4 0.9 fusion.8
  315.3 0.8 slice.188
  316.0 0.8 slice.183
  316.8 0.8 slice.190
  317.6 1.3 concatenate.4.refs_8_
  318.9 164.6 %shard_map.203 = (f32[128,768]{1,0:T(8,128)}, f32[128,768]{1,0:T(8,128)}, f32[256,128]{1,0:T(8,128)}, f32[256,128]{1,0:T(8,128)}, f32[128,1024]{1,0:T(8,128)}, /...) custom-call(bf16[2,4,128,768]{3,2,1,0:T(8,128)(2,1)} %get-tuple-element.91.refs_0_, ...), custom_call_target="tpu_custom_call" | custom-call | tf_op jit(solution)/shard_map/pallas_call | solution.py:796
  483.5 2.3 pad_maximum_fusion.1
  485.9 1.1 pad_maximum_fusion
  487.0 0.7 pad_maximum_fusion.3
  487.7 0.2 copy.35
  487.8 0.2 copy.36
  488.0 0.1 pad_maximum_fusion.2
  488.1 1.1 copy.38
  489.3 0.6 reshape.102
  489.9 0.6 reshape.101
  490.5 0.1 slice_reduce_fusion.1
  490.6 0.6 copy.42
  491.2 0.6 slice.199
  491.9 1.4 slice.179
  493.3 0.1 reshape.99
  493.4 0.5 copy-done.10
  493.9 1.9 fusion.1
  (36 shorter events, 0.2 us)
Async XLA Ops:
  0.6 1.6 copy-start
  3.5 1.5 copy-start.13
  12.8 2.2 copy-start.12
  51.8 6.0 %copy-start.11 = (f32[2,1024]{1,0:T(2,128)S(1)}, f32[2,1024]{1,0:T(2,128)}, u32[]{:S(2)}) copy-start(f32[2,1024]{1,0:T(2,128)} %param.21) | copy-start | bytes 24580
  163.9 1.1 copy-start.2
  483.5 2.4 copy-start.3
  483.5 2.3 copy-start.4
  485.8 1.1 copy-start.8
  485.8 1.1 copy-start.9
  485.8 1.8 copy-start.6
  485.9 2.0 copy-start.5
  488.0 1.2 copy-start.7
  493.2 0.7 copy-start.10
  493.2 2.6 copy-start.1

commit v4 on v1

v4 whole, which is shorter than its diff:
```python
from functools import partial

import jax
import jax.numpy as jnp
from jax import lax
from jax.experimental import pallas as pl
from jax.experimental.pallas import tpu as pltpu
from jax.sharding import PartitionSpec as P

D = 1024
HEAD = 64
FF = 4096
LAYERS = 2
PATCHES = 50
EPS = 1e-06
HIGHEST = lax.Precision.HIGHEST
F32 = jnp.float32
BF16 = jnp.bfloat16

GROUPS = 2
ROWS = 160
LIVE = 150
COLS = 128
SCALE = HEAD ** (-0.5)


def dot(a, b, lhs=1, rhs=0):
    return lax.dot_general(a, b, (((lhs,), (rhs,)), ((), ())), preferred_element_type=F32)


def remote(src, dst, send, recv, peer):
    return pltpu.make_async_remote_copy(
        src_ref=src,
        dst_ref=dst,
        send_sem=send,
        recv_sem=recv,
        device_id={"tensor": peer},
        device_id_type=pl.DeviceIdType.MESH,
    )


def norm_parts(values):
    average = jnp.mean(values, axis=-1, keepdims=True)
    centred = values - average
    variance = jnp.mean(centred * centred, axis=-1, keepdims=True)
    scale = lax.rsqrt(variance + EPS)
    return centred * scale, scale


def head_mask(h, width):
    lane = lax.broadcasted_iota(jnp.int32, (1, width), 1)
    return (lane // HEAD == h).astype(F32).astype(BF16)


class Exchange:
    def __init__(self, gath, part, bufs, sems):
        self.gath, self.part = gath, part
        self.out_po, self.out_pd, self.out_y, self.in_po, self.in_pd, self.in_y = bufs
        self.sem = sems
        me = lax.axis_index("tensor")
        self.me = me
        self.mate = me + 1 - 2 * (me % 2)
        self.far = (me + 2) % 4
        self.diag = (self.mate + 2) % 4
        self.stage = 0

    def barrier(self):
        sem = pltpu.get_barrier_semaphore()
        for peer in (self.mate, self.far):
            pl.semaphore_signal(
                sem, inc=1, device_id={"tensor": peer}, device_id_type=pl.DeviceIdType.MESH
            )
        pl.semaphore_wait(sem, 2)

    def own(self, g):
        return GROUPS * self.me + g

    def rows(self, slot):
        return self.gath.at[self.stage % 2, slot]

    def copy(self, kind, g):
        s = self.sem
        own, slot = self.rows(self.own(g)), self.rows(GROUPS * self.far + g)
        src, dst, peer = (
            (own, own, self.far),
            (own, own, self.mate),
            (slot, slot, self.mate),
            (self.out_po.at[g], self.in_po.at[g], self.mate),
            (self.out_pd.at[g], self.in_pd.at[g], self.mate),
            (self.out_y.at[g], self.in_y.at[g], self.far),
        )[kind]
        return remote(src, dst, s.at[0, kind, g], s.at[1, kind, g], peer)

    def again(self, kind, g):
        if self.stage:
            self.copy(kind, g).wait_send()

    def send(self, kind, g):
        self.copy(kind, g).start()

    def share(self, g):
        for kind in range(2):
            self.again(kind, g)
            self.send(kind, g)

    def slot(self, i):
        even = i % 2 == 0
        owner = jnp.where(
            i < 4,
            jnp.where(even, self.me, self.mate),
            jnp.where(even, self.far, self.diag),
        )
        return GROUPS * owner + (i // 2) % 2

    def before(self, i):
        for g in range(GROUPS):

            @pl.when(i == 1 + 2 * g)
            def _():
                self.copy(1, g).wait_recv()

            @pl.when(i == 4 + 2 * g)
            def _():
                self.copy(0, g).wait_recv()
                self.again(2, g)
                self.send(2, g)

            @pl.when(i == 5 + 2 * g)
            def _():
                self.copy(2, g).wait_recv()

    def after(self, i):
        for g in range(GROUPS):

            @pl.when(i == 1 + 2 * g)
            def _():
                self.again(3, g)
                self.out_po[g] = self.part[1 + 2 * g].astype(BF16)
                self.send(3, g)

            @pl.when(i == 5 + 2 * g)
            def _():
                self.again(4, g)
                self.out_pd[g] = self.part[5 + 2 * g].astype(BF16)
                self.send(4, g)
                self.copy(4, g).wait_recv()
                self.again(5, g)
                self.out_y[g] = (self.part[4 + 2 * g] + self.in_pd[g].astype(F32)).astype(BF16)
                self.send(5, g)

    def total(self, g):
        self.copy(3, g).wait_recv()
        self.copy(5, g).wait_recv()
        return self.part[2 * g] + self.in_po[g].astype(F32) + self.in_y[g].astype(F32)

    def end(self):
        for g in range(GROUPS):
            for kind in range(6):
                self.copy(kind, g).wait_send()


def exchange_scratch():
    return [
        pltpu.VMEM((2, 8, ROWS, D), BF16),
        pltpu.VMEM((8, ROWS, D), F32),
    ] + [pltpu.VMEM((GROUPS, ROWS, D), BF16)] * 6 + [pltpu.SemaphoreType.DMA((2, 6, GROUPS))]


def picker(keep, g):
    patch = lax.broadcasted_iota(jnp.int32, (ROWS, ROWS), 0)
    return (keep[g] == patch).astype(F32).astype(BF16)


def attend(x, q_bias, v_bias, wqkv, wout, counts, keep_parts):
    width = wout.shape[0]
    triple = dot(x, wqkv[...])
    q = (triple[:, :width] + q_bias).astype(BF16)
    k = triple[:, width : 2 * width].astype(BF16)
    v = (triple[:, 2 * width :] + v_bias).astype(BF16)
    keep_parts(0, q, k, v)
    lane = lax.broadcasted_iota(jnp.int32, (1, ROWS), 1)
    image = lane // PATCHES
    count = jnp.where(image == 0, counts[6:7], jnp.where(image == 1, counts[7:8], counts[8:9]))
    fits = (lane - image * PATCHES).astype(F32) < count
    row = lax.broadcasted_iota(jnp.int32, (ROWS, ROWS), 0)
    col = lax.broadcasted_iota(jnp.int32, (ROWS, ROWS), 1)
    same = jnp.minimum(row // PATCHES, 2) == col // PATCHES
    veil = jnp.where(same, 0.0, -1e30) + jnp.where(fits, 0.0, -1e30)
    mixed = jnp.zeros((ROWS, width), F32)
    for h in range(width // HEAD):
        mask = head_mask(h, width)
        scores = dot(q * mask, k, 1, 1) * SCALE + veil
        peak = jnp.max(scores, axis=-1, keepdims=True)
        raised = jnp.exp(scores - peak)
        weight = raised * (1.0 / jnp.sum(raised, axis=-1, keepdims=True))
        rounded = weight.astype(BF16)
        keep_parts(1 + h, rounded)
        mixed = mixed + dot(rounded, v * mask)
    return mixed.astype(BF16)


def erf_parts(pre):
    cdf = 0.5 * (1.0 + lax.erf(pre * (0.5 ** 0.5)))
    pdf = jnp.exp(-0.5 * pre * pre) * 0.3989422804014327
    return cdf, pdf


def forward_kernel(
    patches, keep, counts, gains, shifts, bias_qv, bias_fc1, wqkv_h, wout_h, w1_h, w2_h,
    flow_h, gath_h, qkv_h, prob_h, att_h, gmlp_h, act_h, slope_h,
    gath, part, out_po, out_pd, out_y, in_po, in_pd, in_y, ex_sem,
    flow, wqkv, wout, w1, w2, qkv, prob, att, act, slope, load_sem, save_sem, flow_sem,
):
    ex = Exchange(gath, part, (out_po, out_pd, out_y, in_po, in_pd, in_y), ex_sem)
    width, hidden = wout.shape[1], w1.shape[2]
    stages = 2 * LAYERS
    loads = []
    for n in range(LAYERS):
        pieces = [
            (wqkv_h.at[n, c], wqkv.at[n, :, pl.ds(c * width, width)]) for c in range(3)
        ] + [(wout_h.at[n], wout.at[n])]
        loads.append([pltpu.make_async_copy(*p, load_sem.at[6 * n + m]) for m, p in enumerate(pieces)])
        pieces = [(w1_h.at[n], w1.at[n]), (w2_h.at[n], w2.at[n])]
        loads.append(
            [pltpu.make_async_copy(*p, load_sem.at[6 * n + 4 + m]) for m, p in enumerate(pieces)]
        )
    for group in loads:
        for copy in group:
            copy.start()
    ex.barrier()

    def save_flow(s, g):
        return pltpu.make_async_copy(flow.at[s, g], flow_h.at[s, g], flow_sem.at[s, g])

    def produce(s, g):
        n = s // 2
        if s == 0:
            value = dot(picker(keep, g), patches[g], 0, 0)
        else:
            before = (s - 1) // 2
            shift = shifts[before, 2 + (s - 1) % 2].reshape(1, D)
            value = flow[s - 1, g] + ex_last.total(g) + shift
        flow[s, g] = value
        save_flow(s, g).start()
        if s == stages:
            return
        unit, _ = norm_parts(value)
        gain, shift = gains[n, s % 2].reshape(1, D), shifts[n, s % 2].reshape(1, D)
        own = ex.own(g)
        gath[s % 2, own] = (unit * gain + shift).astype(BF16)
        tail = gath[s % 2, own, ROWS - 16 : ROWS, 0:256].astype(F32)
        row = lax.broadcasted_iota(jnp.int32, (16, 256), 0)
        tail = jnp.where(row >= LIVE - ROWS + 16, counts[g], tail)
        gath[s % 2, own, ROWS - 16 : ROWS, 0:256] = tail.astype(BF16)
        ex.share(g)

    def saves(s, slot):
        n = s // 2
        if s % 2 == 0:
            pairs = ((gath.at[0], gath_h), (qkv, qkv_h), (prob, prob_h), (att, att_h))
        else:
            pairs = ((gath.at[1], gmlp_h), (act, act_h), (slope, slope_h))
        return [
            pltpu.make_async_copy(a.at[slot], b.at[n, slot], save_sem.at[m, slot])
            for m, (a, b) in enumerate(pairs)
        ]

    def drain(s):
        def one(slot, _):
            for copy in saves(s, slot):
                copy.wait()
            return 0

        lax.fori_loop(0, 8, one, 0)

    ex_last = ex
    for s in range(stages):
        n = s // 2
        ex.stage = s
        produce(s, 0)
        if s == 0:
            produce(s, 1)
        else:
            drain(s - 1)
        for copy in loads[s]:
            copy.wait()

        def step(i, _, s=s, n=n):
            if s:

                @pl.when(i == 2)
                def _():
                    produce(s, 1)

            ex.before(i)
            slot = ex.slot(i)
            x = gath[s % 2, slot]
            if s % 2 == 0:

                def keep_parts(kind, *values):
                    if kind == 0:
                        for c, value in enumerate(values):
                            qkv[slot, :, c * width : (c + 1) * width] = value
                    else:
                        prob[slot, (kind - 1) * ROWS : kind * ROWS] = values[0]

                tail = gath[0, slot, ROWS - 16 : ROWS, 0:256][:, 0:ROWS].astype(F32)
                mixed = attend(
                    x, bias_qv[n, 0:1], bias_qv[n, 1:2], wqkv.at[n], wout.at[n], tail, keep_parts
                )
                att[slot] = mixed
                part[i] = dot(mixed, wout[n])
            else:
                for block in range(hidden // 256):
                    at = slice(block * 256, block * 256 + 256)
                    pre = dot(x, w1[n, :, at]) + bias_fc1[n : n + 1, at]
                    cdf, pdf = erf_parts(pre)
                    act[slot, :, at] = (pre * cdf).astype(BF16)
                    slope[slot, :, at] = (cdf + pre * pdf).astype(BF16)
                part[i] = dot(act[slot], w2[n])
            for copy in saves(s, slot):
                copy.start()
            ex.after(i)
            return 0

        lax.fori_loop(0, 8, step, 0)
    for g in range(GROUPS):
        produce(stages, g)
    drain(stages - 1)
    ex.end()
    for s in range(stages + 1):
        for g in range(GROUPS):
            save_flow(s, g).wait()


VM = pl.BlockSpec(memory_space=pltpu.VMEM)
HB = pl.BlockSpec(memory_space=pl.ANY)


def sds(shape, dtype):
    return jax.ShapeDtypeStruct(shape, dtype)


def params(n):
    return pltpu.CompilerParams(
        collective_id=n, has_side_effects=True, vmem_limit_bytes=67043328
    )


def forward(patches, keep, counts, gains, shifts, bias_qv, bias_fc1, wqkv, wout, w1, w2):
    width, hidden = wout.shape[1], w1.shape[2]
    heads = width // HEAD
    wide = (8, ROWS, D)
    inner = ((8, ROWS, 3 * width), (8, heads * ROWS, ROWS), (8, ROWS, width))
    mlp = ((8, ROWS, hidden), (8, ROWS, hidden))
    kept = (wide,) + inner + (wide,) + mlp
    steps = (2 * LAYERS + 1, GROUPS, ROWS, D)
    dma = pltpu.SemaphoreType.DMA
    return pl.pallas_call(
        forward_kernel,
        out_shape=(sds(steps, F32),) + tuple(sds((LAYERS,) + k, BF16) for k in kept),
        in_specs=[VM] * 7 + [HB] * 4,
        out_specs=(HB,) * 8,
        scratch_shapes=exchange_scratch()
        + [
            pltpu.VMEM(steps, F32),
            pltpu.VMEM((LAYERS, D, 3 * width), BF16),
            pltpu.VMEM((LAYERS, width, D), BF16),
            pltpu.VMEM((LAYERS, D, hidden), BF16),
            pltpu.VMEM((LAYERS, hidden, D), BF16),
        ]
        + [pltpu.VMEM(k, BF16) for k in inner + mlp]
        + [dma((6 * LAYERS,)), dma((4, 8)), dma((2 * LAYERS + 1, GROUPS))],
        compiler_params=params(1),
    )(patches, keep, counts, gains, shifts, bias_qv, bias_fc1, wqkv, wout, w1, w2)


def column_sums(values):
    return jnp.sum(values, axis=0, keepdims=True)


class Scatter:
    def __init__(self, made, halves, arrivals, totals, outs, sems):
        self.made, self.halves, self.arrivals = made, halves, arrivals
        self.totals, self.outs = totals, outs
        self.x_sem, self.z_sem, self.out_sem, self.x_free, self.z_free = sems
        me = lax.axis_index("dp")
        self.x, self.z = me % 2, me // 2
        self.across = me + 1 - 2 * self.x

    def peer(self, k):
        return 2 * ((self.z + k) % 4) + self.x

    def shard(self, k):
        return (self.z + k) % 4

    def over_x(self, kind, part, k):
        n = self.shard(k)
        return to_peer(
            "dp",
            self.made[kind][part].at[1 - self.x, n],
            self.halves[kind][part].at[n],
            self.x_sem.at[kind, part, k, 0],
            self.x_sem.at[kind, part, k, 1],
            self.across,
        )

    def over_z(self, kind, part, k):
        return to_peer(
            "dp",
            self.made[kind][part].at[self.x, self.shard(k)],
            self.arrivals[kind][part].at[k - 1],
            self.z_sem.at[kind, part, k, 0],
            self.z_sem.at[kind, part, k, 1],
            self.peer(k),
        )

    def ready(self, s, part):
        if s >= 2:
            for k in range(4):
                self.over_x(s % 2, part, k).wait_send()
                if k:
                    self.over_z(s % 2, part, k).wait_send()

    def send(self, s, part, k):
        if s >= 2:
            pl.semaphore_wait(self.x_free.at[s % 2, part], 1)
        self.over_x(s % 2, part, k).start()

    def fold(self, s, part, k):
        kind = s % 2
        made, half = self.made[kind][part], self.halves[kind][part]
        total = self.totals[kind][part]
        n = self.shard(k)
        self.over_x(kind, part, k).wait_recv()
        last = isinstance(k, int) and k == 0
        if last and s >= 2:
            self.store(s - 2, part, wait=True)

        def add(i, _):
            at = pl.ds(pl.multiple_of(i * COLS, COLS), COLS)
            both = made[self.x, n, at, :].astype(F32) + half[n, at, :].astype(F32)
            if last:
                total[at, :] = both
            else:
                made[self.x, n, at, :] = both.astype(BF16)
            return 0

        lax.fori_loop(0, half.shape[1] // COLS, add, 0)
        if s < 2:
            pl.semaphore_signal(
                self.x_free.at[kind, part],
                inc=1,
                device_id={"dp": self.across},
                device_id_type=pl.DeviceIdType.MESH,
            )
        if not last:
            if s >= 2:
                pl.semaphore_wait(self.z_free.at[kind, part, k], 1)
            self.over_z(kind, part, k).start()

    def store(self, s, part, wait=False):
        kind, n = s % 2, LAYERS - 1 - s // 2
        total, out = self.totals[kind][part], self.outs[kind][part]
        if kind == 1 and part == 1:
            width = out.shape[-1]
            pairs = [(total.at[:, pl.ds(c * width, width)], out.at[n, c]) for c in range(3)]
        else:
            pairs = [(total, out.at[n])]
        for c, pair in enumerate(pairs):
            copy = pltpu.make_async_copy(*pair, self.out_sem.at[kind, part, c])
            if wait:
                copy.wait()
            else:
                copy.start()

    def finish(self, s, part):
        kind = s % 2
        total, arrivals = self.totals[kind][part], self.arrivals[kind][part]
        for k in range(1, 4):
            self.over_z(kind, part, k).wait_recv()

        def add(i, _):
            at = pl.ds(pl.multiple_of(i * COLS, COLS), COLS)
            value = total[at, :]
            for k in range(3):
                value = value + arrivals[k, at, :].astype(F32)
            total[at, :] = value
            return 0

        lax.fori_loop(0, total.shape[0] // COLS, add, 0)
        self.store(s, part)
        if s < 2:
            for k in range(1, 4):
                pl.semaphore_signal(
                    self.z_free.at[kind, part, k],
                    inc=1,
                    device_id={"dp": self.peer(4 - k)},
                    device_id_type=pl.DeviceIdType.MESH,
                )

    def end(self):
        for s in (2, 3):
            for part in range(2):
                self.ready(s, part)
                self.store(s, part, wait=True)


def to_peer(axis, src, dst, send, recv, peer):
    return pltpu.make_async_remote_copy(
        src_ref=src,
        dst_ref=dst,
        send_sem=send,
        recv_sem=recv,
        device_id={axis: peer},
        device_id_type=pl.DeviceIdType.MESH,
    )


def sum_small(lines, arrived, over_z, out, sem, sc, mine):
    across = to_peer("dp", lines, arrived, sem.at[0, 0], sem.at[1, 0], sc.across)
    across.start()
    across.wait_recv()
    across.wait_send()
    over_z[sc.z] = lines[...] + arrived[...]

    def along(k):
        part = over_z.at[sc.z]
        return to_peer("dp", part, part, sem.at[0, k], sem.at[1, k], sc.peer(k))

    for k in range(1, 4):
        along(k).start()
    for k in range(1, 4):
        along(k).wait_recv()
    out[mine] = over_z[0] + over_z[1] + over_z[2] + over_z[3]

    def around(k):
        part = out.at[mine]
        return to_peer("tensor", part, part, sem.at[0, 3 + k], sem.at[1, 3 + k], (mine + k) % 4)

    for k in range(1, 4):
        around(k).start()
    for k in range(1, 4):
        along(k).wait_send()
        around(k).wait()


def backward_kernel(
    fused,
    cot, keep, gains, flow_h, wqkv_h, wout_h, w1_h, w2_h,
    gath_h, qkv_h, prob_h, att_h, gmlp_h, act_h, slope_h,
    patch_grad, small_out, o_fc2, o_fc1, o_out, o_qkv,
    gath, part, out_po, out_pd, out_y, in_po, in_pd, in_y, ex_sem,
    gradient, source, wqkv, wout, w1, w2, qkv, prob, att, norm_a, act, slope, norm_m,
    pre, triple, lines, cols_m, rows_m, cols_a, rows_a, load_sem, *rest,
):
    ex = Exchange(gath, part, (out_po, out_pd, out_y, in_po, in_pd, in_y), ex_sem)
    width, hidden = wout.shape[0], w1.shape[1]
    stages = 2 * LAYERS
    flat = 8 * ROWS
    made = ((cols_m, rows_m), (cols_a, rows_a))
    outs = ((o_fc2, o_fc1), (o_out, o_qkv))
    if fused:
        halves, arrivals, totals = (
            ((rest[4 * n], rest[4 * n + 1]), (rest[4 * n + 2], rest[4 * n + 3])) for n in range(3)
        )
        small_in, small_z, small_sem = rest[12:15]
        sc = Scatter(made, halves, arrivals, totals, outs, rest[15:20])
        z = sc.z
    else:
        sc, z = None, 0
        save_sem = rest[0]

    def layer(s):
        return LAYERS - 1 - s // 2

    def loads(s):
        n = layer(s)
        if s % 2 == 0:
            pairs = (
                (w2_h.at[n], w2),
                (slope_h.at[n], slope),
                (w1_h.at[n], w1),
                (act_h.at[n], act),
                (gmlp_h.at[n], norm_m),
                (flow_h.at[2 * n + 1], source.at[0]),
            )
        else:
            pairs = tuple(
                (wqkv_h.at[n, c], wqkv.at[:, pl.ds(c * width, width)]) for c in range(3)
            ) + (
                (wout_h.at[n], wout),
                (qkv_h.at[n], qkv),
                (prob_h.at[n], prob),
                (att_h.at[n], att),
                (gath_h.at[n], norm_a),
                (flow_h.at[2 * n], source.at[1]),
            )
        return [
            pltpu.make_async_copy(*pair, load_sem.at[s % 2, m]) for m, pair in enumerate(pairs)
        ]

    for s in range(2):
        for copy in loads(s):
            copy.start()
    barrier = pltpu.get_barrier_semaphore()
    peers = [{"tensor": ex.mate}, {"tensor": ex.far}]
    if fused:
        peers += [{"tensor": ex.diag}, {"dp": sc.across}]
        peers += [{"dp": sc.peer(k)} for k in range(1, 4)]
    for peer in peers:
        pl.semaphore_signal(barrier, inc=1, device_id=peer, device_id_type=pl.DeviceIdType.MESH)
    pl.semaphore_wait(barrier, len(peers))

    def note(at, g, row):
        lines[at : at + 1] = row if g == 0 else lines[at : at + 1] + row

    def produce(s, g):
        if s == 0:
            rounded = cot[g]
            gradient[g] = rounded.astype(F32)
        else:
            n, side = layer(s - 1), s % 2
            gain = gains[n, side].reshape(1, D)
            moved = ex.total(g)
            unit, scale = norm_parts(source[1 - side, g])
            note(2 * n + side, g, column_sums(moved * unit))
            note(4 + 4 * n + side, g, column_sums(moved))
            scaled = moved * gain
            lean = jnp.mean(scaled, axis=-1, keepdims=True)
            tilt = jnp.mean(scaled * unit, axis=-1, keepdims=True)
            grad = gradient[g] + scale * (scaled - lean - unit * tilt)
            rounded = grad.astype(BF16)
            if s < stages:
                gradient[g] = grad
            else:
                pick = picker(keep, g)
                rest_of = (grad - rounded.astype(F32)).astype(BF16)
                patch_grad[g] = dot(pick, rounded) + dot(pick, rest_of)
                return
        if s % 2 == 0:
            note(4 + 4 * layer(s) + 3, g, column_sums(rounded.astype(F32)))
        else:
            note(4 + 4 * layer(s) + 2, g, column_sums(rounded.astype(F32)))
        gath[s % 2, ex.own(g)] = rounded
        ex.share(g)

    def spill(s, part, k):
        m = (z + k) % 4
        return [
            pltpu.make_async_copy(
                made[s % 2][part].at[half, m],
                outs[s % 2][part].at[layer(s), half, m],
                save_sem.at[s % 2, part, k, half],
            )
            for half in range(2)
        ]

    def column_block(s, j):
        k = (j + 1) % 4
        n = (z + k) % 4
        at = pl.ds(pl.multiple_of(n * 256, 256), 256)
        some = gath[s % 2, :, :, at].reshape(flat, 256)
        left = (act, att)[s % 2]
        wide = dot(left[...].reshape(flat, left.shape[-1]), some, 0, 0).astype(BF16)
        out = made[s % 2][0]
        out[0, n] = wide[:, :COLS]
        out[1, n] = wide[:, COLS:]
        if fused:
            sc.send(s, 0, k)
        else:
            for copy in spill(s, 0, k):
                copy.start()

    def row_block(s, j):
        k = (j + 1) % 4
        n = (z + k) % 4
        at = pl.ds(pl.multiple_of(n * 256, 256), 256)
        left, right = ((norm_m, pre), (norm_a, triple))[s % 2]
        some = left[:, :, at].reshape(flat, 256)
        tall = dot(some, right[...].reshape(flat, right.shape[-1]), 0, 0).astype(BF16)
        out = made[s % 2][1]
        out[0, n] = tall[:COLS]
        out[1, n] = tall[COLS:]
        if fused:
            sc.send(s, 1, k)
        else:
            for copy in spill(s, 1, k):
                copy.start()

    def settle(s, part):
        if fused:
            sc.ready(s, part)
        elif s >= 2:
            for k in range(4):
                for copy in spill(s - 2, part, k):
                    copy.wait()

    def columns(s):
        settle(s, 0)

        def one(j, _):
            column_block(s, j)
            return 0

        lax.fori_loop(0, 4, one, 0)

    def some_rows(s, start, count):
        def one(j, _):
            row_block(s, start + j)
            return 0

        lax.fori_loop(0, count, one, 0)

    def bias_sums(s):
        n = layer(s)
        ones = jnp.ones((8, flat), BF16)
        if s % 2 == 0:
            lines[12 + n : 13 + n] = dot(ones, pre[...].reshape(flat, hidden))[0:1]
        else:
            sums = dot(ones, triple[...].reshape(flat, 3 * width))[0:1]
            at = 2 * n * width
            lines[14:15, at : at + width] = sums[:, :width]
            lines[14:15, at + width : at + 2 * width] = sums[:, 2 * width :]

    def folds(s, part, first, count):
        if not fused:
            return
        away = min(first + count, 4) - first

        def one(k, _):
            sc.fold(s, part, k)
            return 0

        if away > 0:
            lax.fori_loop(first, first + away, one, 0)
        if first + count > 4:
            sc.fold(s, part, 0)

    def finish(s):
        if fused:
            for part in range(2):
                sc.finish(s, part)

    lines[15:16] = jnp.zeros((1, D), F32)
    plan = {
        (1, 4): lambda: folds(0, 0, 1, 1),
        (1, 6): lambda: folds(0, 0, 2, 2),
        (1, 8): lambda: folds(0, 0, 4, 1),
        (2, 2): lambda: folds(0, 1, 1, 1),
        (2, 4): lambda: folds(0, 1, 2, 1),
        (2, 6): lambda: folds(0, 1, 3, 2),
        (3, 2): lambda: folds(1, 0, 1, 4),
        (3, 4): lambda: folds(1, 1, 1, 2),
        (3, 6): lambda: folds(1, 1, 3, 2),
        (3, 8): lambda: finish(0),
    }

    for s in range(stages):
        ex.stage = s
        if s:
            columns(s - 1)
        produce(s, 0)
        if s == 0:
            produce(s, 1)
        early = (3, 6)[s % 2]
        for copy in loads(s)[:early]:
            copy.wait()

        def step(i, _, s=s):
            if s:

                @pl.when(i == 2)
                def _():
                    settle(s - 1, 1)

                @pl.when((i == 2) | (i == 4))
                def _():
                    some_rows(s - 1, i - 2, 2)

                @pl.when(i == 2)
                def _():
                    produce(s, 1)

                @pl.when(i == 6)
                def _():
                    bias_sums(s - 1)
                    if s + 1 < stages:
                        for copy in loads(s + 1) if s >= 1 else ():
                            copy.start()

            for (stage, at), task in plan.items():
                if stage == s and at < 8:
                    pl.when(i == at)(task)
            ex.before(i)
            slot = ex.slot(i)
            grad = gath[s % 2, slot]
            if s % 2 == 0:
                for block in range(hidden // 256):
                    at = slice(block * 256, block * 256 + 256)
                    d_act = dot(grad, w2[at, :], 1, 1)
                    pre[slot, :, at] = (d_act * slope[slot, :, at].astype(F32)).astype(BF16)
                part[i] = dot(pre[slot], w1[...], 1, 1)
            else:
                d_att = dot(grad, wout[...], 1, 1).astype(BF16)
                q = qkv[slot, :, 0:width]
                k = qkv[slot, :, width : 2 * width]
                v = qkv[slot, :, 2 * width :]
                d_q = jnp.zeros((ROWS, width), F32)
                d_k = jnp.zeros((ROWS, width), F32)
                d_v = jnp.zeros((ROWS, width), F32)
                for h in range(width // HEAD):
                    mask = head_mask(h, width)
                    d_one = d_att * mask
                    rounded = prob[slot, h * ROWS : (h + 1) * ROWS]
                    weight = rounded.astype(F32)
                    d_prob = dot(d_one, v, 1, 1)
                    centre = jnp.sum(weight * d_prob, axis=-1, keepdims=True)
                    d_scores = (weight * (d_prob - centre)).astype(BF16)
                    d_q = d_q + dot(d_scores, k * mask)
                    d_k = d_k + dot(d_scores, q * mask, 0, 0)
                    d_v = d_v + dot(rounded, d_one, 0, 0)
                triple[slot, :, 0:width] = (d_q * SCALE).astype(BF16)
                triple[slot, :, width : 2 * width] = (d_k * SCALE).astype(BF16)
                triple[slot, :, 2 * width :] = d_v.astype(BF16)
                part[i] = dot(triple[slot], wqkv[...], 1, 1)
            ex.after(i)
            return 0

        lax.fori_loop(0, 8, step, 0)
        for copy in loads(s)[early:]:
            copy.wait()
        if (s, 8) in plan:
            plan[s, 8]()
    last = stages - 1
    columns(last)
    settle(last, 1)
    some_rows(last, 0, 4)
    bias_sums(last)
    for g in range(GROUPS):
        produce(stages, g)
    ex.end()
    if fused:
        folds(2, 0, 1, 2)
        sum_small(lines, small_in, small_z, small_out, small_sem, sc, ex.me)
        finish(1)
        folds(2, 0, 3, 2)
        folds(2, 1, 1, 4)
        folds(3, 0, 1, 4)
        sc.finish(2, 0)
        folds(3, 1, 1, 4)
        sc.finish(2, 1)
        finish(3)
        sc.end()
    else:
        small_out[...] = lines[...]
        for s in (2, 3):
            for side in range(2):
                for k in range(4):
                    for copy in spill(s, side, k):
                        copy.wait()


def backward(fused, cot, keep, gains, flow, wqkv, wout, w1, w2, kept):
    width, hidden = wout.shape[1], w1.shape[2]
    heads = width // HEAD
    wide = (8, ROWS, D)
    dma = pltpu.SemaphoreType.DMA
    tall = D // 256
    mine = ((hidden, COLS), (COLS, hidden), (width, COLS), (COLS, 3 * width))
    blocks = [(2, tall) + m for m in mine]
    if fused:
        outs = [
            sds((LAYERS, hidden, COLS), F32),
            sds((LAYERS, COLS, hidden), F32),
            sds((LAYERS, width, COLS), F32),
            sds((LAYERS, 3, COLS, width), F32),
        ]
        small = sds((4, 16, D), F32)
        regular = pltpu.SemaphoreType.REGULAR
        more = (
            [pltpu.VMEM((4,) + m, BF16) for m in mine]
            + [pltpu.VMEM((3,) + m, BF16) for m in mine]
            + [pltpu.VMEM(m, F32) for m in mine]
            + [pltpu.VMEM((16, D), F32), pltpu.VMEM((4, 16, D), F32), dma((2, 7))]
            + [dma((2, 2, 4, 2)), dma((2, 2, 4, 2)), dma((2, 2, 3))]
            + [regular((2, 2)), regular((2, 2, 4))]
        )
    else:
        outs = [sds((LAYERS,) + b, BF16) for b in blocks]
        small = sds((16, D), F32)
        more = [dma((2, 2, 4, 2))]
    kept_shapes = (
        (8, ROWS, 3 * width), (8, heads * ROWS, ROWS), (8, ROWS, width), wide,
        (8, ROWS, hidden), (8, ROWS, hidden), wide, (8, ROWS, hidden), (8, ROWS, 3 * width),
    )
    return pl.pallas_call(
        partial(backward_kernel, fused),
        out_shape=[sds((GROUPS, ROWS, D), F32), small] + outs,
        in_specs=[VM] * 3 + [HB] * 12,
        out_specs=[VM] * 2 + [HB] * 4,
        scratch_shapes=exchange_scratch()
        + [
            pltpu.VMEM((GROUPS, ROWS, D), F32),
            pltpu.VMEM((2, GROUPS, ROWS, D), F32),
            pltpu.VMEM((D, 3 * width), BF16),
            pltpu.VMEM((width, D), BF16),
            pltpu.VMEM((D, hidden), BF16),
            pltpu.VMEM((hidden, D), BF16),
        ]
        + [pltpu.VMEM(k, BF16) for k in kept_shapes]
        + [pltpu.VMEM((16, D), F32)]
        + [pltpu.VMEM(b, BF16) for b in blocks]
        + [dma((2, 9))]
        + more,
        compiler_params=params(2),
    )(cot, keep, gains, flow, wqkv, wout, w1, w2, *kept)


def to_groups(array, dtype):
    images = array.shape[0] // GROUPS
    rows = array.reshape(GROUPS, images * PATCHES, D)
    return jnp.pad(rows, ((0, 0), (0, ROWS - images * PATCHES), (0, 0))).astype(dtype)


def from_groups(array):
    return array[:, :LIVE].reshape(GROUPS * (LIVE // PATCHES), PATCHES, D)


def collect_weight(partial_grad, split_dim):
    return lax.psum_scatter(
        partial_grad, "dp", scatter_dimension=split_dim, tiled=True
    ).astype(F32)


def join_rows(blocks):
    return jnp.transpose(blocks, (1, 0, 2, 3)).reshape(D, -1)


def join_columns(blocks):
    return jnp.transpose(blocks, (2, 1, 0, 3)).reshape(blocks.shape[2], -1)


def local(
    patches,
    keep_index,
    kept_count,
    norm_gain,
    shifts,
    w_qkv,
    bias_qv,
    w_out,
    w_fc1,
    bias_fc1,
    w_fc2,
    cotangent,
):
    width = w_qkv.shape[-1]
    hidden = w_fc1.shape[-1]
    dp_size, ways = lax.axis_size("dp"), lax.axis_size("tensor")
    assert ways == 4
    per = kept_count.shape[0] // GROUPS
    slot_ids = jnp.arange(PATCHES, dtype=jnp.int32)
    counts = kept_count.reshape(GROUPS, per, 1).astype(F32)
    first = LIVE - ROWS + 16
    counts = jnp.broadcast_to(
        jnp.pad(counts, ((0, 0), (first, 16 - first - per), (0, 0))), (GROUPS, 16, 256)
    )
    places = keep_index.reshape(GROUPS, per, PATCHES) + PATCHES * jnp.arange(per)[:, None]
    places = places.reshape(GROUPS, 1, per * PATCHES)
    places = jnp.pad(places, ((0, 0), (0, 0), (0, ROWS - LIVE)), constant_values=-1)
    wqkv = jnp.transpose(w_qkv, (0, 2, 1, 3))
    flow, *kept = forward(
        to_groups(patches, BF16), places, counts, norm_gain, shifts, bias_qv, bias_fc1,
        wqkv, w_out, w_fc1, w_fc2,
    )
    own_mask = (slot_ids[None, :] < kept_count[:, None])[:, :, None]
    layer_out = from_groups(flow[2 * LAYERS]) * own_mask.astype(F32)
    fused = dp_size == 8 and hidden == D and 4 * width == D
    patch_grad, small, g_fc2, g_fc1, g_out, g_qkv = backward(
        fused, to_groups(cotangent * own_mask.astype(BF16), BF16), places, norm_gain, flow,
        wqkv, w_out, w_fc1, w_fc2, kept,
    )
    grad_patches = from_groups(patch_grad)
    if fused:
        grad_qkv, grad_out, grad_fc1, grad_fc2 = g_qkv, g_out, g_fc1, g_fc2
    else:
        grad_qkv, grad_out, grad_fc1, grad_fc2 = (
            jnp.stack([collect_weight(join(array[n]), split) for n in range(LAYERS)])
            for array, join, split in (
                (g_qkv, join_rows, 0),
                (g_out, join_columns, 1),
                (g_fc1, join_rows, 0),
                (g_fc2, join_columns, 1),
            )
        )
        grad_qkv = jnp.transpose(grad_qkv.reshape(LAYERS, -1, 3, width), (0, 2, 1, 3))
        small = lax.all_gather(lax.psum(small, "dp"), "tensor")
    grad_qkv = jnp.transpose(grad_qkv, (0, 2, 1, 3))
    summed = jnp.sum(small[:, :12], axis=0)
    grad_gain = summed[:4].reshape(LAYERS, 2, D)
    grad_shifts = summed[4:].reshape(LAYERS, 4, D)
    grad_bias_fc1 = jnp.transpose(small[:, 12:14], (1, 0, 2)).reshape(LAYERS, ways * hidden)
    quarters = small[:, 14, : 2 * LAYERS * width].reshape(ways, LAYERS, 2, width)
    grad_bias_qv = jnp.transpose(quarters, (1, 2, 0, 3)).reshape(LAYERS, 2, ways * width)
    return (
        layer_out,
        grad_patches,
        grad_gain,
        grad_shifts,
        grad_qkv,
        grad_bias_qv,
        grad_out,
        grad_fc1,
        grad_bias_fc1,
        grad_fc2,
    )


def solution(mesh):
    in_specs = (
        P(("dp", "tensor"), None, None),
        P(("dp", "tensor"), None),
        P(("dp", "tensor")),
        P(),
        P(),
        P(None, None, None, "tensor"),
        P(None, None, "tensor"),
        P(None, "tensor", None),
        P(None, None, "tensor"),
        P(None, "tensor"),
        P(None, "tensor", None),
        P(("dp", "tensor"), None, None),
    )
    out_specs = (
        P(("dp", "tensor"), None, None),
        P(("dp", "tensor"), None, None),
        P(),
        P(),
        P(None, "dp", None, "tensor"),
        P(),
        P(None, "tensor", "dp"),
        P(None, "dp", "tensor"),
        P(),
        P(None, "tensor", "dp"),
    )
    return jax.shard_map(local, mesh=mesh, in_specs=in_specs, out_specs=out_specs, check_vma=False)
```

time: 1420 us -> 371 us (0.26)
  waiting for transfers between devices: 1030 us -> 0 us
  Pallas kernels: 0 us -> 347 us
  matrix products: 164 us -> 0 us
  other arithmetic: 89.3 us -> 3.41 us
  local copies, waits for them, and re-layouts: 99.4 us -> 17.1 us
  between operations: 16.4 us -> 0.79 us
    reduce_scatter x12 -> x0, waiting for transfers between devices: 547 us -> none  [the longest x4 273 us: collect_weight(): lax.psum_scatter(partial_grad.astype(jnp.bfloat16), 'dp', scatter_dimensi...]
    pallas_call x0 -> x2, Pallas kernels: none -> 347 us  [the longest x1 226 us: backward(): pl.pallas_call(partial(backward_kernel, fused), out_shape=[sds((GROUPS, R...]
    unnamed x29 -> x0, waiting for transfers between devices: 203 us -> none
    dot_general x38 -> x0, matrix products: 164 us -> none  [the longest x2 22.6 us: local(): jnp.einsum('bsd,fd->bsf', grad_rows, w_fc2[layer_no], preferred_element_t...]
    all_gather x8 -> x0, waiting for transfers between devices: 155 us -> none  [the longest x4 96.1 us: spread(): lax.all_gather(rows, 'tensor', axis=0, tiled=True)]
    psum x1 -> x0, waiting for transfers between devices: 120 us -> none  [local(): lax.psum((jnp.stack(gain_terms), jnp.stack(shift_terms), qv_full, fc1_ful...]
    convert_element_type x13 -> x2, other arithmetic: 43.7 us -> 2.04 us  [the longest x1 1.32 us: local(): own_mask.astype(BF16)]
    reduce_sum x23 -> x1, other arithmetic: 38.1 us -> 0.02 us  [local(): summed = jnp.sum(small[:, :12], axis=0)]
  transfers between devices with their start and end apart: 25 -> 0, of which waited for: 24 -> 0; matrix products, arithmetic and copies ran while one was open for 10% -> 0% of each run, Pallas kernels for 0% -> 0%
where the time goes in v4:
time: 371 us; the launch traced here: 368 us
  Pallas kernels  347 us (94%)
  local copies, waits for them, and re-layouts  17.1 us (5%)
    pallas_call x1, Pallas kernels, backward(): pl.pallas_call(partial(backward_kernel, fused), out_shape=[sds((GROUPS, R...  226 us
    pallas_call x1, Pallas kernels, forward(): pl.pallas_call(forward_kernel, out_shape=(sds(steps, F32),) + tuple((sds(...  120 us

profile of v4, /device:TPU:0, one launch (start us, length us, event | category | flops | bytes accessed | tf_op | source)
XLA Modules:
  0.0 368.1 jit_solution(8931081528331183506)
XLA Ops:
  0.6 0.0 copy-start.5
  0.7 0.7 convert_element_type.35
  1.4 0.1 convert_element_type.36
  1.5 0.1 pad_bitcast_fusion
  1.5 0.1 add.27
  1.6 0.1 add.28
  1.7 0.8 reshape.143
  2.5 0.6 pad.16.keep
  3.1 1.3 fusion
  4.4 0.7 broadcast_in_dim.5.counts
  5.1 1.3 reshape.142
  6.3 0.9 pad.15.patches
  7.2 0.0 copy-done.5
  7.2 0.1 broadcast_multiply_fusion.1
  7.3 0.2 reshape.145
  7.5 0.9 pad.18.cot
  8.4 120.3 %shard_map.195 = (f32[5,2,160,1024]{3,2,1,0:T(8,128)}, bf16[2,8,160,1024]{3,2,1,0:T(8,128)(2,1)}, bf16[2,8,160,768]{3,2,1,0:T(8,128)(2,1)}, bf16[2,8,640,160]{3,...) custom-call(bf16[2,160,1024]{2,1,0:T(8,128)(2,1)} %pad.15.patches, ...), custom_call_target="tpu_custom_call" | custom-call | tf_op jit(solution)/shard_map/pallas_call | solution.py:359
  128.7 226.5 %shard_map.196 = (f32[2,160,1024]{2,1,0:T(8,128)}, f32[4,16,1024]{2,1,0:T(8,128)}, f32[2,1024,128]{2,1,0:T(8,128)}, f32[2,128,1024]{2,1,0:T(8,128)}, f32[2,256,128]{2,1,0:T(8,128)}, /*index=5*/f32[2,3,128,256]{3,2,1,0:T(8,128)}) custom-call(bf16[2,160,1024]{2,1,0:T(8,128)(2,1)} %pad.18.cot, s32[2,1,160]{2,1,0:T(1,128)} %pad.16.keep, f32[2,2,1024]{2,1,0:T(2,128)} %gains.3, ...), custom_call_target="tpu_custom_call" | custom-call | tf_op jit(solution)/shard_map/pallas_call | solution.py:897
  355.2 1.4 slice_bitcast_fusion
  356.6 0.0 copy-start
  356.6 0.0 copy-start.1
  356.6 0.0 copy-start.6
  356.6 1.8 copy-done.1
  358.4 0.1 slice.26
  358.5 0.0 copy-done
  358.5 0.0 copy-done.6
  358.6 0.1 slice_reduce_fusion.1
  358.6 0.6 copy.24
  359.3 0.6 slice.31
  359.9 0.0 slice-start
  359.9 0.6 reshape.148
  360.6 0.6 reshape.147
  361.2 1.2 reshape.146
  362.4 0.0 slice-done
  362.4 0.0 copy-start.8
  362.4 0.1 reshape.144
  362.6 0.5 copy-done.8
  363.1 0.0 copy-start.4
  363.1 1.2 broadcast_multiply_fusion
  364.3 0.0 copy-done.4
  364.4 0.0 copy-start.7
  364.4 0.0 copy-start.3
  364.4 0.9 copy.29
  365.3 0.2 copy-done.7
  365.5 0.0 copy-start.2
  365.5 0.7 copy.30
  366.2 0.0 copy-done.3
  366.2 1.0 copy.31
  367.1 0.0 copy-done.2
  367.1 1.0 copy.32
  (6 shorter events, 0.1 us)
Async XLA Ops:
  0.6 6.6 %copy-start.5 = (bf16[6,50,1024]{2,1,0:T(8,128)(2,1)S(1)}, bf16[6,50,1024]{2,1,0:T(8,128)(2,1)}, u32[]{:S(2)}) copy-start(bf16[6,50,1024]{2,1,0:T(8,128)(2,1)} %param.23) | copy-start | bytes 1843204
  356.6 1.9 copy-start
  356.6 1.8 copy-start.1
  356.6 1.9 copy-start.6
  359.9 2.5 slice-start
  362.4 0.7 copy-start.8
  363.1 1.3 copy-start.4
  364.4 1.1 copy-start.7
  364.4 1.8 copy-start.3
  365.5 1.7 copy-start.2

commit v5 on v4

--- a/solution.py
+++ b/solution.py
@@ -380,6 +380,8 @@
 
 
 class Scatter:
+    order = (3, 1, 2, 0)
+
     def __init__(self, made, halves, arrivals, totals, outs, sems):
         self.made, self.halves, self.arrivals = made, halves, arrivals
         self.totals, self.outs = totals, outs
@@ -387,76 +389,92 @@
         me = lax.axis_index("dp")
         self.x, self.z = me % 2, me // 2
         self.across = me + 1 - 2 * self.x
-
-    def peer(self, k):
-        return 2 * ((self.z + k) % 4) + self.x
+        self.near = self.z + 1 - 2 * (self.z % 2)
+        self.far = (self.z + 2) % 4
+
+    def device(self, z):
+        return 2 * z + self.x
 
     def shard(self, k):
-        return (self.z + k) % 4
-
-    def over_x(self, kind, part, k):
-        n = self.shard(k)
+        return (self.z, self.near, self.far, (self.near + 2) % 4)[k]
+
+    def number(self, j):
+        third = (self.near + 2) % 4
+        return jnp.where(
+            j < 2, jnp.where(j == 0, third, self.near), jnp.where(j == 2, self.far, self.z)
+        )
+
+    def over_x(self, kind, part, j):
+        n = self.number(j)
         return to_peer(
             "dp",
             self.made[kind][part].at[1 - self.x, n],
             self.halves[kind][part].at[n],
-            self.x_sem.at[kind, part, k, 0],
-            self.x_sem.at[kind, part, k, 1],
+            self.x_sem.at[kind, part, j, 0],
+            self.x_sem.at[kind, part, j, 1],
             self.across,
         )
 
     def over_z(self, kind, part, k):
+        there, slot = {1: (self.near, 0), 3: (self.near, 1), 2: (self.far, 2)}[k]
         return to_peer(
             "dp",
             self.made[kind][part].at[self.x, self.shard(k)],
-            self.arrivals[kind][part].at[k - 1],
-            self.z_sem.at[kind, part, k, 0],
-            self.z_sem.at[kind, part, k, 1],
-            self.peer(k),
+            self.arrivals[kind][part].at[slot],
+            self.z_sem.at[kind, part, slot, 0],
+            self.z_sem.at[kind, part, slot, 1],
+            self.device(there),
         )
 
     def ready(self, s, part):
         if s >= 2:
-            for k in range(4):
-                self.over_x(s % 2, part, k).wait_send()
-                if k:
-                    self.over_z(s % 2, part, k).wait_send()
-
-    def send(self, s, part, k):
+            for j in range(4):
+                self.over_x(s % 2, part, j).wait_send()
+            for k in (1, 2, 3):
+                self.over_z(s % 2, part, k).wait_send()
+
+    def send(self, s, part, j):
         if s >= 2:
             pl.semaphore_wait(self.x_free.at[s % 2, part], 1)
-        self.over_x(s % 2, part, k).start()
-
-    def fold(self, s, part, k):
+        self.over_x(s % 2, part, j).start()
+
+    def signal(self, sem, device):
+        pl.semaphore_signal(
+            sem, inc=1, device_id={"dp": device}, device_id_type=pl.DeviceIdType.MESH
+        )
+
+    def sum_rows(self, out, terms):
+        def one(i, _):
+            at = pl.ds(pl.multiple_of(i * COLS, COLS), COLS)
+            value = terms[0][at, :].astype(F32)
+            for term in terms[1:]:
+                value = value + term[at, :].astype(F32)
+            out[at, :] = value.astype(out.dtype)
+            return 0
+
+        lax.fori_loop(0, out.shape[0] // COLS, one, 0)
+
+    def take(self, s, part, k):
         kind = s % 2
-        made, half = self.made[kind][part], self.halves[kind][part]
-        total = self.totals[kind][part]
-        n = self.shard(k)
-        self.over_x(kind, part, k).wait_recv()
-        last = isinstance(k, int) and k == 0
-        if last and s >= 2:
-            self.store(s - 2, part, wait=True)
-
-        def add(i, _):
-            at = pl.ds(pl.multiple_of(i * COLS, COLS), COLS)
-            both = made[self.x, n, at, :].astype(F32) + half[n, at, :].astype(F32)
-            if last:
-                total[at, :] = both
-            else:
-                made[self.x, n, at, :] = both.astype(BF16)
-            return 0
-
-        lax.fori_loop(0, half.shape[1] // COLS, add, 0)
+        mine = self.made[kind][part].at[self.x, self.shard(k)]
+        terms = [mine, self.halves[kind][part].at[self.shard(k)]]
+        self.over_x(kind, part, self.order.index(k)).wait_recv()
+        if k == 2:
+            self.over_z(kind, part, 3).wait_recv()
+            terms.append(self.arrivals[kind][part].at[1])
+        if k == 0:
+            if s >= 2:
+                self.store(s - 2, part, wait=True)
+            mine = self.totals[kind][part]
+        self.sum_rows(mine, terms)
         if s < 2:
-            pl.semaphore_signal(
-                self.x_free.at[kind, part],
-                inc=1,
-                device_id={"dp": self.across},
-                device_id_type=pl.DeviceIdType.MESH,
-            )
-        if not last:
+            self.signal(self.x_free.at[kind, part], self.across)
+            if k == 2:
+                self.signal(self.z_free.at[kind, part, 1], self.device(self.near))
+        if k:
             if s >= 2:
-                pl.semaphore_wait(self.z_free.at[kind, part, k], 1)
+                slot = {1: 0, 3: 1, 2: 2}[k]
+                pl.semaphore_wait(self.z_free.at[kind, part, slot], 1)
             self.over_z(kind, part, k).start()
 
     def store(self, s, part, wait=False):
@@ -477,27 +495,13 @@
     def finish(self, s, part):
         kind = s % 2
         total, arrivals = self.totals[kind][part], self.arrivals[kind][part]
-        for k in range(1, 4):
-            self.over_z(kind, part, k).wait_recv()
-
-        def add(i, _):
-            at = pl.ds(pl.multiple_of(i * COLS, COLS), COLS)
-            value = total[at, :]
-            for k in range(3):
-                value = value + arrivals[k, at, :].astype(F32)
-            total[at, :] = value
-            return 0
-
-        lax.fori_loop(0, total.shape[0] // COLS, add, 0)
+        self.over_z(kind, part, 1).wait_recv()
+        self.over_z(kind, part, 2).wait_recv()
+        self.sum_rows(total, [total, arrivals.at[0], arrivals.at[2]])
         self.store(s, part)
         if s < 2:
-            for k in range(1, 4):
-                pl.semaphore_signal(
-                    self.z_free.at[kind, part, k],
-                    inc=1,
-                    device_id={"dp": self.peer(4 - k)},
-                    device_id_type=pl.DeviceIdType.MESH,
-                )
+            self.signal(self.z_free.at[kind, part, 0], self.device(self.near))
+            self.signal(self.z_free.at[kind, part, 2], self.device(self.far))
 
     def end(self):
         for s in (2, 3):
@@ -517,32 +521,41 @@
     )
 
 
-def sum_small(lines, arrived, over_z, out, sem, sc, mine):
-    across = to_peer("dp", lines, arrived, sem.at[0, 0], sem.at[1, 0], sc.across)
-    across.start()
-    across.wait_recv()
-    across.wait_send()
-    over_z[sc.z] = lines[...] + arrived[...]
-
-    def along(k):
-        part = over_z.at[sc.z]
-        return to_peer("dp", part, part, sem.at[0, k], sem.at[1, k], sc.peer(k))
-
-    for k in range(1, 4):
-        along(k).start()
-    for k in range(1, 4):
-        along(k).wait_recv()
-    out[mine] = over_z[0] + over_z[1] + over_z[2] + over_z[3]
-
-    def around(k):
-        part = out.at[mine]
-        return to_peer("tensor", part, part, sem.at[0, 3 + k], sem.at[1, 3 + k], (mine + k) % 4)
-
-    for k in range(1, 4):
-        around(k).start()
-    for k in range(1, 4):
-        along(k).wait_send()
-        around(k).wait()
+class SmallSum:
+    def __init__(self, lines, arrived, over_z, out, sem, sc, mine):
+        self.lines, self.arrived, self.over_z, self.out = lines, arrived, over_z, out
+        self.sem, self.sc, self.mine = sem, sc, mine
+
+    def across(self):
+        s = self.sem
+        return to_peer("dp", self.lines, self.arrived, s.at[0, 0], s.at[1, 0], self.sc.across)
+
+    def along(self, k):
+        part, s = self.over_z.at[self.sc.z], self.sem
+        return to_peer("dp", part, part, s.at[0, k], s.at[1, k], self.sc.device((self.sc.z + k) % 4))
+
+    def around(self, k):
+        part, s = self.out.at[self.mine], self.sem
+        peer = (self.mine + k) % 4
+        return to_peer("tensor", part, part, s.at[0, 3 + k], s.at[1, 3 + k], peer)
+
+    def second(self):
+        self.across().wait()
+        self.over_z[self.sc.z] = self.lines[...] + self.arrived[...]
+        for k in range(1, 4):
+            self.along(k).start()
+
+    def third(self):
+        for k in range(1, 4):
+            self.along(k).wait()
+        z = self.over_z
+        self.out[self.mine] = z[0] + z[1] + z[2] + z[3]
+        for k in range(1, 4):
+            self.around(k).start()
+
+    def last(self):
+        for k in range(1, 4):
+            self.around(k).wait()
 
 
 def backward_kernel(
@@ -566,9 +579,8 @@
         )
         small_in, small_z, small_sem = rest[12:15]
         sc = Scatter(made, halves, arrivals, totals, outs, rest[15:20])
-        z = sc.z
     else:
-        sc, z = None, 0
+        sc = None
         save_sem = rest[0]
 
     def layer(s):
@@ -607,7 +619,7 @@
     peers = [{"tensor": ex.mate}, {"tensor": ex.far}]
     if fused:
         peers += [{"tensor": ex.diag}, {"dp": sc.across}]
-        peers += [{"dp": sc.peer(k)} for k in range(1, 4)]
+        peers += [{"dp": sc.device((sc.z + k) % 4)} for k in range(1, 4)]
     for peer in peers:
         pl.semaphore_signal(barrier, inc=1, device_id=peer, device_id_type=pl.DeviceIdType.MESH)
     pl.semaphore_wait(barrier, len(peers))
@@ -646,19 +658,17 @@
         ex.share(g)
 
     def spill(s, part, k):
-        m = (z + k) % 4
         return [
             pltpu.make_async_copy(
-                made[s % 2][part].at[half, m],
-                outs[s % 2][part].at[layer(s), half, m],
+                made[s % 2][part].at[half, k],
+                outs[s % 2][part].at[layer(s), half, k],
                 save_sem.at[s % 2, part, k, half],
             )
             for half in range(2)
         ]
 
     def column_block(s, j):
-        k = (j + 1) % 4
-        n = (z + k) % 4
+        n = sc.number(j) if fused else j
         at = pl.ds(pl.multiple_of(n * 256, 256), 256)
         some = gath[s % 2, :, :, at].reshape(flat, 256)
         left = (act, att)[s % 2]
@@ -667,14 +677,14 @@
         out[0, n] = wide[:, :COLS]
         out[1, n] = wide[:, COLS:]
         if fused:
-            sc.send(s, 0, k)
+            if s < stages - 1:
+                sc.send(s, 0, j)
         else:
-            for copy in spill(s, 0, k):
+            for copy in spill(s, 0, j):
                 copy.start()
 
     def row_block(s, j):
-        k = (j + 1) % 4
-        n = (z + k) % 4
+        n = sc.number(j) if fused else j
         at = pl.ds(pl.multiple_of(n * 256, 256), 256)
         left, right = ((norm_m, pre), (norm_a, triple))[s % 2]
         some = left[:, :, at].reshape(flat, 256)
@@ -683,9 +693,10 @@
         out[0, n] = tall[:COLS]
         out[1, n] = tall[COLS:]
         if fused:
-            sc.send(s, 1, k)
+            if s < stages - 1:
+                sc.send(s, 1, j)
         else:
-            for copy in spill(s, 1, k):
+            for copy in spill(s, 1, j):
                 copy.start()
 
     def settle(s, part):
@@ -723,37 +734,30 @@
             lines[14:15, at : at + width] = sums[:, :width]
             lines[14:15, at + width : at + 2 * width] = sums[:, 2 * width :]
 
-    def folds(s, part, first, count):
-        if not fused:
-            return
-        away = min(first + count, 4) - first
-
-        def one(k, _):
-            sc.fold(s, part, k)
-            return 0
-
-        if away > 0:
-            lax.fori_loop(first, first + away, one, 0)
-        if first + count > 4:
-            sc.fold(s, part, 0)
-
-    def finish(s):
-        if fused:
-            for part in range(2):
-                sc.finish(s, part)
+    def take(*work):
+        def run():
+            if fused:
+                for s, part, k in work:
+                    if k == 4:
+                        sc.finish(s, part)
+                    else:
+                        sc.take(s, part, k)
+
+        return run
 
     lines[15:16] = jnp.zeros((1, D), F32)
     plan = {
-        (1, 4): lambda: folds(0, 0, 1, 1),
-        (1, 6): lambda: folds(0, 0, 2, 2),
-        (1, 8): lambda: folds(0, 0, 4, 1),
-        (2, 2): lambda: folds(0, 1, 1, 1),
-        (2, 4): lambda: folds(0, 1, 2, 1),
-        (2, 6): lambda: folds(0, 1, 3, 2),
-        (3, 2): lambda: folds(1, 0, 1, 4),
-        (3, 4): lambda: folds(1, 1, 1, 2),
-        (3, 6): lambda: folds(1, 1, 3, 2),
-        (3, 8): lambda: finish(0),
+        (1, 4): take((0, 0, 3)),
+        (1, 6): take((0, 0, 1)),
+        (1, 8): take((0, 0, 2)),
+        (2, 2): take((0, 0, 0), (0, 1, 3)),
+        (2, 4): take((0, 1, 1)),
+        (2, 6): take((0, 1, 2)),
+        (2, 8): take((0, 1, 0), (0, 0, 4), (1, 0, 3), (1, 0, 1)),
+        (3, 2): take((1, 0, 2), (1, 0, 0), (1, 1, 3), (1, 1, 1)),
+        (3, 4): take((0, 1, 4), (1, 1, 2)),
+        (3, 6): take((1, 0, 4), (1, 1, 0)),
+        (3, 8): take((2, 0, 3), (2, 0, 1)),
     }
 
     for s in range(stages):
@@ -837,21 +841,22 @@
     settle(last, 1)
     some_rows(last, 0, 4)
     bias_sums(last)
+    take((2, 0, 2), (1, 1, 4))()
     for g in range(GROUPS):
         produce(stages, g)
-    ex.end()
     if fused:
-        folds(2, 0, 1, 2)
-        sum_small(lines, small_in, small_z, small_out, small_sem, sc, ex.me)
-        finish(1)
-        folds(2, 0, 3, 2)
-        folds(2, 1, 1, 4)
-        folds(3, 0, 1, 4)
-        sc.finish(2, 0)
-        folds(3, 1, 1, 4)
-        sc.finish(2, 1)
-        finish(3)
+        tiny = SmallSum(lines, small_in, small_z, small_out, small_sem, sc, ex.me)
+        tiny.across().start()
+        for side in range(2):
+            for j in range(4):
+                sc.send(last, side, j)
+        take((2, 0, 0), (2, 1, 3), (2, 1, 1), (2, 0, 4), (2, 1, 2), (2, 1, 0))()
+        tiny.second()
+        take((3, 0, 3), (3, 0, 1), (3, 0, 2), (3, 0, 0))()
+        tiny.third()
+        take((2, 1, 4), (3, 1, 3), (3, 1, 1), (3, 1, 2), (3, 0, 4), (3, 1, 0), (3, 1, 4))()
         sc.end()
+        tiny.last()
     else:
         small_out[...] = lines[...]
         for s in (2, 3):
@@ -859,6 +864,7 @@
                 for k in range(4):
                     for copy in spill(s, side, k):
                         copy.wait()
+    ex.end()
 
 
 def backward(fused, cot, keep, gains, flow, wqkv, wout, w1, w2, kept):
@@ -883,8 +889,8 @@
             + [pltpu.VMEM((3,) + m, BF16) for m in mine]
             + [pltpu.VMEM(m, F32) for m in mine]
             + [pltpu.VMEM((16, D), F32), pltpu.VMEM((4, 16, D), F32), dma((2, 7))]
-            + [dma((2, 2, 4, 2)), dma((2, 2, 4, 2)), dma((2, 2, 3))]
-            + [regular((2, 2)), regular((2, 2, 4))]
+            + [dma((2, 2, 4, 2)), dma((2, 2, 3, 2)), dma((2, 2, 3))]
+            + [regular((2, 2)), regular((2, 2, 3))]
         )
     else:
         outs = [sds((LAYERS,) + b, BF16) for b in blocks]

time: 371 us -> 315 us (0.85)
  Pallas kernels: 347 us -> 293 us
    pallas_call x1, Pallas kernels: 226 us -> 173 us  [backward(): pl.pallas_call(partial(backward_kernel, fused), out_shape=[sds((GROUPS, R...]
where the time goes in v5:
time: 315 us; the launch traced here: 314 us
  Pallas kernels  293 us (93%)
  local copies, waits for them, and re-layouts  17.1 us (5%)
  other arithmetic  3.41 us (1%)
    pallas_call x1, Pallas kernels, backward(): pl.pallas_call(partial(backward_kernel, fused), out_shape=[sds((GROUPS, R...  173 us
    pallas_call x1, Pallas kernels, forward(): pl.pallas_call(forward_kernel, out_shape=(sds(steps, F32),) + tuple((sds(...  120 us

profile of v5, /device:TPU:0, one launch (start us, length us, event | category | flops | bytes accessed | tf_op | source)
XLA Modules:
  0.0 314.3 jit_solution(16231269871062226923)
XLA Ops:
  0.6 0.0 copy-start.5
  0.7 0.7 convert_element_type.35
  1.4 0.1 convert_element_type.36
  1.5 0.1 pad_bitcast_fusion
  1.5 0.1 add.27
  1.6 0.1 add.28
  1.7 0.8 reshape.143
  2.5 0.6 pad.16.keep
  3.1 1.3 fusion
  4.4 0.7 broadcast_in_dim.5.counts
  5.1 1.3 reshape.142
  6.3 0.9 pad.15.patches
  7.2 0.0 copy-done.5
  7.2 0.1 broadcast_multiply_fusion.1
  7.3 0.2 reshape.145
  7.5 0.9 pad.18.cot
  8.4 120.3 %shard_map.195 = (f32[5,2,160,1024]{3,2,1,0:T(8,128)}, bf16[2,8,160,1024]{3,2,1,0:T(8,128)(2,1)}, bf16[2,8,160,768]{3,2,1,0:T(8,128)(2,1)}, bf16[2,8,640,160]{3,...) custom-call(bf16[2,160,1024]{2,1,0:T(8,128)(2,1)} %pad.15.patches, ...), custom_call_target="tpu_custom_call" | custom-call | tf_op jit(solution)/shard_map/pallas_call | solution.py:359
  128.7 172.7 %shard_map.196 = (f32[2,160,1024]{2,1,0:T(8,128)}, f32[4,16,1024]{2,1,0:T(8,128)}, f32[2,1024,128]{2,1,0:T(8,128)}, f32[2,128,1024]{2,1,0:T(8,128)}, f32[2,256,128]{2,1,0:T(8,128)}, /*index=5*/f32[2,3,128,256]{3,2,1,0:T(8,128)}) custom-call(bf16[2,160,1024]{2,1,0:T(8,128)(2,1)} %pad.18.cot, s32[2,1,160]{2,1,0:T(1,128)} %pad.16.keep, f32[2,2,1024]{2,1,0:T(2,128)} %gains.3, ...), custom_call_target="tpu_custom_call" | custom-call | tf_op jit(solution)/shard_map/pallas_call | solution.py:903
  301.4 1.4 slice_bitcast_fusion
  302.8 0.0 copy-start
  302.8 0.0 copy-start.1
  302.8 0.0 copy-start.6
  302.9 1.8 copy-done.1
  304.6 0.1 slice.26
  304.8 0.0 copy-done
  304.8 0.0 copy-done.6
  304.8 0.1 slice_reduce_fusion.1
  304.9 0.6 copy.24
  305.5 0.6 slice.31
  306.1 0.0 slice-start
  306.2 0.6 reshape.148
  306.8 0.6 reshape.147
  307.4 1.2 reshape.146
  308.6 0.0 slice-done
  308.6 0.0 copy-start.8
  308.6 0.1 reshape.144
  308.8 0.5 copy-done.8
  309.3 0.0 copy-start.4
  309.3 1.2 broadcast_multiply_fusion
  310.6 0.0 copy-done.4
  310.6 0.0 copy-start.7
  310.6 0.0 copy-start.3
  310.6 0.9 copy.29
  311.5 0.2 copy-done.7
  311.7 0.0 copy-start.2
  311.7 0.7 copy.30
  312.4 0.0 copy-done.3
  312.4 1.0 copy.31
  313.4 0.0 copy-done.2
  313.4 1.0 copy.32
  (6 shorter events, 0.1 us)
Async XLA Ops:
  0.6 6.6 %copy-start.5 = (bf16[6,50,1024]{2,1,0:T(8,128)(2,1)S(1)}, bf16[6,50,1024]{2,1,0:T(8,128)(2,1)}, u32[]{:S(2)}) copy-start(bf16[6,50,1024]{2,1,0:T(8,128)(2,1)} %param.23) | copy-start | bytes 1843204
  302.8 1.9 copy-start
  302.8 1.8 copy-start.1
  302.8 1.9 copy-start.6
  306.1 2.5 slice-start
  308.6 0.7 copy-start.8
  309.3 1.3 copy-start.4
  310.6 1.1 copy-start.7
  310.6 1.8 copy-start.3
  311.7 1.7 copy-start.2

commit v6 on v5

--- a/solution.py
+++ b/solution.py
@@ -112,6 +112,9 @@
         )
         return GROUPS * owner + (i // 2) % 2
 
+    def place(self, i):
+        return jnp.where(i % 2 == 0, i // 2, 4)
+
     def before(self, i):
         for g in range(GROUPS):
 
@@ -135,23 +138,23 @@
             @pl.when(i == 1 + 2 * g)
             def _():
                 self.again(3, g)
-                self.out_po[g] = self.part[1 + 2 * g].astype(BF16)
+                self.out_po[g] = self.part[4].astype(BF16)
                 self.send(3, g)
 
             @pl.when(i == 5 + 2 * g)
             def _():
                 self.again(4, g)
-                self.out_pd[g] = self.part[5 + 2 * g].astype(BF16)
+                self.out_pd[g] = self.part[4].astype(BF16)
                 self.send(4, g)
                 self.copy(4, g).wait_recv()
                 self.again(5, g)
-                self.out_y[g] = (self.part[4 + 2 * g] + self.in_pd[g].astype(F32)).astype(BF16)
+                self.out_y[g] = (self.part[2 + g] + self.in_pd[g].astype(F32)).astype(BF16)
                 self.send(5, g)
 
     def total(self, g):
         self.copy(3, g).wait_recv()
         self.copy(5, g).wait_recv()
-        return self.part[2 * g] + self.in_po[g].astype(F32) + self.in_y[g].astype(F32)
+        return self.part[g] + self.in_po[g].astype(F32) + self.in_y[g].astype(F32)
 
     def end(self):
         for g in range(GROUPS):
@@ -162,13 +165,23 @@
 def exchange_scratch():
     return [
         pltpu.VMEM((2, 8, ROWS, D), BF16),
-        pltpu.VMEM((8, ROWS, D), F32),
+        pltpu.VMEM((5, ROWS, D), F32),
     ] + [pltpu.VMEM((GROUPS, ROWS, D), BF16)] * 6 + [pltpu.SemaphoreType.DMA((2, 6, GROUPS))]
 
 
-def picker(keep, g):
-    patch = lax.broadcasted_iota(jnp.int32, (ROWS, ROWS), 0)
-    return (keep[g] == patch).astype(F32).astype(BF16)
+def picker(keep, image):
+    patch = lax.broadcasted_iota(jnp.int32, (PATCHES, PATCHES), 0)
+    return (keep[image : image + 1] == patch).astype(F32).astype(BF16)
+
+
+def images_of(g):
+    per = LIVE // PATCHES
+    return [(g * per + m, m * PATCHES) for m in range(per)]
+
+
+def live_rows(count, image):
+    row = lax.broadcasted_iota(jnp.int32, (PATCHES, D), 0)
+    return row < count[image]
 
 
 def attend(x, q_bias, v_bias, wqkv, wout, counts, keep_parts):
@@ -205,134 +218,6 @@
     return cdf, pdf
 
 
-def forward_kernel(
-    patches, keep, counts, gains, shifts, bias_qv, bias_fc1, wqkv_h, wout_h, w1_h, w2_h,
-    flow_h, gath_h, qkv_h, prob_h, att_h, gmlp_h, act_h, slope_h,
-    gath, part, out_po, out_pd, out_y, in_po, in_pd, in_y, ex_sem,
-    flow, wqkv, wout, w1, w2, qkv, prob, att, act, slope, load_sem, save_sem, flow_sem,
-):
-    ex = Exchange(gath, part, (out_po, out_pd, out_y, in_po, in_pd, in_y), ex_sem)
-    width, hidden = wout.shape[1], w1.shape[2]
-    stages = 2 * LAYERS
-    loads = []
-    for n in range(LAYERS):
-        pieces = [
-            (wqkv_h.at[n, c], wqkv.at[n, :, pl.ds(c * width, width)]) for c in range(3)
-        ] + [(wout_h.at[n], wout.at[n])]
-        loads.append([pltpu.make_async_copy(*p, load_sem.at[6 * n + m]) for m, p in enumerate(pieces)])
-        pieces = [(w1_h.at[n], w1.at[n]), (w2_h.at[n], w2.at[n])]
-        loads.append(
-            [pltpu.make_async_copy(*p, load_sem.at[6 * n + 4 + m]) for m, p in enumerate(pieces)]
-        )
-    for group in loads:
-        for copy in group:
-            copy.start()
-    ex.barrier()
-
-    def save_flow(s, g):
-        return pltpu.make_async_copy(flow.at[s, g], flow_h.at[s, g], flow_sem.at[s, g])
-
-    def produce(s, g):
-        n = s // 2
-        if s == 0:
-            value = dot(picker(keep, g), patches[g], 0, 0)
-        else:
-            before = (s - 1) // 2
-            shift = shifts[before, 2 + (s - 1) % 2].reshape(1, D)
-            value = flow[s - 1, g] + ex_last.total(g) + shift
-        flow[s, g] = value
-        save_flow(s, g).start()
-        if s == stages:
-            return
-        unit, _ = norm_parts(value)
-        gain, shift = gains[n, s % 2].reshape(1, D), shifts[n, s % 2].reshape(1, D)
-        own = ex.own(g)
-        gath[s % 2, own] = (unit * gain + shift).astype(BF16)
-        tail = gath[s % 2, own, ROWS - 16 : ROWS, 0:256].astype(F32)
-        row = lax.broadcasted_iota(jnp.int32, (16, 256), 0)
-        tail = jnp.where(row >= LIVE - ROWS + 16, counts[g], tail)
-        gath[s % 2, own, ROWS - 16 : ROWS, 0:256] = tail.astype(BF16)
-        ex.share(g)
-
-    def saves(s, slot):
-        n = s // 2
-        if s % 2 == 0:
-            pairs = ((gath.at[0], gath_h), (qkv, qkv_h), (prob, prob_h), (att, att_h))
-        else:
-            pairs = ((gath.at[1], gmlp_h), (act, act_h), (slope, slope_h))
-        return [
-            pltpu.make_async_copy(a.at[slot], b.at[n, slot], save_sem.at[m, slot])
-            for m, (a, b) in enumerate(pairs)
-        ]
-
-    def drain(s):
-        def one(slot, _):
-            for copy in saves(s, slot):
-                copy.wait()
-            return 0
-
-        lax.fori_loop(0, 8, one, 0)
-
-    ex_last = ex
-    for s in range(stages):
-        n = s // 2
-        ex.stage = s
-        produce(s, 0)
-        if s == 0:
-            produce(s, 1)
-        else:
-            drain(s - 1)
-        for copy in loads[s]:
-            copy.wait()
-
-        def step(i, _, s=s, n=n):
-            if s:
-
-                @pl.when(i == 2)
-                def _():
-                    produce(s, 1)
-
-            ex.before(i)
-            slot = ex.slot(i)
-            x = gath[s % 2, slot]
-            if s % 2 == 0:
-
-                def keep_parts(kind, *values):
-                    if kind == 0:
-                        for c, value in enumerate(values):
-                            qkv[slot, :, c * width : (c + 1) * width] = value
-                    else:
-                        prob[slot, (kind - 1) * ROWS : kind * ROWS] = values[0]
-
-                tail = gath[0, slot, ROWS - 16 : ROWS, 0:256][:, 0:ROWS].astype(F32)
-                mixed = attend(
-                    x, bias_qv[n, 0:1], bias_qv[n, 1:2], wqkv.at[n], wout.at[n], tail, keep_parts
-                )
-                att[slot] = mixed
-                part[i] = dot(mixed, wout[n])
-            else:
-                for block in range(hidden // 256):
-                    at = slice(block * 256, block * 256 + 256)
-                    pre = dot(x, w1[n, :, at]) + bias_fc1[n : n + 1, at]
-                    cdf, pdf = erf_parts(pre)
-                    act[slot, :, at] = (pre * cdf).astype(BF16)
-                    slope[slot, :, at] = (cdf + pre * pdf).astype(BF16)
-                part[i] = dot(act[slot], w2[n])
-            for copy in saves(s, slot):
-                copy.start()
-            ex.after(i)
-            return 0
-
-        lax.fori_loop(0, 8, step, 0)
-    for g in range(GROUPS):
-        produce(stages, g)
-    drain(stages - 1)
-    ex.end()
-    for s in range(stages + 1):
-        for g in range(GROUPS):
-            save_flow(s, g).wait()
-
-
 VM = pl.BlockSpec(memory_space=pltpu.VMEM)
 HB = pl.BlockSpec(memory_space=pl.ANY)
 
@@ -345,34 +230,6 @@
     return pltpu.CompilerParams(
         collective_id=n, has_side_effects=True, vmem_limit_bytes=67043328
     )
-
-
-def forward(patches, keep, counts, gains, shifts, bias_qv, bias_fc1, wqkv, wout, w1, w2):
-    width, hidden = wout.shape[1], w1.shape[2]
-    heads = width // HEAD
-    wide = (8, ROWS, D)
-    inner = ((8, ROWS, 3 * width), (8, heads * ROWS, ROWS), (8, ROWS, width))
-    mlp = ((8, ROWS, hidden), (8, ROWS, hidden))
-    kept = (wide,) + inner + (wide,) + mlp
-    steps = (2 * LAYERS + 1, GROUPS, ROWS, D)
-    dma = pltpu.SemaphoreType.DMA
-    return pl.pallas_call(
-        forward_kernel,
-        out_shape=(sds(steps, F32),) + tuple(sds((LAYERS,) + k, BF16) for k in kept),
-        in_specs=[VM] * 7 + [HB] * 4,
-        out_specs=(HB,) * 8,
-        scratch_shapes=exchange_scratch()
-        + [
-            pltpu.VMEM(steps, F32),
-            pltpu.VMEM((LAYERS, D, 3 * width), BF16),
-            pltpu.VMEM((LAYERS, width, D), BF16),
-            pltpu.VMEM((LAYERS, D, hidden), BF16),
-            pltpu.VMEM((LAYERS, hidden, D), BF16),
-        ]
-        + [pltpu.VMEM(k, BF16) for k in inner + mlp]
-        + [dma((6 * LAYERS,)), dma((4, 8)), dma((2 * LAYERS + 1, GROUPS))],
-        compiler_params=params(1),
-    )(patches, keep, counts, gains, shifts, bias_qv, bias_fc1, wqkv, wout, w1, w2)
 
 
 def column_sums(values):
@@ -558,14 +415,15 @@
             self.around(k).wait()
 
 
-def backward_kernel(
+def step_kernel(
     fused,
-    cot, keep, gains, flow_h, wqkv_h, wout_h, w1_h, w2_h,
-    gath_h, qkv_h, prob_h, att_h, gmlp_h, act_h, slope_h,
-    patch_grad, small_out, o_fc2, o_fc1, o_out, o_qkv,
+    count, patches, cot, keep, gains, shifts, bias_qv, bias_fc1, wqkv_h, wout_h, w1_h, w2_h,
+    layer_h, patch_h, small_out, o_fc2, o_fc1, o_out, o_qkv,
+    flow_h, gath_h, qkv_h, prob_h, att_h, gmlp_h, act_h, slope_h,
     gath, part, out_po, out_pd, out_y, in_po, in_pd, in_y, ex_sem,
-    gradient, source, wqkv, wout, w1, w2, qkv, prob, att, norm_a, act, slope, norm_m,
-    pre, triple, lines, cols_m, rows_m, cols_a, rows_a, load_sem, *rest,
+    gradient, source, final, wqkv, wout, w1, w2,
+    qkv, prob, att, norm_a, act, slope, norm_m,
+    pre, triple, lines, cols_m, rows_m, cols_a, rows_a, load_sem, keep_sem, flow_sem, *rest,
 ):
     ex = Exchange(gath, part, (out_po, out_pd, out_y, in_po, in_pd, in_y), ex_sem)
     width, hidden = wout.shape[0], w1.shape[1]
@@ -588,32 +446,46 @@
 
     def loads(s):
         n = layer(s)
+        if s < 2:
+            return []
         if s % 2 == 0:
             pairs = (
                 (w2_h.at[n], w2),
-                (slope_h.at[n], slope),
+                (slope_h, slope),
                 (w1_h.at[n], w1),
-                (act_h.at[n], act),
-                (gmlp_h.at[n], norm_m),
-                (flow_h.at[2 * n + 1], source.at[0]),
+                (act_h, act),
+                (gmlp_h, norm_m),
+                (flow_h.at[1], source.at[0]),
             )
         else:
             pairs = tuple(
                 (wqkv_h.at[n, c], wqkv.at[:, pl.ds(c * width, width)]) for c in range(3)
             ) + (
                 (wout_h.at[n], wout),
-                (qkv_h.at[n], qkv),
-                (prob_h.at[n], prob),
-                (att_h.at[n], att),
-                (gath_h.at[n], norm_a),
-                (flow_h.at[2 * n], source.at[1]),
+                (qkv_h, qkv),
+                (prob_h, prob),
+                (att_h, att),
+                (gath_h, norm_a),
+                (flow_h.at[0], source.at[1]),
             )
         return [
             pltpu.make_async_copy(*pair, load_sem.at[s % 2, m]) for m, pair in enumerate(pairs)
         ]
 
+    def forward_loads(s):
+        n = s // 2
+        if s % 2 == 0:
+            pairs = [
+                (wqkv_h.at[n, c], wqkv.at[:, pl.ds(c * width, width)]) for c in range(3)
+            ] + [(wout_h.at[n], wout)]
+        else:
+            pairs = [(w1_h.at[n], w1), (w2_h.at[n], w2)]
+        return [
+            pltpu.make_async_copy(*pair, load_sem.at[s % 2, m]) for m, pair in enumerate(pairs)
+        ]
+
     for s in range(2):
-        for copy in loads(s):
+        for copy in forward_loads(s):
             copy.start()
     barrier = pltpu.get_barrier_semaphore()
     peers = [{"tensor": ex.mate}, {"tensor": ex.far}]
@@ -624,13 +496,132 @@
         pl.semaphore_signal(barrier, inc=1, device_id=peer, device_id_type=pl.DeviceIdType.MESH)
     pl.semaphore_wait(barrier, len(peers))
 
+    def hold(s):
+        return final if s == stages else source.at[(s + 1) % 2]
+
+    def save_flow(s, g):
+        out = layer_h if s == stages else flow_h.at[s]
+        return pltpu.make_async_copy(hold(s).at[g], out.at[g], flow_sem.at[s % 2, g])
+
+    def begin(s, g):
+        n = s // 2
+        held = hold(s)
+        if 2 <= s < stages:
+            save_flow(s - 2, g).wait()
+        if s == 0:
+            for image, at in images_of(g):
+                held[g, at : at + PATCHES] = dot(picker(keep, image), patches[image], 0, 0)
+            held[g, LIVE:] = jnp.zeros((ROWS - LIVE, D), F32)
+            value = held[g]
+        else:
+            shift = shifts[(s - 1) // 2, 2 + (s - 1) % 2].reshape(1, D)
+            value = hold(s - 1)[g] + ex.total(g) + shift
+            held[g] = value
+        if s < 2 or s == stages:
+            save_flow(s, g).start()
+        if s == stages:
+            return
+        unit, _ = norm_parts(value)
+        gain, shift = gains[n, s % 2].reshape(1, D), shifts[n, s % 2].reshape(1, D)
+        own = ex.own(g)
+        gath[s % 2, own] = (unit * gain + shift).astype(BF16)
+        tail = gath[s % 2, own, ROWS - 16 : ROWS, 0:256].astype(F32)
+        row = lax.broadcasted_iota(jnp.int32, (16, 256), 0) - (LIVE - ROWS + 16)
+        for m, (image, _) in enumerate(images_of(g)):
+            tail = jnp.where(row == m, count[image].astype(F32), tail)
+        gath[s % 2, own, ROWS - 16 : ROWS, 0:256] = tail.astype(BF16)
+        ex.share(g)
+
+    def saves(s, slot):
+        if s == 0:
+            pairs = (
+                (gath.at[0, slot], gath_h),
+                (qkv.at[slot], qkv_h),
+                (prob.at[slot], prob_h),
+                (att.at[slot], att_h),
+            )
+        elif s == 1:
+            pairs = ((gath.at[1, slot], gmlp_h), (act.at[slot], act_h), (slope.at[slot], slope_h))
+        else:
+            pairs = ((gath.at[s % 2, slot], (norm_a, norm_m)[s % 2]),)
+        return [
+            pltpu.make_async_copy(a, b.at[slot], keep_sem.at[m, slot])
+            for m, (a, b) in enumerate(pairs)
+        ]
+
+    def drain(s):
+        def one(slot, _):
+            for copy in saves(s, slot):
+                copy.wait()
+            return 0
+
+        lax.fori_loop(0, 8, one, 0)
+
+    for s in range(stages):
+        n = s // 2
+        ex.stage = s
+        begin(s, 0)
+        if s == 0:
+            begin(s, 1)
+        else:
+            drain(s - 1)
+        for copy in forward_loads(s):
+            copy.wait()
+        if 1 <= s < stages - 1:
+            for copy in forward_loads(s + 1):
+                copy.start()
+
+        def step(i, _, s=s, n=n):
+            if s:
+
+                @pl.when(i == 2)
+                def _():
+                    begin(s, 1)
+
+            ex.before(i)
+            slot = ex.slot(i)
+            x = gath[s % 2, slot]
+            if s % 2 == 0:
+
+                def keep_parts(kind, *values):
+                    if kind == 0:
+                        for c, value in enumerate(values):
+                            qkv[slot, :, c * width : (c + 1) * width] = value
+                    else:
+                        prob[slot, (kind - 1) * ROWS : kind * ROWS] = values[0]
+
+                tail = gath[0, slot, ROWS - 16 : ROWS, 0:256][:, 0:ROWS].astype(F32)
+                mixed = attend(
+                    x, bias_qv[n, 0:1], bias_qv[n, 1:2], wqkv, wout, tail, keep_parts
+                )
+                att[slot] = mixed
+                part[ex.place(i)] = dot(mixed, wout[...])
+            else:
+                for block in range(hidden // 256):
+                    at = slice(block * 256, block * 256 + 256)
+                    pre_act = dot(x, w1[:, at]) + bias_fc1[n : n + 1, at]
+                    cdf, pdf = erf_parts(pre_act)
+                    act[slot, :, at] = (pre_act * cdf).astype(BF16)
+                    slope[slot, :, at] = (cdf + pre_act * pdf).astype(BF16)
+                part[ex.place(i)] = dot(act[slot], w2[...])
+            for copy in saves(s, slot):
+                copy.start()
+            ex.after(i)
+            return 0
+
+        lax.fori_loop(0, 8, step, 0)
+
     def note(at, g, row):
         lines[at : at + 1] = row if g == 0 else lines[at : at + 1] + row
 
     def produce(s, g):
         if s == 0:
-            rounded = cot[g]
-            gradient[g] = rounded.astype(F32)
+            begin(stages, g)
+            gradient[g, LIVE:] = jnp.zeros((ROWS - LIVE, D), F32)
+            for image, at in images_of(g):
+                piece = jnp.where(live_rows(count, image), cot[image].astype(F32), 0.0)
+                gradient[g, at : at + PATCHES] = piece
+            rounded = gradient[g].astype(BF16)
         else:
             n, side = layer(s - 1), s % 2
             gain = gains[n, side].reshape(1, D)
@@ -646,9 +637,15 @@
             if s < stages:
                 gradient[g] = grad
             else:
-                pick = picker(keep, g)
-                rest_of = (grad - rounded.astype(F32)).astype(BF16)
-                patch_grad[g] = dot(pick, rounded) + dot(pick, rest_of)
+                gradient[g] = grad
+                save_flow(stages, g).wait()
+                for image, at in images_of(g):
+                    exact = gradient[g, at : at + PATCHES]
+                    high = exact.astype(BF16)
+                    low = (exact - high.astype(F32)).astype(BF16)
+                    pick = picker(keep, image)
+                    final[g, at : at + PATCHES] = dot(pick, high) + dot(pick, low)
+                pltpu.make_async_copy(final.at[g], patch_h.at[g], flow_sem.at[0, g]).start()
                 return
         if s % 2 == 0:
             note(4 + 4 * layer(s) + 3, g, column_sums(rounded.astype(F32)))
@@ -761,12 +758,12 @@
     }
 
     for s in range(stages):
-        ex.stage = s
+        ex.stage = stages + s
         if s:
             columns(s - 1)
         produce(s, 0)
         if s == 0:
-            produce(s, 1)
+            drain(stages - 1)
         early = (3, 6)[s % 2]
         for copy in loads(s)[:early]:
             copy.wait()
@@ -782,9 +779,11 @@
                 def _():
                     some_rows(s - 1, i - 2, 2)
 
-                @pl.when(i == 2)
-                def _():
-                    produce(s, 1)
+            @pl.when(i == 2)
+            def _():
+                produce(s, 1)
+
+            if s:
 
                 @pl.when(i == 6)
                 def _():
@@ -804,7 +803,7 @@
                     at = slice(block * 256, block * 256 + 256)
                     d_act = dot(grad, w2[at, :], 1, 1)
                     pre[slot, :, at] = (d_act * slope[slot, :, at].astype(F32)).astype(BF16)
-                part[i] = dot(pre[slot], w1[...], 1, 1)
+                part[ex.place(i)] = dot(pre[slot], w1[...], 1, 1)
             else:
                 d_att = dot(grad, wout[...], 1, 1).astype(BF16)
                 q = qkv[slot, :, 0:width]
@@ -827,7 +826,7 @@
                 triple[slot, :, 0:width] = (d_q * SCALE).astype(BF16)
                 triple[slot, :, width : 2 * width] = (d_k * SCALE).astype(BF16)
                 triple[slot, :, 2 * width :] = d_v.astype(BF16)
-                part[i] = dot(triple[slot], wqkv[...], 1, 1)
+                part[ex.place(i)] = dot(triple[slot], wqkv[...], 1, 1)
             ex.after(i)
             return 0
 
@@ -865,12 +864,14 @@
                     for copy in spill(s, side, k):
                         copy.wait()
     ex.end()
-
-
-def backward(fused, cot, keep, gains, flow, wqkv, wout, w1, w2, kept):
+    for g in range(GROUPS):
+        pltpu.make_async_copy(final.at[g], patch_h.at[g], flow_sem.at[0, g]).wait()
+
+
+def run_step(fused, count, patches, cot, keep, gains, shifts, bias_qv, bias_fc1, wqkv, wout, w1, w2):
     width, hidden = wout.shape[1], w1.shape[2]
     heads = width // HEAD
-    wide = (8, ROWS, D)
+    wide, own = (8, ROWS, D), (GROUPS, ROWS, D)
     dma = pltpu.SemaphoreType.DMA
     tall = D // 256
     mine = ((hidden, COLS), (COLS, hidden), (width, COLS), (COLS, 3 * width))
@@ -896,37 +897,94 @@
         outs = [sds((LAYERS,) + b, BF16) for b in blocks]
         small = sds((16, D), F32)
         more = [dma((2, 2, 4, 2))]
-    kept_shapes = (
-        (8, ROWS, 3 * width), (8, heads * ROWS, ROWS), (8, ROWS, width), wide,
-        (8, ROWS, hidden), (8, ROWS, hidden), wide, (8, ROWS, hidden), (8, ROWS, 3 * width),
-    )
+    inner = ((8, ROWS, 3 * width), (8, heads * ROWS, ROWS), (8, ROWS, width))
+    mlp = ((8, ROWS, hidden), (8, ROWS, hidden))
+    saved = (wide,) + inner + (wide,) + mlp
     return pl.pallas_call(
-        partial(backward_kernel, fused),
-        out_shape=[sds((GROUPS, ROWS, D), F32), small] + outs,
-        in_specs=[VM] * 3 + [HB] * 12,
-        out_specs=[VM] * 2 + [HB] * 4,
+        partial(step_kernel, fused),
+        out_shape=[sds(own, F32), sds(own, F32), small]
+        + outs
+        + [sds((2,) + own, F32)]
+        + [sds(k, BF16) for k in saved],
+        in_specs=[pl.BlockSpec(memory_space=pltpu.SMEM)] + [VM] * 7 + [HB] * 4,
+        out_specs=[HB] * 2 + [VM] + [HB] * 12,
         scratch_shapes=exchange_scratch()
         + [
-            pltpu.VMEM((GROUPS, ROWS, D), F32),
-            pltpu.VMEM((2, GROUPS, ROWS, D), F32),
+            pltpu.VMEM(own, F32),
+            pltpu.VMEM((2,) + own, F32),
+            pltpu.VMEM(own, F32),
             pltpu.VMEM((D, 3 * width), BF16),
             pltpu.VMEM((width, D), BF16),
             pltpu.VMEM((D, hidden), BF16),
             pltpu.VMEM((hidden, D), BF16),
         ]
-        + [pltpu.VMEM(k, BF16) for k in kept_shapes]
+        + [pltpu.VMEM(k, BF16) for k in inner + (wide,) + mlp + (wide,)]
+        + [pltpu.VMEM((8, ROWS, hidden), BF16), pltpu.VMEM((8, ROWS, 3 * width), BF16)]
         + [pltpu.VMEM((16, D), F32)]
         + [pltpu.VMEM(b, BF16) for b in blocks]
-        + [dma((2, 9))]
+        + [dma((2, 9)), dma((4, 8)), dma((2, GROUPS))]
         + more,
-        compiler_params=params(2),
-    )(cot, keep, gains, flow, wqkv, wout, w1, w2, *kept)
-
-
-def to_groups(array, dtype):
-    images = array.shape[0] // GROUPS
-    rows = array.reshape(GROUPS, images * PATCHES, D)
-    return jnp.pad(rows, ((0, 0), (0, ROWS - images * PATCHES), (0, 0))).astype(dtype)
+        compiler_params=params(1),
+    )(count, patches, cot, keep, gains, shifts, bias_qv, bias_fc1, wqkv, wout, w1, w2)[:7]
+
+
+def deliver_kernel(
+    count, layer, patch, small, a_h, b_h, c_h, d_h,
+    layer_out, patch_out, gain, shift, qv, fc1, a_out, b_out, c_out, d_out,
+    a, b, c, d, sems,
+):
+    held = ((a_h, a, a_out), (b_h, b, b_out), (c_h, c, c_out), (d_h, d, d_out))
+
+    def inward(n):
+        return pltpu.make_async_copy(held[n][0], held[n][1], sems.at[0, n])
+
+    def outward(n):
+        return pltpu.make_async_copy(held[n][1], held[n][2], sems.at[1, n])
+
+    for n in range(4):
+        inward(n).start()
+    for g in range(GROUPS):
+        for image, at in images_of(g):
+            rows = layer[g, at : at + PATCHES]
+            layer_out[image] = jnp.where(live_rows(count, image), rows, 0.0)
+            patch_out[image] = patch[g, at : at + PATCHES]
+    for n in range(4):
+        inward(n).wait()
+        outward(n).start()
+    summed = small[0, 0:12] + small[1, 0:12] + small[2, 0:12] + small[3, 0:12]
+    for n in range(LAYERS):
+        gain[n] = summed[2 * n : 2 * n + 2]
+        shift[n] = summed[4 + 4 * n : 8 + 4 * n]
+        for t in range(4):
+            hidden = fc1.shape[1] // 4
+            fc1[n : n + 1, t * hidden : (t + 1) * hidden] = small[t, 12 + n : 13 + n]
+            width = D // 4
+            for side in range(2):
+                at = (2 * n + side) * width
+                piece = small[t, 14:15, at : at + width]
+                qv[n, side : side + 1, t * width : (t + 1) * width] = piece
+    for n in range(4):
+        outward(n).wait()
+
+
+def deliver(count, layer, patch, small, grads):
+    images = (GROUPS * LIVE // PATCHES, PATCHES, D)
+    shapes = [g.shape for g in grads]
+    return pl.pallas_call(
+        deliver_kernel,
+        out_shape=[
+            sds(images, F32),
+            sds(images, F32),
+            sds((LAYERS, 2, D), F32),
+            sds((LAYERS, 4, D), F32),
+            sds((LAYERS, 2, D), F32),
+            sds((LAYERS, FF), F32),
+        ]
+        + [sds(s, F32) for s in shapes],
+        in_specs=[pl.BlockSpec(memory_space=pltpu.SMEM)] + [VM] * 3 + [HB] * 4,
+        out_specs=[VM] * 6 + [HB] * 4,
+        scratch_shapes=[pltpu.VMEM(s, F32) for s in shapes] + [pltpu.SemaphoreType.DMA((2, 4))],
+    )(count, layer, patch, small, *grads)
 
 
 def from_groups(array):
@@ -965,44 +1023,33 @@
     hidden = w_fc1.shape[-1]
     dp_size, ways = lax.axis_size("dp"), lax.axis_size("tensor")
     assert ways == 4
-    per = kept_count.shape[0] // GROUPS
-    slot_ids = jnp.arange(PATCHES, dtype=jnp.int32)
-    counts = kept_count.reshape(GROUPS, per, 1).astype(F32)
-    first = LIVE - ROWS + 16
-    counts = jnp.broadcast_to(
-        jnp.pad(counts, ((0, 0), (first, 16 - first - per), (0, 0))), (GROUPS, 16, 256)
-    )
-    places = keep_index.reshape(GROUPS, per, PATCHES) + PATCHES * jnp.arange(per)[:, None]
-    places = places.reshape(GROUPS, 1, per * PATCHES)
-    places = jnp.pad(places, ((0, 0), (0, 0), (0, ROWS - LIVE)), constant_values=-1)
     wqkv = jnp.transpose(w_qkv, (0, 2, 1, 3))
-    flow, *kept = forward(
-        to_groups(patches, BF16), places, counts, norm_gain, shifts, bias_qv, bias_fc1,
+    fused = dp_size == 8 and hidden == D and 4 * width == D
+    layer, patch, small, g_fc2, g_fc1, g_out, g_qkv = run_step(
+        fused, kept_count, patches, cotangent, keep_index, norm_gain, shifts, bias_qv, bias_fc1,
         wqkv, w_out, w_fc1, w_fc2,
     )
+    if fused:
+        layer_out, grad_patches, gain, shift, qv, fc1, g_fc2, g_fc1, g_out, g_qkv = deliver(
+            kept_count, layer, patch, small, (g_fc2, g_fc1, g_out, g_qkv)
+        )
+        grad_qkv = jnp.transpose(g_qkv, (0, 2, 1, 3))
+        return layer_out, grad_patches, gain, shift, grad_qkv, qv, g_out, g_fc1, fc1, g_fc2
+    slot_ids = jnp.arange(PATCHES, dtype=jnp.int32)
     own_mask = (slot_ids[None, :] < kept_count[:, None])[:, :, None]
-    layer_out = from_groups(flow[2 * LAYERS]) * own_mask.astype(F32)
-    fused = dp_size == 8 and hidden == D and 4 * width == D
-    patch_grad, small, g_fc2, g_fc1, g_out, g_qkv = backward(
-        fused, to_groups(cotangent * own_mask.astype(BF16), BF16), places, norm_gain, flow,
-        wqkv, w_out, w_fc1, w_fc2, kept,
+    layer_out = from_groups(layer) * own_mask.astype(F32)
+    grad_patches = from_groups(patch)
+    grad_qkv, grad_out, grad_fc1, grad_fc2 = (
+        jnp.stack([collect_weight(join(array[n]), split) for n in range(LAYERS)])
+        for array, join, split in (
+            (g_qkv, join_rows, 0),
+            (g_out, join_columns, 1),
+            (g_fc1, join_rows, 0),
+            (g_fc2, join_columns, 1),
+        )
     )
-    grad_patches = from_groups(patch_grad)
-    if fused:
-        grad_qkv, grad_out, grad_fc1, grad_fc2 = g_qkv, g_out, g_fc1, g_fc2
-    else:
-        grad_qkv, grad_out, grad_fc1, grad_fc2 = (
-            jnp.stack([collect_weight(join(array[n]), split) for n in range(LAYERS)])
-            for array, join, split in (
-                (g_qkv, join_rows, 0),
-                (g_out, join_columns, 1),
-                (g_fc1, join_rows, 0),
-                (g_fc2, join_columns, 1),
-            )
-        )
-        grad_qkv = jnp.transpose(grad_qkv.reshape(LAYERS, -1, 3, width), (0, 2, 1, 3))
-        small = lax.all_gather(lax.psum(small, "dp"), "tensor")
-    grad_qkv = jnp.transpose(grad_qkv, (0, 2, 1, 3))
+    grad_qkv = grad_qkv.reshape(LAYERS, -1, 3, width)
+    small = lax.all_gather(lax.psum(small, "dp"), "tensor")
     summed = jnp.sum(small[:, :12], axis=0)
     grad_gain = summed[:4].reshape(LAYERS, 2, D)
     grad_shifts = summed[4:].reshape(LAYERS, 4, D)

time: 315 us -> 297 us (0.943)
  local copies, waits for them, and re-layouts: 17.1 us -> 0 us
  other arithmetic: 3.41 us -> 0 us
    unnamed x22 -> x0, local copies, waits for them, and re-layouts: 6.11 us -> none
    reshape x8 -> x0, local copies, waits for them, and re-layouts: 5.39 us -> none  [the longest x2 1.4 us: to_groups(): rows = array.reshape(GROUPS, images * PATCHES, D)]
where the time goes in v6:
time: 297 us; the launch traced here: 296 us
  Pallas kernels  296 us (100%)
    pallas_call x1, Pallas kernels, run_step(): pl.pallas_call(partial(step_kernel, fused), out_shape=[sds(own, F32), sds...  289 us
    pallas_call x1, Pallas kernels, deliver(): pl.pallas_call(deliver_kernel, out_shape=[sds(images, F32), sds(images, F...  6.31 us

profile of v6, /device:TPU:0, one launch (start us, length us, event | category | flops | bytes accessed | tf_op | source)
XLA Modules:
  0.0 296.5 jit_solution(10382291726368230502)
XLA Ops:
  0.6 289.3 %shard_map.195 = (f32[2,160,1024]{2,1,0:T(8,128)}, f32[2,160,1024]{2,1,0:T(8,128)}, f32[4,16,1024]{2,1,0:T(8,128)}, f32[2,1024,128]{2,1,0:T(8,128)}, f32[2,128,1...) custom-call(s32[6]{0:T(128)} %count.3, ...), custom_call_target="tpu_custom_call" | custom-call | tf_op jit(solution)/shard_map/pallas_call | solution.py:903
  290.0 6.3 %shard_map.196 = (f32[6,50,1024]{2,1,0:T(8,128)}, f32[6,50,1024]{2,1,0:T(8,128)}, f32[2,2,1024]{2,1,0:T(2,128)}, f32[2,4,1024]{2,1,0:T(4,128)}, f32[2,2,1024]{2,...) custom-call(s32[6]{0:T(128)} %count.3, ...), custom_call_target="tpu_custom_call" | custom-call | tf_op jit(solution)/shard_map/pallas_call | solution.py:973

commit v7 on v6

--- a/solution.py
+++ b/solution.py
@@ -53,9 +53,10 @@
 
 
 class Exchange:
-    def __init__(self, gath, part, bufs, sems):
+    def __init__(self, gath, part, bufs, spare, late_y, sems):
         self.gath, self.part = gath, part
         self.out_po, self.out_pd, self.out_y, self.in_po, self.in_pd, self.in_y = bufs
+        self.spare, self.late_y = spare, late_y
         self.sem = sems
         me = lax.axis_index("tensor")
         self.me = me
@@ -81,6 +82,8 @@
     def copy(self, kind, g):
         s = self.sem
         own, slot = self.rows(self.own(g)), self.rows(GROUPS * self.far + g)
+        own_0, slot_0 = self.gath.at[0, self.own(g)], self.gath.at[0, GROUPS * self.far + g]
+        spare = self.spare
         src, dst, peer = (
             (own, own, self.far),
             (own, own, self.mate),
@@ -88,6 +91,12 @@
             (self.out_po.at[g], self.in_po.at[g], self.mate),
             (self.out_pd.at[g], self.in_pd.at[g], self.mate),
             (self.out_y.at[g], self.in_y.at[g], self.far),
+            (own_0, own_0, self.far),
+            (own_0, own_0, self.mate),
+            (slot_0, slot_0, self.mate),
+            (spare.at[g], spare.at[2 + g], self.mate),
+            (spare.at[4 + g], spare.at[6 + g], self.mate),
+            (self.late_y.at[g], self.in_pd.at[g], self.far),
         )[kind]
         return remote(src, dst, s.at[0, kind, g], s.at[1, kind, g], peer)
 
@@ -98,9 +107,12 @@
     def send(self, kind, g):
         self.copy(kind, g).start()
 
+    def clear(self, g):
+        for kind in range(2):
+            self.again(kind, g)
+
     def share(self, g):
         for kind in range(2):
-            self.again(kind, g)
             self.send(kind, g)
 
     def slot(self, i):
@@ -125,7 +137,6 @@
             @pl.when(i == 4 + 2 * g)
             def _():
                 self.copy(0, g).wait_recv()
-                self.again(2, g)
                 self.send(2, g)
 
             @pl.when(i == 5 + 2 * g)
@@ -149,6 +160,7 @@
                 self.copy(4, g).wait_recv()
                 self.again(5, g)
                 self.out_y[g] = (self.part[2 + g] + self.in_pd[g].astype(F32)).astype(BF16)
+                self.copy(2, g).wait_send()
                 self.send(5, g)
 
     def total(self, g):
@@ -156,9 +168,51 @@
         self.copy(5, g).wait_recv()
         return self.part[g] + self.in_po[g].astype(F32) + self.in_y[g].astype(F32)
 
+    def before_both(self, i):
+        self.before(i)
+        for g in range(GROUPS):
+
+            @pl.when(i == 1 + 2 * g)
+            def _():
+                self.copy(7, g).wait_recv()
+
+            @pl.when(i == 4 + 2 * g)
+            def _():
+                self.copy(6, g).wait_recv()
+                self.send(8, g)
+
+            @pl.when(i == 5 + 2 * g)
+            def _():
+                self.copy(8, g).wait_recv()
+
+    def set_aside(self, i, value, own_total):
+        self.part[4] = value
+        for g in range(GROUPS):
+
+            @pl.when(i == 2 * g)
+            def _():
+                own_total(g, self.part[4])
+
+            @pl.when(i == 1 + 2 * g)
+            def _():
+                self.spare[g] = self.part[4].astype(BF16)
+                self.send(9, g)
+
+            @pl.when(i == 4 + 2 * g)
+            def _():
+                self.late_y[g] = self.part[4].astype(BF16)
+
+            @pl.when(i == 5 + 2 * g)
+            def _():
+                self.spare[4 + g] = self.part[4].astype(BF16)
+                self.send(10, g)
+                self.copy(10, g).wait_recv()
+                both = self.late_y[g].astype(F32) + self.spare[6 + g].astype(F32)
+                self.late_y[g] = both.astype(BF16)
+
     def end(self):
         for g in range(GROUPS):
-            for kind in range(6):
+            for kind in (0, 1, 3, 4, 5, 11):
                 self.copy(kind, g).wait_send()
 
 
@@ -166,7 +220,7 @@
     return [
         pltpu.VMEM((2, 8, ROWS, D), BF16),
         pltpu.VMEM((5, ROWS, D), F32),
-    ] + [pltpu.VMEM((GROUPS, ROWS, D), BF16)] * 6 + [pltpu.SemaphoreType.DMA((2, 6, GROUPS))]
+    ] + [pltpu.VMEM((GROUPS, ROWS, D), BF16)] * 6 + [pltpu.SemaphoreType.DMA((2, 12, GROUPS))]
 
 
 def picker(keep, image):
@@ -421,11 +475,12 @@
     layer_h, patch_h, small_out, o_fc2, o_fc1, o_out, o_qkv,
     flow_h, gath_h, qkv_h, prob_h, att_h, gmlp_h, act_h, slope_h,
     gath, part, out_po, out_pd, out_y, in_po, in_pd, in_y, ex_sem,
-    gradient, source, final, wqkv, wout, w1, w2,
+    gradient, source, final, late_y, wqkv, wout, w1, w2,
     qkv, prob, att, norm_a, act, slope, norm_m,
     pre, triple, lines, cols_m, rows_m, cols_a, rows_a, load_sem, keep_sem, flow_sem, *rest,
 ):
-    ex = Exchange(gath, part, (out_po, out_pd, out_y, in_po, in_pd, in_y), ex_sem)
+    bufs = (out_po, out_pd, out_y, in_po, in_pd, in_y)
+    ex = Exchange(gath, part, bufs, slope, late_y, ex_sem)
     width, hidden = wout.shape[0], w1.shape[1]
     stages = 2 * LAYERS
     flat = 8 * ROWS
@@ -496,17 +551,19 @@
         pl.semaphore_signal(barrier, inc=1, device_id=peer, device_id_type=pl.DeviceIdType.MESH)
     pl.semaphore_wait(barrier, len(peers))
 
+    def note(at, g, row):
+        lines[at : at + 1] = row if g == 0 else lines[at : at + 1] + row
+
     def hold(s):
-        return final if s == stages else source.at[(s + 1) % 2]
+        return source.at[(s + 1) % 2]
 
     def save_flow(s, g):
-        out = layer_h if s == stages else flow_h.at[s]
-        return pltpu.make_async_copy(hold(s).at[g], out.at[g], flow_sem.at[s % 2, g])
+        return pltpu.make_async_copy(hold(s).at[g], flow_h.at[s, g], flow_sem.at[s, g])
 
     def begin(s, g):
         n = s // 2
         held = hold(s)
-        if 2 <= s < stages:
+        if s >= 2:
             save_flow(s - 2, g).wait()
         if s == 0:
             for image, at in images_of(g):
@@ -517,13 +574,12 @@
             shift = shifts[(s - 1) // 2, 2 + (s - 1) % 2].reshape(1, D)
             value = hold(s - 1)[g] + ex.total(g) + shift
             held[g] = value
-        if s < 2 or s == stages:
+        if s < 2:
             save_flow(s, g).start()
-        if s == stages:
-            return
         unit, _ = norm_parts(value)
         gain, shift = gains[n, s % 2].reshape(1, D), shifts[n, s % 2].reshape(1, D)
         own = ex.own(g)
+        ex.clear(g)
         gath[s % 2, own] = (unit * gain + shift).astype(BF16)
         tail = gath[s % 2, own, ROWS - 16 : ROWS, 0:256].astype(F32)
         row = lax.broadcasted_iota(jnp.int32, (16, 256), 0) - (LIVE - ROWS + 16)
@@ -531,6 +587,17 @@
             tail = jnp.where(row == m, count[image].astype(F32), tail)
         gath[s % 2, own, ROWS - 16 : ROWS, 0:256] = tail.astype(BF16)
         ex.share(g)
+        if s < stages - 1:
+            return
+        gradient[g, LIVE:] = jnp.zeros((ROWS - LIVE, D), F32)
+        for image, at in images_of(g):
+            piece = jnp.where(live_rows(count, image), cot[image].astype(F32), 0.0)
+            gradient[g, at : at + PATCHES] = piece
+        rounded = gradient[g].astype(BF16)
+        note(4 + 4 * n + 3, g, column_sums(rounded.astype(F32)))
+        gath[0, own] = rounded
+        ex.send(6, g)
+        ex.send(7, g)
 
     def saves(s, slot):
         if s == 0:
@@ -543,7 +610,7 @@
         elif s == 1:
             pairs = ((gath.at[1, slot], gmlp_h), (act.at[slot], act_h), (slope.at[slot], slope_h))
         else:
-            pairs = ((gath.at[s % 2, slot], (norm_a, norm_m)[s % 2]),)
+            pairs = ()
         return [
             pltpu.make_async_copy(a, b.at[slot], keep_sem.at[m, slot])
             for m, (a, b) in enumerate(pairs)
@@ -557,13 +624,17 @@
 
         lax.fori_loop(0, 8, one, 0)
 
+    def own_total(g, value):
+        final[g] = source[0, g] + value + shifts[LAYERS - 1, 3].reshape(1, D)
+
+    lines[15:16] = jnp.zeros((1, D), F32)
     for s in range(stages):
         n = s // 2
         ex.stage = s
         begin(s, 0)
         if s == 0:
             begin(s, 1)
-        else:
+        elif s <= 2:
             drain(s - 1)
         for copy in forward_loads(s):
             copy.wait()
@@ -578,9 +649,12 @@
                 def _():
                     begin(s, 1)
 
-            ex.before(i)
+            both = s == stages - 1
+            (ex.before_both if both else ex.before)(i)
             slot = ex.slot(i)
             x = gath[s % 2, slot]
+            if s >= 2:
+                (norm_a, norm_m)[s % 2][slot] = x
             if s % 2 == 0:
 
                 def keep_parts(kind, *values):
@@ -602,8 +676,17 @@
                     pre_act = dot(x, w1[:, at]) + bias_fc1[n : n + 1, at]
                     cdf, pdf = erf_parts(pre_act)
                     act[slot, :, at] = (pre_act * cdf).astype(BF16)
-                    slope[slot, :, at] = (cdf + pre_act * pdf).astype(BF16)
-                part[ex.place(i)] = dot(act[slot], w2[...])
+                    steep = cdf + pre_act * pdf
+                    if both:
+                        d_act = dot(gath[0, slot], w2[at, :], 1, 1)
+                        pre[slot, :, at] = (d_act * steep).astype(BF16)
+                    else:
+                        slope[slot, :, at] = steep.astype(BF16)
+                value = dot(act[slot], w2[...])
+                if both:
+                    ex.set_aside(i, value, own_total)
+                    value = dot(pre[slot], w1[...], 1, 1)
+                part[ex.place(i)] = value
             for copy in saves(s, slot):
                 copy.start()
             ex.after(i)
@@ -611,46 +694,42 @@
 
         lax.fori_loop(0, 8, step, 0)
 
-    def note(at, g, row):
-        lines[at : at + 1] = row if g == 0 else lines[at : at + 1] + row
+    for g in range(GROUPS):
+        for kind in (6, 7, 8):
+            ex.copy(kind, g).wait_send()
+        ex.copy(9, g).wait()
+        ex.copy(10, g).wait_send()
+        final[g] = final[g] + ex.spare[2 + g].astype(F32)
 
     def produce(s, g):
-        if s == 0:
-            begin(stages, g)
-            gradient[g, LIVE:] = jnp.zeros((ROWS - LIVE, D), F32)
+        n, side = layer(s - 1), s % 2
+        gain = gains[n, side].reshape(1, D)
+        moved = ex.total(g)
+        unit, scale = norm_parts(source[1 - side, g])
+        note(2 * n + side, g, column_sums(moved * unit))
+        note(4 + 4 * n + side, g, column_sums(moved))
+        scaled = moved * gain
+        lean = jnp.mean(scaled, axis=-1, keepdims=True)
+        tilt = jnp.mean(scaled * unit, axis=-1, keepdims=True)
+        grad = gradient[g] + scale * (scaled - lean - unit * tilt)
+        rounded = grad.astype(BF16)
+        if s < stages:
+            gradient[g] = grad
+        else:
+            gradient[g] = grad
             for image, at in images_of(g):
-                piece = jnp.where(live_rows(count, image), cot[image].astype(F32), 0.0)
-                gradient[g, at : at + PATCHES] = piece
-            rounded = gradient[g].astype(BF16)
-        else:
-            n, side = layer(s - 1), s % 2
-            gain = gains[n, side].reshape(1, D)
-            moved = ex.total(g)
-            unit, scale = norm_parts(source[1 - side, g])
-            note(2 * n + side, g, column_sums(moved * unit))
-            note(4 + 4 * n + side, g, column_sums(moved))
-            scaled = moved * gain
-            lean = jnp.mean(scaled, axis=-1, keepdims=True)
-            tilt = jnp.mean(scaled * unit, axis=-1, keepdims=True)
-            grad = gradient[g] + scale * (scaled - lean - unit * tilt)
-            rounded = grad.astype(BF16)
-            if s < stages:
-                gradient[g] = grad
-            else:
-                gradient[g] = grad
-                save_flow(stages, g).wait()
-                for image, at in images_of(g):
-                    exact = gradient[g, at : at + PATCHES]
-                    high = exact.astype(BF16)
-                    low = (exact - high.astype(F32)).astype(BF16)
-                    pick = picker(keep, image)
-                    final[g, at : at + PATCHES] = dot(pick, high) + dot(pick, low)
-                pltpu.make_async_copy(final.at[g], patch_h.at[g], flow_sem.at[0, g]).start()
-                return
+                exact = gradient[g, at : at + PATCHES]
+                high = exact.astype(BF16)
+                low = (exact - high.astype(F32)).astype(BF16)
+                pick = picker(keep, image)
+                source[0, g, at : at + PATCHES] = dot(pick, high) + dot(pick, low)
+            pltpu.make_async_copy(source.at[0, g], patch_h.at[g], flow_sem.at[0, g]).start()
+            return
         if s % 2 == 0:
             note(4 + 4 * layer(s) + 3, g, column_sums(rounded.astype(F32)))
         else:
             note(4 + 4 * layer(s) + 2, g, column_sums(rounded.astype(F32)))
+        ex.clear(g)
         gath[s % 2, ex.own(g)] = rounded
         ex.share(g)
 
@@ -742,7 +821,6 @@
 
         return run
 
-    lines[15:16] = jnp.zeros((1, D), F32)
     plan = {
         (1, 4): take((0, 0, 3)),
         (1, 6): take((0, 0, 1)),
@@ -753,17 +831,14 @@
         (2, 8): take((0, 1, 0), (0, 0, 4), (1, 0, 3), (1, 0, 1)),
         (3, 2): take((1, 0, 2), (1, 0, 0), (1, 1, 3), (1, 1, 1)),
         (3, 4): take((0, 1, 4), (1, 1, 2)),
-        (3, 6): take((1, 0, 4), (1, 1, 0)),
-        (3, 8): take((2, 0, 3), (2, 0, 1)),
+        (3, 6): take((1, 0, 4), (1, 1, 0), (2, 0, 3)),
+        (3, 8): take((2, 0, 1), (1, 1, 4)),
     }
 
-    for s in range(stages):
+    for s in range(1, stages):
         ex.stage = stages + s
-        if s:
-            columns(s - 1)
+        columns(s - 1)
         produce(s, 0)
-        if s == 0:
-            drain(stages - 1)
         early = (3, 6)[s % 2]
         for copy in loads(s)[:early]:
             copy.wait()
@@ -840,20 +915,22 @@
     settle(last, 1)
     some_rows(last, 0, 4)
     bias_sums(last)
-    take((2, 0, 2), (1, 1, 4))()
+    take((2, 0, 2), (2, 0, 0))()
     for g in range(GROUPS):
         produce(stages, g)
+    for g in range(GROUPS):
+        ex.send(11, g)
     if fused:
         tiny = SmallSum(lines, small_in, small_z, small_out, small_sem, sc, ex.me)
         tiny.across().start()
-        for side in range(2):
+        for side in (1, 0):
             for j in range(4):
                 sc.send(last, side, j)
-        take((2, 0, 0), (2, 1, 3), (2, 1, 1), (2, 0, 4), (2, 1, 2), (2, 1, 0))()
+        take((2, 1, 3), (2, 1, 1), (2, 0, 4), (2, 1, 2), (2, 1, 0))()
         tiny.second()
-        take((3, 0, 3), (3, 0, 1), (3, 0, 2), (3, 0, 0))()
+        take((2, 1, 4), (3, 1, 3), (3, 1, 1))()
         tiny.third()
-        take((2, 1, 4), (3, 1, 3), (3, 1, 1), (3, 1, 2), (3, 0, 4), (3, 1, 0), (3, 1, 4))()
+        take((3, 1, 2), (3, 1, 0), (3, 0, 3), (3, 0, 1), (3, 0, 2), (3, 1, 4), (3, 0, 0), (3, 0, 4))()
         sc.end()
         tiny.last()
     else:
@@ -863,9 +940,14 @@
                 for k in range(4):
                     for copy in spill(s, side, k):
                         copy.wait()
+    for g in range(GROUPS):
+        ex.copy(11, g).wait_recv()
+        final[g] = final[g] + in_pd[g].astype(F32)
+        pltpu.make_async_copy(final.at[g], layer_h.at[g], flow_sem.at[1, g]).start()
     ex.end()
     for g in range(GROUPS):
-        pltpu.make_async_copy(final.at[g], patch_h.at[g], flow_sem.at[0, g]).wait()
+        pltpu.make_async_copy(source.at[0, g], patch_h.at[g], flow_sem.at[0, g]).wait()
+        pltpu.make_async_copy(final.at[g], layer_h.at[g], flow_sem.at[1, g]).wait()
 
 
 def run_step(fused, count, patches, cot, keep, gains, shifts, bias_qv, bias_fc1, wqkv, wout, w1, w2):
@@ -913,6 +995,7 @@
             pltpu.VMEM(own, F32),
             pltpu.VMEM((2,) + own, F32),
             pltpu.VMEM(own, F32),
+            pltpu.VMEM(own, BF16),
             pltpu.VMEM((D, 3 * width), BF16),
             pltpu.VMEM((width, D), BF16),
             pltpu.VMEM((D, hidden), BF16),

time: 297 us -> 286 us (0.963)
  Pallas kernels: 296 us -> 283 us
    pallas_call x1, Pallas kernels: 289 us -> 277 us  [run_step(): pl.pallas_call(partial(step_kernel, fused), out_shape=[sds(own, F32), sds...]
where the time goes in v7:
time: 286 us; the launch traced here: 284 us
  Pallas kernels  283 us (99%)
    pallas_call x1, Pallas kernels, run_step(): pl.pallas_call(partial(step_kernel, fused), out_shape=[sds(own, F32), sds...  277 us
    pallas_call x1, Pallas kernels, deliver(): pl.pallas_call(deliver_kernel, out_shape=[sds(images, F32), sds(images, F...  6.31 us

profile of v7, /device:TPU:0, one launch (start us, length us, event | category | flops | bytes accessed | tf_op | source)
XLA Modules:
  0.0 284.0 jit_solution(11831864302419172565)
XLA Ops:
  0.6 276.9 %shard_map.195 = (f32[2,160,1024]{2,1,0:T(8,128)}, f32[2,160,1024]{2,1,0:T(8,128)}, f32[4,16,1024]{2,1,0:T(8,128)}, f32[2,1024,128]{2,1,0:T(8,128)}, f32[2,128,1...) custom-call(s32[6]{0:T(128)} %count.3, ...), custom_call_target="tpu_custom_call" | custom-call | tf_op jit(solution)/shard_map/pallas_call | solution.py:985
  277.5 6.3 %shard_map.196 = (f32[6,50,1024]{2,1,0:T(8,128)}, f32[6,50,1024]{2,1,0:T(8,128)}, f32[2,2,1024]{2,1,0:T(2,128)}, f32[2,4,1024]{2,1,0:T(4,128)}, f32[2,2,1024]{2,...) custom-call(s32[6]{0:T(128)} %count.3, ...), custom_call_target="tpu_custom_call" | custom-call | tf_op jit(solution)/shard_map/pallas_call | solution.py:1056

commit v8 on v7

--- a/solution.py
+++ b/solution.py
@@ -20,6 +20,7 @@
 GROUPS = 2
 ROWS = 160
 LIVE = 150
+MOST, EDGE = 144, 152
 COLS = 128
 SCALE = HEAD ** (-0.5)
 
@@ -53,7 +54,8 @@
 
 
 class Exchange:
-    def __init__(self, gath, part, bufs, spare, late_y, sems):
+    def __init__(self, gath, part, bufs, spare, late_y, edges, sems):
+        self.edge_out, self.edge_in = edges
         self.gath, self.part = gath, part
         self.out_po, self.out_pd, self.out_y, self.in_po, self.in_pd, self.in_y = bufs
         self.spare, self.late_y = spare, late_y
@@ -82,21 +84,27 @@
     def copy(self, kind, g):
         s = self.sem
         own, slot = self.rows(self.own(g)), self.rows(GROUPS * self.far + g)
+        most = pl.ds(0, MOST)
+        far_own = self.gath.at[self.stage % 2, self.own(g), most]
+        far_own_0 = self.gath.at[0, self.own(g), most]
         own_0, slot_0 = self.gath.at[0, self.own(g)], self.gath.at[0, GROUPS * self.far + g]
         spare = self.spare
         src, dst, peer = (
-            (own, own, self.far),
+            (far_own, far_own, self.far),
             (own, own, self.mate),
             (slot, slot, self.mate),
             (self.out_po.at[g], self.in_po.at[g], self.mate),
             (self.out_pd.at[g], self.in_pd.at[g], self.mate),
-            (self.out_y.at[g], self.in_y.at[g], self.far),
-            (own_0, own_0, self.far),
+            (self.out_y.at[g, most], self.in_y.at[g, most], self.far),
+            (far_own_0, far_own_0, self.far),
             (own_0, own_0, self.mate),
             (slot_0, slot_0, self.mate),
             (spare.at[g], spare.at[2 + g], self.mate),
             (spare.at[4 + g], spare.at[6 + g], self.mate),
             (self.late_y.at[g], self.in_pd.at[g], self.far),
+            (self.edge_out.at[0, g], self.edge_in.at[0, g], self.far),
+            (self.edge_out.at[1, g], self.edge_in.at[1, g], self.far),
+            (self.edge_out.at[2, g], self.edge_in.at[2, g], self.far),
         )[kind]
         return remote(src, dst, s.at[0, kind, g], s.at[1, kind, g], peer)
 
@@ -108,10 +116,19 @@
         self.copy(kind, g).start()
 
     def clear(self, g):
-        for kind in range(2):
+        for kind in (0, 1, 12):
             self.again(kind, g)
 
+    def set_edge(self, n, g, rows):
+        self.edge_out[n, g] = rows.astype(F32)[0 : EDGE - MOST].astype(BF16)
+
+    def get_edge(self, n, g):
+        rows = self.edge_in[n, g].astype(F32)
+        return jnp.concatenate([rows, jnp.zeros((ROWS - EDGE, D), F32)]).astype(BF16)
+
     def share(self, g):
+        self.set_edge(0, g, self.gath[self.stage % 2, self.own(g), MOST:ROWS])
+        self.send(12, g)
         for kind in range(2):
             self.send(kind, g)
 
@@ -137,6 +154,8 @@
             @pl.when(i == 4 + 2 * g)
             def _():
                 self.copy(0, g).wait_recv()
+                self.copy(12, g).wait_recv()
+                self.gath[self.stage % 2, GROUPS * self.far + g, MOST:ROWS] = self.get_edge(0, g)
                 self.send(2, g)
 
             @pl.when(i == 5 + 2 * g)
@@ -160,12 +179,17 @@
                 self.copy(4, g).wait_recv()
                 self.again(5, g)
                 self.out_y[g] = (self.part[2 + g] + self.in_pd[g].astype(F32)).astype(BF16)
+                self.again(13, g)
+                self.set_edge(1, g, self.out_y[g, MOST:ROWS])
                 self.copy(2, g).wait_send()
                 self.send(5, g)
+                self.send(13, g)
 
     def total(self, g):
         self.copy(3, g).wait_recv()
         self.copy(5, g).wait_recv()
+        self.copy(13, g).wait_recv()
+        self.in_y[g, MOST:ROWS] = self.get_edge(1, g)
         return self.part[g] + self.in_po[g].astype(F32) + self.in_y[g].astype(F32)
 
     def before_both(self, i):
@@ -179,6 +203,8 @@
             @pl.when(i == 4 + 2 * g)
             def _():
                 self.copy(6, g).wait_recv()
+                self.copy(14, g).wait_recv()
+                self.gath[0, GROUPS * self.far + g, MOST:ROWS] = self.get_edge(2, g)
                 self.send(8, g)
 
             @pl.when(i == 5 + 2 * g)
@@ -212,7 +238,7 @@
 
     def end(self):
         for g in range(GROUPS):
-            for kind in (0, 1, 3, 4, 5, 11):
+            for kind in (0, 1, 3, 4, 5, 11, 12, 13):
                 self.copy(kind, g).wait_send()
 
 
@@ -220,7 +246,9 @@
     return [
         pltpu.VMEM((2, 8, ROWS, D), BF16),
         pltpu.VMEM((5, ROWS, D), F32),
-    ] + [pltpu.VMEM((GROUPS, ROWS, D), BF16)] * 6 + [pltpu.SemaphoreType.DMA((2, 12, GROUPS))]
+    ] + [pltpu.VMEM((GROUPS, ROWS, D), BF16)] * 6 + [pltpu.VMEM((3, GROUPS, EDGE - MOST, D), BF16)] * 2 + [
+        pltpu.SemaphoreType.DMA((2, 15, GROUPS))
+    ]
 
 
 def picker(keep, image):
@@ -247,7 +275,7 @@
     keep_parts(0, q, k, v)
     lane = lax.broadcasted_iota(jnp.int32, (1, ROWS), 1)
     image = lane // PATCHES
-    count = jnp.where(image == 0, counts[6:7], jnp.where(image == 1, counts[7:8], counts[8:9]))
+    count = counts[LIVE - ROWS + 16 : LIVE - ROWS + 17]
     fits = (lane - image * PATCHES).astype(F32) < count
     row = lax.broadcasted_iota(jnp.int32, (ROWS, ROWS), 0)
     col = lax.broadcasted_iota(jnp.int32, (ROWS, ROWS), 1)
@@ -474,13 +502,13 @@
     count, patches, cot, keep, gains, shifts, bias_qv, bias_fc1, wqkv_h, wout_h, w1_h, w2_h,
     layer_h, patch_h, small_out, o_fc2, o_fc1, o_out, o_qkv,
     flow_h, gath_h, qkv_h, prob_h, att_h, gmlp_h, act_h, slope_h,
-    gath, part, out_po, out_pd, out_y, in_po, in_pd, in_y, ex_sem,
+    gath, part, out_po, out_pd, out_y, in_po, in_pd, in_y, edge_out, edge_in, ex_sem,
     gradient, source, final, late_y, wqkv, wout, w1, w2,
     qkv, prob, att, norm_a, act, slope, norm_m,
     pre, triple, lines, cols_m, rows_m, cols_a, rows_a, load_sem, keep_sem, flow_sem, *rest,
 ):
     bufs = (out_po, out_pd, out_y, in_po, in_pd, in_y)
-    ex = Exchange(gath, part, bufs, slope, late_y, ex_sem)
+    ex = Exchange(gath, part, bufs, slope, late_y, (edge_out, edge_in), ex_sem)
     width, hidden = wout.shape[0], w1.shape[1]
     stages = 2 * LAYERS
     flat = 8 * ROWS
@@ -549,7 +577,6 @@
         peers += [{"dp": sc.device((sc.z + k) % 4)} for k in range(1, 4)]
     for peer in peers:
         pl.semaphore_signal(barrier, inc=1, device_id=peer, device_id_type=pl.DeviceIdType.MESH)
-    pl.semaphore_wait(barrier, len(peers))
 
     def note(at, g, row):
         lines[at : at + 1] = row if g == 0 else lines[at : at + 1] + row
@@ -582,10 +609,14 @@
         ex.clear(g)
         gath[s % 2, own] = (unit * gain + shift).astype(BF16)
         tail = gath[s % 2, own, ROWS - 16 : ROWS, 0:256].astype(F32)
-        row = lax.broadcasted_iota(jnp.int32, (16, 256), 0) - (LIVE - ROWS + 16)
-        for m, (image, _) in enumerate(images_of(g)):
-            tail = jnp.where(row == m, count[image].astype(F32), tail)
+        row = lax.broadcasted_iota(jnp.int32, (16, 256), 0)
+        lane = lax.broadcasted_iota(jnp.int32, (16, 256), 1)
+        for image, at in images_of(g):
+            here = (row == LIVE - ROWS + 16) & (lane >= at)
+            tail = jnp.where(here, count[image].astype(F32), tail)
         gath[s % 2, own, ROWS - 16 : ROWS, 0:256] = tail.astype(BF16)
+        if s == 0 and g == 0:
+            pl.semaphore_wait(barrier, len(peers))
         ex.share(g)
         if s < stages - 1:
             return
@@ -596,6 +627,8 @@
         rounded = gradient[g].astype(BF16)
         note(4 + 4 * n + 3, g, column_sums(rounded.astype(F32)))
         gath[0, own] = rounded
+        ex.set_edge(2, g, gath[0, own, MOST:ROWS])
+        ex.send(14, g)
         ex.send(6, g)
         ex.send(7, g)
 
@@ -694,12 +727,11 @@
 
         lax.fori_loop(0, 8, step, 0)
 
-    for g in range(GROUPS):
-        for kind in (6, 7, 8):
-            ex.copy(kind, g).wait_send()
-        ex.copy(9, g).wait()
-        ex.copy(10, g).wait_send()
-        final[g] = final[g] + ex.spare[2 + g].astype(F32)
+    def complete_output():
+        for g in range(GROUPS):
+            ex.copy(11, g).wait_recv()
+            final[g] = final[g] + in_pd[g].astype(F32)
+            pltpu.make_async_copy(final.at[g], layer_h.at[g], flow_sem.at[1, g]).start()
 
     def produce(s, g):
         n, side = layer(s - 1), s % 2
@@ -838,6 +870,13 @@
     for s in range(1, stages):
         ex.stage = stages + s
         columns(s - 1)
+        if s == 1:
+            for g in range(GROUPS):
+                for kind in (6, 7, 8, 14):
+                    ex.copy(kind, g).wait_send()
+                ex.copy(9, g).wait()
+                ex.copy(10, g).wait_send()
+                final[g] = final[g] + ex.spare[2 + g].astype(F32)
         produce(s, 0)
         early = (3, 6)[s % 2]
         for copy in loads(s)[:early]:
@@ -927,6 +966,7 @@
             for j in range(4):
                 sc.send(last, side, j)
         take((2, 1, 3), (2, 1, 1), (2, 0, 4), (2, 1, 2), (2, 1, 0))()
+        complete_output()
         tiny.second()
         take((2, 1, 4), (3, 1, 3), (3, 1, 1))()
         tiny.third()
@@ -934,16 +974,13 @@
         sc.end()
         tiny.last()
     else:
+        complete_output()
         small_out[...] = lines[...]
         for s in (2, 3):
             for side in range(2):
                 for k in range(4):
                     for copy in spill(s, side, k):
                         copy.wait()
-    for g in range(GROUPS):
-        ex.copy(11, g).wait_recv()
-        final[g] = final[g] + in_pd[g].astype(F32)
-        pltpu.make_async_copy(final.at[g], layer_h.at[g], flow_sem.at[1, g]).start()
     ex.end()
     for g in range(GROUPS):
         pltpu.make_async_copy(source.at[0, g], patch_h.at[g], flow_sem.at[0, g]).wait()

time: 286 us -> 277 us (0.969)
  Pallas kernels: 283 us -> 276 us
    pallas_call x1, Pallas kernels: 277 us -> 270 us  [run_step(): pl.pallas_call(partial(step_kernel, fused), out_shape=[sds(own, F32), sds...]
where the time goes in v8:
time: 277 us
  Pallas kernels  276 us (100%)
    pallas_call x1, Pallas kernels, run_step(): pl.pallas_call(partial(step_kernel, fused), out_shape=[sds(own, F32), sds...  270 us
    pallas_call x1, Pallas kernels, deliver(): pl.pallas_call(deliver_kernel, out_shape=[sds(images, F32), sds(images, F...  6.31 us

profile of v8, /device:TPU:0, one launch (start us, length us, event | category | flops | bytes accessed | tf_op | source)
XLA Modules:
  0.0 277.2 jit_solution(16501962673166685126)
XLA Ops:
  0.6 270.0 %shard_map.195 = (f32[2,160,1024]{2,1,0:T(8,128)}, f32[2,160,1024]{2,1,0:T(8,128)}, f32[4,16,1024]{2,1,0:T(8,128)}, f32[2,1024,128]{2,1,0:T(8,128)}, f32[2,128,1...) custom-call(s32[6]{0:T(128)} %count.3, ...), custom_call_target="tpu_custom_call" | custom-call | tf_op jit(solution)/shard_map/pallas_call | solution.py:1022
  270.7 6.3 %shard_map.196 = (f32[6,50,1024]{2,1,0:T(8,128)}, f32[6,50,1024]{2,1,0:T(8,128)}, f32[2,2,1024]{2,1,0:T(2,128)}, f32[2,4,1024]{2,1,0:T(4,128)}, f32[2,2,1024]{2,...) custom-call(s32[6]{0:T(128)} %count.3, ...), custom_call_target="tpu_custom_call" | custom-call | tf_op jit(solution)/shard_map/pallas_call | solution.py:1093

commit v9 on v8

--- a/solution.py
+++ b/solution.py
@@ -863,8 +863,8 @@
         (2, 8): take((0, 1, 0), (0, 0, 4), (1, 0, 3), (1, 0, 1)),
         (3, 2): take((1, 0, 2), (1, 0, 0), (1, 1, 3), (1, 1, 1)),
         (3, 4): take((0, 1, 4), (1, 1, 2)),
-        (3, 6): take((1, 0, 4), (1, 1, 0), (2, 0, 3)),
-        (3, 8): take((2, 0, 1), (1, 1, 4)),
+        (3, 6): take((1, 1, 0), (2, 0, 3), (2, 0, 1)),
+        (3, 8): take((2, 0, 2), (1, 0, 4), (1, 1, 4)),
     }
 
     for s in range(1, stages):
@@ -889,9 +889,9 @@
                 def _():
                     settle(s - 1, 1)
 
-                @pl.when((i == 2) | (i == 4))
+                @pl.when(i == 2)
                 def _():
-                    some_rows(s - 1, i - 2, 2)
+                    some_rows(s - 1, 0, 4)
 
             @pl.when(i == 2)
             def _():
@@ -954,7 +954,7 @@
     settle(last, 1)
     some_rows(last, 0, 4)
     bias_sums(last)
-    take((2, 0, 2), (2, 0, 0))()
+    take((2, 0, 0), (2, 1, 3))()
     for g in range(GROUPS):
         produce(stages, g)
     for g in range(GROUPS):
@@ -965,7 +965,7 @@
         for side in (1, 0):
             for j in range(4):
                 sc.send(last, side, j)
-        take((2, 1, 3), (2, 1, 1), (2, 0, 4), (2, 1, 2), (2, 1, 0))()
+        take((2, 1, 1), (2, 0, 4), (2, 1, 2), (2, 1, 0))()
         complete_output()
         tiny.second()
         take((2, 1, 4), (3, 1, 3), (3, 1, 1))()

time: 277 us -> 277 us (level)
  no operation moved by 1% of the time
where the time goes in v9:
time: 277 us
  Pallas kernels  276 us (100%)
    pallas_call x1, Pallas kernels, run_step(): pl.pallas_call(partial(step_kernel, fused), out_shape=[sds(own, F32), sds...  270 us
    pallas_call x1, Pallas kernels, deliver(): pl.pallas_call(deliver_kernel, out_shape=[sds(images, F32), sds(images, F...  6.31 us

profile of v9, /device:TPU:0, one launch (start us, length us, event | category | flops | bytes accessed | tf_op | source)
XLA Modules:
  0.0 277.3 jit_solution(2552324545653701256)
XLA Ops:
  0.6 270.1 %shard_map.195 = (f32[2,160,1024]{2,1,0:T(8,128)}, f32[2,160,1024]{2,1,0:T(8,128)}, f32[4,16,1024]{2,1,0:T(8,128)}, f32[2,1024,128]{2,1,0:T(8,128)}, f32[2,128,1...) custom-call(s32[6]{0:T(128)} %count.3, ...), custom_call_target="tpu_custom_call" | custom-call | tf_op jit(solution)/shard_map/pallas_call | solution.py:1022
  270.8 6.3 %shard_map.196 = (f32[6,50,1024]{2,1,0:T(8,128)}, f32[6,50,1024]{2,1,0:T(8,128)}, f32[2,2,1024]{2,1,0:T(2,128)}, f32[2,4,1024]{2,1,0:T(4,128)}, f32[2,2,1024]{2,...) custom-call(s32[6]{0:T(128)} %count.3, ...), custom_call_target="tpu_custom_call" | custom-call | tf_op jit(solution)/shard_map/pallas_call | solution.py:1093
